TPU v7x, 128 devices: a whole 4x4x4 slice. The times are simulated.
128 devices in a mesh: gx: 16 (over x, z), gz: 8 (over y, core).
Axes of the slice: x: 4, y: 4, z: 4, core: 2. Of those that a mesh axis runs over, the one named last changes fastest.
Arguments:
- grains: float32 [8, 128, 128, 256], P(None, 'gx', 'gz'), may hold values from 0 to 1
- block_owner: int32 [32, 32, 64], P('gx', 'gz'), may hold values from 0 to 127, as said below
- element_anchor: int32 [65536], P(('gx', 'gz')), may hold values from 0 to 1023
- strain_step: float32 [6, 8, 65536], P(None, None, ('gx', 'gz')), may hold values from -3 to 3
- stress: float32 [6, 8, 65536], P(None, None, ('gx', 'gz')), may hold values from -6 to 6
- resistance: float32 [24, 8, 65536], P(None, None, ('gx', 'gz')), may hold values from 0.5 to 2
- slip_active: int32 [24, 65536], P(None, ('gx', 'gz')), may hold values 0 or 1
- orientation_schmid: float32 [8, 24, 6], replicated, may hold values from -2.5 to 2.5
- latent_hardening: float32 [24, 24], replicated, may hold values from 0.2 to 1.4
- mobility: float32 [8], replicated, may hold values from 0.5 to 2
- grain_state: float32 [8], replicated, may hold values from 0 to 1
Outputs:
- grains_out: float32 [8, 128, 128, 256], P(None, 'gx', 'gz')
- stress_out: float32 [6, 8, 65536], P(None, None, ('gx', 'gz'))
- resistance_out: float32 [24, 8, 65536], P(None, None, ('gx', 'gz'))
Inputs may be any that keep to these rules, and one draw needn't show every extreme that they name: `block_owner`: the 512 blocks of one device name any one owner at most 8 times, and some owner exactly 8 times; every device owns exactly 512 blocks.
All inputs are finite; a program needn't handle non-finite values. No bound on the sum of `slip_active` on one device may be relied on, other than what follows from the above.
Results may differ from a plain program's by a relative error of at most 0.0003.
Values sent between devices are 32-bit elements; how exact they have to be, the bound alone decides.
No kernel may reach another device: no remote copies, remote signals or barrier semaphores. Data moves between devices by JAX's collectives and lax.ppermute only.
A program may use at most 64 MiB of HBM per device.

v0:
```python
import jax
import jax.numpy as jnp
from jax import lax
from jax.sharding import PartitionSpec as P

ITERS = 4
STEPS = 3
SUB = 2


CROSS_TERM = 1.5
DRIVE_SCALE = 6.0
TIME_STEP = 0.02
SLIP_RATE = 0.1
HARDENING = 0.5
HIGHEST = lax.Precision.HIGHEST


def in_blocks(array, dim, size):
    lengths = array.shape
    parts = array.reshape(*lengths[:dim], size, lengths[dim] // size, *lengths[dim + 1 :])
    return jnp.moveaxis(parts, dim, 0)


def joined_along(parts, dim):
    parts = jnp.moveaxis(parts, 0, dim)
    lengths = parts.shape
    return parts.reshape(*lengths[:dim], lengths[dim] * lengths[dim + 1], *lengths[dim + 2 :])


def exchange_both(array, axis, axes, splits, concats):
    sizes = [lax.axis_size(a) for a in axes]
    parts = in_blocks(array, splits[0], sizes[0])
    parts = jnp.moveaxis(in_blocks(parts, splits[1] + 1, sizes[1]), 0, 1)
    inside = parts.shape[2:]
    parts = parts.reshape(-1, *inside)
    parts = lax.all_to_all(parts, axis, split_axis=0, concat_axis=0, tiled=True)
    parts = joined_along(parts.reshape(*sizes, *inside), concats[0] + 1)
    return joined_along(parts, concats[1])


def padded_2(array, sides, width):
    for axis, dim in sides:
        size, length = (lax.axis_size(axis), array.shape[dim])
        up = [(i, (i + 1) % size) for i in range(size)]
        down = [(j, i) for i, j in up]
        last = lax.slice_in_dim(array, length - width, length, axis=dim)
        first = lax.slice_in_dim(array, 0, width, axis=dim)
        before = lax.ppermute(last, axis, up)
        after = lax.ppermute(first, axis, down)
        array = jnp.concatenate([before, array, after], axis=dim)
    return array


def column_map(width):
    quarter = width // 4
    row_index = jnp.arange(width, dtype=jnp.int32)[:, None]
    col_index = jnp.arange(2 * quarter, dtype=jnp.int32)[None, :]
    member = (row_index // 4 == col_index % quarter) & (row_index % 4 // 2 == col_index // quarter)
    return member.astype(jnp.float32)


def restrict(field):
    orders, size_x, size_z, size_y = field.shape
    squares = (field * field).reshape(orders * size_x * size_z, size_y)
    along_y = jnp.dot(
        squares, column_map(size_y), precision=HIGHEST, preferred_element_type=jnp.float32
    )
    along_y = along_y.reshape(orders, size_x // 4, 2, 2, size_z // 4, 2, 2, 2, size_y // 4)
    averaged = jnp.sum(along_y, axis=(3, 6)) * 0.125
    averaged = averaged.transpose(0, 2, 4, 5, 1, 3, 6)
    return averaged.reshape(orders * 8, size_x // 4 * (size_z // 4) * (size_y // 4))


def prolong(stored, size_x, size_z, size_y):
    quarter = size_y // 4
    spread = stored.reshape(2, 2, 2, size_x // 4, size_z // 4, quarter).transpose(3, 0, 4, 1, 2, 5)
    spread = spread.reshape(size_x // 4 * 2 * (size_z // 4) * 2, 2 * quarter)
    cell_energy = jnp.dot(
        spread, column_map(size_y).T, precision=HIGHEST, preferred_element_type=jnp.float32
    )
    cell_energy = cell_energy.reshape(size_x // 4, 2, 1, size_z // 4, 2, 1, size_y)
    cell_energy = jnp.broadcast_to(cell_energy, (size_x // 4, 2, 2, size_z // 4, 2, 2, size_y))
    return cell_energy.reshape(size_x, size_z, size_y)


def pair_rank(owners, count_all):
    onehot = (owners[:, None] == jnp.arange(count_all, dtype=jnp.int32)[None, :]).astype(jnp.int32)
    before = jnp.cumsum(onehot, axis=0) - onehot
    return jnp.sum(before * onehot, axis=1)


def mechanics(
    mix_weights, strain_step, stress, resistance, slip_active, orientation_schmid, latent_hardening
):
    orders, systems = (orientation_schmid.shape[0], orientation_schmid.shape[1])
    points, elements = (stress.shape[1], stress.shape[2])
    flat = points * elements
    weights_flat = mix_weights.reshape(orders, flat)
    schmid_rows = orientation_schmid.transpose(2, 1, 0).reshape(6 * systems, orders)
    tensor = jnp.dot(
        schmid_rows, weights_flat, precision=HIGHEST, preferred_element_type=jnp.float32
    ).reshape(6, systems, flat)
    trial_stress = (stress + 2.0 * strain_step).reshape(6, flat)
    active = jnp.broadcast_to(
        slip_active.astype(jnp.float32)[:, None, :], (systems, points, elements)
    ).reshape(systems, flat)
    resist = resistance.reshape(systems, flat)
    components = [trial_stress[comp] for comp in range(6)]
    slip_amount = jnp.zeros((systems, flat), jnp.float32)
    for sweep in range(ITERS):
        resolved = tensor[0] * components[0][None, :]
        for comp in range(1, 6):
            resolved = resolved + tensor[comp] * components[comp][None, :]
        slip_amount = active * SLIP_RATE * resolved / (resist + jnp.abs(resolved))
        components = [
            trial_stress[comp] - 2.0 * jnp.sum(tensor[comp] * slip_amount, axis=0)
            for comp in range(6)
        ]
    stress_now = jnp.stack(components, axis=0)
    harden = jnp.dot(
        latent_hardening,
        jnp.abs(slip_amount),
        precision=HIGHEST,
        preferred_element_type=jnp.float32,
    )
    resist_new = resist + HARDENING * harden
    stored = jnp.sum(resist_new * jnp.abs(slip_amount), axis=0)
    return (
        stress_now.reshape(6, points, elements),
        resist_new.reshape(systems, points, elements),
        stored.reshape(points, elements),
    )


def phase_update(center, x_plus, x_minus, z_plus, z_minus, energy, mobility, grain_state):
    laplace = (
        x_plus
        + x_minus
        + z_plus
        + z_minus
        + jnp.roll(center, 1, 3)
        + jnp.roll(center, -1, 3)
        - 6.0 * center
    )
    sum_squares = jnp.sum(center * center, axis=0, keepdims=True)
    keep_share = (1.0 - grain_state)[:, None, None, None]
    driving = (
        -center
        + center * center * center
        + 2.0 * CROSS_TERM * center * (sum_squares - center * center)
        - laplace
        + 2.0 * DRIVE_SCALE * energy[None] * keep_share * center
    )
    return center - TIME_STEP * mobility[:, None, None, None] * driving


def advance(padded, energy, mobility, grain_state):
    center = padded[:, 1:-1, 1:-1]
    return phase_update(
        center,
        padded[:, 2:, 1:-1],
        padded[:, :-2, 1:-1],
        padded[:, 1:-1, 2:],
        padded[:, 1:-1, :-2],
        energy,
        mobility,
        grain_state,
    )


def shards(
    grains,
    block_owner,
    element_anchor,
    strain_step,
    stress,
    resistance,
    slip_active,
    orientation_schmid,
    latent_hardening,
    mobility,
    grain_state,
):
    count_all = lax.axis_size(("gx", "gz"))
    across = lax.axis_size("gx")
    owners = block_owner.reshape(-1)
    per_dev = owners.shape[0]
    capacity = 2 * per_dev // count_all
    slots_all = count_all * capacity
    mailbox = owners * capacity + pair_rank(owners, count_all)
    slot_index = jnp.arange(slots_all, dtype=jnp.int32)
    slot_hit = (slot_index[:, None] == mailbox[None, :]).astype(jnp.float32)
    element_pick = (element_anchor[:, None] == slot_index[None, :]).astype(jnp.float32)
    orders, size_x, size_z, size_y = grains.shape
    points = stress.shape[1]
    for cycle in range(STEPS):
        weights = restrict(grains)
        feature = weights.shape[0]
        outbox = lax.dot_general(
            slot_hit,
            weights,
            (((1,), (1,)), ((), ())),
            precision=HIGHEST,
            preferred_element_type=jnp.float32,
        )
        sectioned = outbox.reshape(across, count_all // across, capacity * feature)
        inbox = exchange_both(sectioned, ("gx", "gz"), ("gx", "gz"), (0, 1), (0, 1)).reshape(
            slots_all, feature
        )
        elem_weights = lax.dot_general(
            inbox,
            element_pick,
            (((0,), (1,)), ((), ())),
            precision=HIGHEST,
            preferred_element_type=jnp.float32,
        ).reshape(orders, points, per_dev)
        stress, resistance, stored = mechanics(
            elem_weights,
            strain_step,
            stress,
            resistance,
            slip_active,
            orientation_schmid,
            latent_hardening,
        )
        reply = lax.dot_general(
            element_pick,
            stored,
            (((0,), (1,)), ((), ())),
            precision=HIGHEST,
            preferred_element_type=jnp.float32,
        )
        sectioned_reply = reply.reshape(across, count_all // across, capacity * points)
        returned = exchange_both(
            sectioned_reply, ("gx", "gz"), ("gx", "gz"), (0, 1), (0, 1)
        ).reshape(slots_all, points)
        block_energy = lax.dot_general(
            returned,
            slot_hit,
            (((0,), (0,)), ((), ())),
            precision=HIGHEST,
            preferred_element_type=jnp.float32,
        )
        cell_energy = prolong(block_energy, size_x, size_z, size_y)
        stacked = jnp.concatenate([grains, cell_energy[None]], axis=0)
        padded = padded_2(stacked, (("gx", 1), ("gz", 2)), SUB)
        field = padded[:orders]
        energy_pad = padded[orders]
        for inner in range(SUB):
            energy_pad = energy_pad[1:-1, 1:-1]
            field = advance(field, energy_pad, mobility, grain_state)
        grains = field
    return (grains, stress, resistance)


def solution(mesh):
    return jax.shard_map(
        shards,
        mesh=mesh,
        in_specs=(
            P(None, "gx", "gz", None),
            P("gx", "gz", None),
            P(("gx", "gz")),
            P(None, None, ("gx", "gz")),
            P(None, None, ("gx", "gz")),
            P(None, None, ("gx", "gz")),
            P(None, ("gx", "gz")),
            P(),
            P(),
            P(),
            P(),
        ),
        out_specs=(
            P(None, "gx", "gz", None),
            P(None, None, ("gx", "gz")),
            P(None, None, ("gx", "gz")),
        ),
        check_vma=False,
    )
```

profile of v0, /device:TPU:0, one launch (start us, length us, event | category | flops | bytes accessed | tf_op | source)
XLA Modules:
  0.0 243.9 jit_solution(11209717889036335398)
XLA Ops:
  7.0 11.3 %all-to-all-start = ((f32[128,1,1,512]{3,2,1,0:T(1,128)}), f32[128,1,1,512]{3,2,1,0:T(1,128)S(1)}, u32[]{:S(2)}, u32[]{:S(2)}) async-start(f32[128,1,1,512]{3,2,1,0:T(1,128)} %reshape_transpose_transpose_reshape_reshape_reshape.24), calls=%async_computation | async-start | bytes 524288 | tf_op jit(solution)/shard_map/all_to_all | solution.py:37
  21.0 8.0 %all-to-all-done = f32[128,1,1,512]{3,2,1,0:T(1,128)S(1)} async-done(((f32[128,1,1,512]{3,2,1,0:T(1,128)}), f32[128,1,1,512]{3,2,1,0:T(1,128)S(1)}, u32[]{:S(2)}, u32[]{:S(2)}) %all-to-all-start) | async-done | bytes 262176 | tf_op jit(solution)/shard_map/all_to_all | solution.py:37
  30.0 2.3 fusion.12
  41.0 4.8 %all-to-all-start.1 = ((f32[128,1,1,64]{3,2,1,0:T(1,128)}), f32[128,1,1,64]{3,2,1,0:T(1,128)S(1)}, u32[]{:S(2)}, u32[]{:S(2)}) async-start(f32[128,1,1,64]{3,2,1,0:T(1,128)} %bitcast.16), calls=%async_computation.1 | async-start | bytes 131072 | tf_op jit(solution)/shard_map/all_to_all | solution.py:37
  45.8 9.2 %all-to-all-done.1 = f32[128,1,1,64]{3,2,1,0:T(1,128)S(1)} async-done(((f32[128,1,1,64]{3,2,1,0:T(1,128)}), f32[128,1,1,64]{3,2,1,0:T(1,128)S(1)}, u32[]{:S(2)}, u32[]{:S(2)}) %all-to-all-start.1) | async-done | bytes 32800 | tf_op jit(solution)/shard_map/all_to_all | solution.py:37
  59.1 4.7 %collective-permute-start.1 = (f32[9,2,16,256]{3,2,1,0:T(8,128)}, f32[9,2,16,256]{3,2,1,0:T(8,128)S(1)}, u32[]{:S(2)}, u32[]{:S(2)}) collective-permute-start(f32[9,2,16,256]{3,2,1,0:T(8,128)} %get-tuple-element.122), channel_id=1, source_target_pairs={{8,0},{16,8},{24,16},{32,24},{40,32},{48,40},{56,48},{64,56},{72,6... | collective-permute-start | bytes 884744 | tf_op jit(solution)/shard_map/ppermute | solution.py:50
  63.8 6.5 %collective-permute-done = f32[9,2,16,256]{3,2,1,0:T(8,128)S(1)} collective-permute-done((f32[9,2,16,256]{3,2,1,0:T(8,128)}, f32[9,2,16,256]{3,2,1,0:T(8,128)S(1)}, u32[]{:S(2)}, u32[]{:S(2)}) %collective-permute-start) | collective-permute-done | bytes 294944 | tf_op jit(solution)/shard_map/ppermute | solution.py:49
  71.1 3.8 %collective-permute-done.3 = f32[9,12,2,256]{3,1,2,0:T(8,128)S(1)} collective-permute-done((f32[9,12,2,256]{3,1,2,0:T(8,128)S(1)}, f32[9,12,2,256]{3,1,2,0:T(8,128)S(1)}, u32[]{:S(2)}, u32[]{:S(2)}) %collective-permute-start.3) | collective-permute-done | bytes 221216 | tf_op jit(solution)/shard_map/ppermute | solution.py:50
  75.0 2.9 %collective-permute-done.2 = f32[9,12,2,256]{3,1,2,0:T(8,128)S(1)} collective-permute-done((f32[9,12,2,256]{3,1,2,0:T(8,128)S(1)}, f32[9,12,2,256]{3,1,2,0:T(8,128)S(1)}, u32[]{:S(2)}, u32[]{:S(2)}) %collective-permute-start.2) | collective-permute-done | bytes 221216 | tf_op jit(solution)/shard_map/ppermute | solution.py:49
  80.1 3.6 %fusion.18 = f32[8,10,18,256]{3,2,1,0:T(8,128)S(1)} fusion(f32[9,12,2,256]{3,2,1,0:T(2,128)S(1)} %copy.95, f32[9,2,16,256]{3,2,1,0:T(8,128)S(1)} %collective-permute-done.1, f32[9,8,16,256]{3,2,1,0:T(8,128)S(1)} %constant_dynamic-update-slice_fusion, f32[9,2,16,256]{3,2,1,0:T(8,128)S(1)} %collective-permute-done, f32[9,12,2,256]{3,2,1,0:T(2,128)S(1)} %copy.96, ...), kind=kLoop, calls=%fused_computation.39 | loop fusion | flops 10690560 | bytes 11427904 | tf_op jit(solution)/shard_map/sub | solution.py:155
  89.6 7.6 %all-to-all-start.2 = ((f32[128,1,1,512]{3,2,1,0:T(1,128)}), f32[128,1,1,512]{3,2,1,0:T(1,128)S(1)}, u32[]{:S(2)}, u32[]{:S(2)}) async-start(f32[128,1,1,512]{3,2,1,0:T(1,128)} %reshape_transpose_transpose_reshape_reshape_reshape.25), calls=%async_computation.2 | async-start | bytes 524288 | tf_op jit(solution)/shard_map/all_to_all | solution.py:37
  97.3 10.6 %all-to-all-done.2 = f32[128,1,1,512]{3,2,1,0:T(1,128)S(1)} async-done(((f32[128,1,1,512]{3,2,1,0:T(1,128)}), f32[128,1,1,512]{3,2,1,0:T(1,128)S(1)}, u32[]{:S(2)}, u32[]{:S(2)}) %all-to-all-start.2) | async-done | bytes 262176 | tf_op jit(solution)/shard_map/all_to_all | solution.py:37
  108.8 2.3 fusion.10
  119.8 4.8 %all-to-all-start.3 = ((f32[128,1,1,64]{3,2,1,0:T(1,128)}), f32[128,1,1,64]{3,2,1,0:T(1,128)S(1)}, u32[]{:S(2)}, u32[]{:S(2)}) async-start(f32[128,1,1,64]{3,2,1,0:T(1,128)} %bitcast.42), calls=%async_computation.3 | async-start | bytes 131072 | tf_op jit(solution)/shard_map/all_to_all | solution.py:37
  124.6 9.2 %all-to-all-done.3 = f32[128,1,1,64]{3,2,1,0:T(1,128)S(1)} async-done(((f32[128,1,1,64]{3,2,1,0:T(1,128)}), f32[128,1,1,64]{3,2,1,0:T(1,128)S(1)}, u32[]{:S(2)}, u32[]{:S(2)}) %all-to-all-start.3) | async-done | bytes 32800 | tf_op jit(solution)/shard_map/all_to_all | solution.py:37
  137.8 4.7 %collective-permute-start.5 = (f32[9,2,16,256]{3,2,1,0:T(8,128)S(1)}, f32[9,2,16,256]{3,2,1,0:T(8,128)S(1)}, u32[]{:S(2)}, u32[]{:S(2)}) collective-permute-start(f32[9,2,16,256]{3,2,1,0:T(8,128)S(1)} %get-tuple-element.120), channel_id=1, source_target_pairs={{8,0},{16,8},{24,16},{32,24},{40,32},{48,40},{56,48},{64,56},{72,6... | collective-permute-start | bytes 884744 | tf_op jit(solution)/shard_map/ppermute | solution.py:50
  143.9 5.1 %collective-permute-done.4 = f32[9,2,16,256]{3,2,1,0:T(8,128)S(1)} collective-permute-done((f32[9,2,16,256]{3,2,1,0:T(8,128)}, f32[9,2,16,256]{3,2,1,0:T(8,128)S(1)}, u32[]{:S(2)}, u32[]{:S(2)}) %collective-permute-start.4) | collective-permute-done | bytes 294944 | tf_op jit(solution)/shard_map/ppermute | solution.py:49
  149.2 2.9 %collective-permute-start.7 = (f32[9,12,2,256]{3,2,1,0:T(2,128)S(1)}, f32[9,12,2,256]{3,2,1,0:T(2,128)S(1)}, u32[]{:S(2)}, u32[]{:S(2)}) collective-permute-start(f32[9,12,2,256]{3,2,1,0:T(2,128)S(1)} %get-tuple-element.114), channel_id=1, source_target_pairs={{1,0},{2,1},{3,2},{4,3},{5,4},{6,5},{7,6},{0,7},{9,8},{10,9},{11,1... | collective-permute-start | bytes 663560 | tf_op jit(solution)/shard_map/ppermute | solution.py:50
  152.9 2.9 %collective-permute-done.6 = f32[9,12,2,256]{3,2,1,0:T(2,128)S(1)} collective-permute-done((f32[9,12,2,256]{3,2,1,0:T(2,128)S(1)}, f32[9,12,2,256]{3,2,1,0:T(2,128)S(1)}, u32[]{:S(2)}, u32[]{:S(2)}) %collective-permute-start.6) | collective-permute-done | bytes 221216 | tf_op jit(solution)/shard_map/ppermute | solution.py:49
  157.7 3.8 %fusion.25 = f32[8,10,18,256]{3,2,1,0:T(8,128)S(1)} fusion(f32[9,12,2,256]{3,2,1,0:T(2,128)S(1)} %collective-permute-done.6, f32[9,2,16,256]{3,2,1,0:T(8,128)S(1)} %collective-permute-done.5, f32[9,2,16,256]{3,2,1,0:T(8,128)S(1)} %collective-permute-done.4, f32[1,8,16,256]{3,2,1,0:T(8,128)S(1)} %broadcast_in_dim_reshape.11, ...), kind=kLoop, calls=%fused_computation.46 | loop fusion | flops 11427840 | bytes 11427904 | tf_op jit(solution)/shard_map/sub | solution.py:155
  167.5 9.5 %all-to-all-start.4 = ((f32[128,1,1,512]{3,2,1,0:T(1,128)}), f32[128,1,1,512]{3,2,1,0:T(1,128)S(1)}, u32[]{:S(2)}, u32[]{:S(2)}) async-start(f32[128,1,1,512]{3,2,1,0:T(1,128)} %reshape_transpose_transpose_reshape_reshape_reshape.26), calls=%async_computation.4 | async-start | bytes 524288 | tf_op jit(solution)/shard_map/all_to_all | solution.py:37
  177.1 10.6 %all-to-all-done.4 = f32[128,1,1,512]{3,2,1,0:T(1,128)S(1)} async-done(((f32[128,1,1,512]{3,2,1,0:T(1,128)}), f32[128,1,1,512]{3,2,1,0:T(1,128)S(1)}, u32[]{:S(2)}, u32[]{:S(2)}) %all-to-all-start.4) | async-done | bytes 262176 | tf_op jit(solution)/shard_map/all_to_all | solution.py:37
  188.7 2.3 fusion.9
  195.2 2.1 multiply_reduce_fusion.6
  199.6 4.8 %all-to-all-start.5 = ((f32[128,1,1,64]{3,2,1,0:T(1,128)}), f32[128,1,1,64]{3,2,1,0:T(1,128)S(1)}, u32[]{:S(2)}, u32[]{:S(2)}) async-start(f32[128,1,1,64]{3,2,1,0:T(1,128)} %bitcast.65), calls=%async_computation.5 | async-start | bytes 131072 | tf_op jit(solution)/shard_map/all_to_all | solution.py:37
  204.4 9.2 %all-to-all-done.5 = f32[128,1,1,64]{3,2,1,0:T(1,128)S(1)} async-done(((f32[128,1,1,64]{3,2,1,0:T(1,128)}), f32[128,1,1,64]{3,2,1,0:T(1,128)S(1)}, u32[]{:S(2)}, u32[]{:S(2)}) %all-to-all-start.5) | async-done | bytes 32800 | tf_op jit(solution)/shard_map/all_to_all | solution.py:37
  217.0 4.7 %collective-permute-start.9 = (f32[9,2,16,256]{3,2,1,0:T(8,128)S(1)}, f32[9,2,16,256]{3,2,1,0:T(8,128)S(1)}, u32[]{:S(2)}, u32[]{:S(2)}) collective-permute-start(f32[9,2,16,256]{3,2,1,0:T(8,128)S(1)} %get-tuple-element.118), channel_id=1, source_target_pairs={{8,0},{16,8},{24,16},{32,24},{40,32},{48,40},{56,48},{64,56},{72,6... | collective-permute-start | bytes 884744 | tf_op jit(solution)/shard_map/ppermute | solution.py:50
  222.7 5.3 %collective-permute-done.8 = f32[9,2,16,256]{3,2,1,0:T(8,128)S(1)} collective-permute-done((f32[9,2,16,256]{3,2,1,0:T(8,128)S(1)}, f32[9,2,16,256]{3,2,1,0:T(8,128)S(1)}, u32[]{:S(2)}, u32[]{:S(2)}) %collective-permute-start.8) | collective-permute-done | bytes 294944 | tf_op jit(solution)/shard_map/ppermute | solution.py:49
  228.7 3.0 %collective-permute-done.11 = f32[9,12,2,256]{3,2,1,0:T(2,128)S(1)} collective-permute-done((f32[9,12,2,256]{3,2,1,0:T(2,128)S(1)}, f32[9,12,2,256]{3,2,1,0:T(2,128)S(1)}, u32[]{:S(2)}, u32[]{:S(2)}) %collective-permute-start.11) | collective-permute-done | bytes 221216 | tf_op jit(solution)/shard_map/ppermute | solution.py:50
  231.7 3.1 %collective-permute-done.10 = f32[9,12,2,256]{3,2,1,0:T(2,128)S(1)} collective-permute-done((f32[9,12,2,256]{3,2,1,0:T(2,128)S(1)}, f32[9,12,2,256]{3,2,1,0:T(2,128)S(1)}, u32[]{:S(2)}, u32[]{:S(2)}) %collective-permute-start.10) | collective-permute-done | bytes 221216 | tf_op jit(solution)/shard_map/ppermute | solution.py:49
  236.8 3.8 %fusion.32 = f32[8,10,18,256]{3,2,1,0:T(8,128)S(1)} fusion(f32[9,12,2,256]{3,2,1,0:T(2,128)S(1)} %collective-permute-done.10, f32[9,2,16,256]{3,2,1,0:T(8,128)S(1)} %collective-permute-done.9, f32[9,2,16,256]{3,2,1,0:T(8,128)S(1)} %collective-permute-done.8, f32[1,8,16,256]{3,2,1,0:T(8,128)S(1)} %broadcast_in_dim_reshape.12, ...), kind=kLoop, calls=%fused_computation.53 | loop fusion | flops 11427840 | bytes 11427904 | tf_op jit(solution)/shard_map/sub | solution.py:155
  241.4 2.2 fusion.74
  (359 shorter events, 69.1 us)
Async XLA Ops:
  0.6 36.0 %copy-start = (f32[24,24]{1,0:T(8,128)S(1)}, f32[24,24]{1,0:T(8,128)}, u32[]{:S(2)}) copy-start(f32[24,24]{1,0:T(8,128)} %param.19) | copy-start | bytes 6916
  2.3 133.4 %copy-start.11 = (s32[256]{0:T(256)}, s32[256]{0:T(256)S(1)}, u32[]{:S(2)}) copy-start(s32[256]{0:T(256)S(1)} %get-tuple-element.147) | copy-start | bytes 3076
  2.3 84.1 %copy-start.13 = (s32[2,64]{1,0:T(2,128)}, s32[2,64]{1,0:T(2,128)S(1)}, u32[]{:S(2)}) copy-start(s32[2,64]{1,0:T(2,128)S(1)} %get-tuple-element.144) | copy-start | bytes 1540
  2.3 84.1 %copy-start.15 = (s32[2,64]{1,0:T(2,128)}, s32[2,64]{1,0:T(2,128)S(1)}, u32[]{:S(2)}) copy-start(s32[2,64]{1,0:T(2,128)S(1)} %get-tuple-element.145) | copy-start | bytes 1540
  3.0 84.5 %copy-start.19 = (s32[512]{0:T(512)}, s32[512]{0:T(512)S(1)}, u32[]{:S(2)}) copy-start(s32[512]{0:T(512)S(1)} %multiply_add_fusion.3) | copy-start | bytes 6148
  7.0 22.1 %all-to-all-start = ((f32[128,1,1,512]{3,2,1,0:T(1,128)}), f32[128,1,1,512]{3,2,1,0:T(1,128)S(1)}, u32[]{:S(2)}, u32[]{:S(2)}) async-start(f32[128,1,1,512]{3,2,1,0:T(1,128)} %reshape_transpose_transpose_reshape_reshape_reshape.24), calls=%async_computation | async-start | bytes 524288 | tf_op jit(solution)/shard_map/all_to_all | solution.py:37
  38.7 18.2 %copy-start.29 = (s32[128]{0:T(128)S(1)}, s32[128]{0:T(128)}, u32[]{:S(2)}) copy-start(s32[128]{0:T(128)} %get-tuple-element.148) | copy-start | bytes 1540
  38.7 18.2 %copy-start.32 = (s32[128]{0:T(128)S(1)}, s32[128]{0:T(128)}, u32[]{:S(2)}) copy-start(s32[128]{0:T(128)} %get-tuple-element.149) | copy-start | bytes 1540
  41.0 14.1 %all-to-all-start.1 = ((f32[128,1,1,64]{3,2,1,0:T(1,128)}), f32[128,1,1,64]{3,2,1,0:T(1,128)S(1)}, u32[]{:S(2)}, u32[]{:S(2)}) async-start(f32[128,1,1,64]{3,2,1,0:T(1,128)} %bitcast.16), calls=%async_computation.1 | async-start | bytes 131072 | tf_op jit(solution)/shard_map/all_to_all | solution.py:37
  58.2 12.1 %collective-permute-start = (f32[9,2,16,256]{3,2,1,0:T(8,128)}, f32[9,2,16,256]{3,2,1,0:T(8,128)S(1)}, u32[]{:S(2)}, u32[]{:S(2)}) collective-permute-start(f32[9,2,16,256]{3,2,1,0:T(8,128)} %get-tuple-element.121), channel_id=1, source_target_pairs={{0,8},{8,16},{16,24},{24,32},{32,40},{40,48},{48,56},{56,64},{64,7... | collective-permute-start | bytes 884744 | tf_op jit(solution)/shard_map/ppermute | solution.py:49
  59.1 11.2 %collective-permute-start.1 = (f32[9,2,16,256]{3,2,1,0:T(8,128)}, f32[9,2,16,256]{3,2,1,0:T(8,128)S(1)}, u32[]{:S(2)}, u32[]{:S(2)}) collective-permute-start(f32[9,2,16,256]{3,2,1,0:T(8,128)} %get-tuple-element.122), channel_id=1, source_target_pairs={{8,0},{16,8},{24,16},{32,24},{40,32},{48,40},{56,48},{64,56},{72,6... | collective-permute-start | bytes 884744 | tf_op jit(solution)/shard_map/ppermute | solution.py:50
  70.6 4.3 %collective-permute-start.3 = (f32[9,12,2,256]{3,1,2,0:T(8,128)S(1)}, f32[9,12,2,256]{3,1,2,0:T(8,128)S(1)}, u32[]{:S(2)}, u32[]{:S(2)}) collective-permute-start(f32[9,12,2,256]{3,1,2,0:T(8,128)S(1)} %copy.94), channel_id=1, source_target_pairs={{1,0},{2,1},{3,2},{4,3},{5,4},{6,5},{7,6},{0,7},{9,8},{10,9},{11,1... | collective-permute-start | bytes 663560 | tf_op jit(solution)/shard_map/ppermute | solution.py:50
  70.6 7.4 %collective-permute-start.2 = (f32[9,12,2,256]{3,1,2,0:T(8,128)S(1)}, f32[9,12,2,256]{3,1,2,0:T(8,128)S(1)}, u32[]{:S(2)}, u32[]{:S(2)}) collective-permute-start(f32[9,12,2,256]{3,1,2,0:T(8,128)S(1)} %copy.93), channel_id=1, source_target_pairs={{0,1},{1,2},{2,3},{3,4},{4,5},{5,6},{6,7},{7,0},{8,9},{9,10},{10,1... | collective-permute-start | bytes 663560 | tf_op jit(solution)/shard_map/ppermute | solution.py:49
  87.5 21.3 %copy-start.26 = (s32[512]{0:T(512)S(1)}, s32[512]{0:T(512)}, u32[]{:S(2)}) copy-start(s32[512]{0:T(512)} %param.13) | copy-start | bytes 6148
  89.6 18.3 %all-to-all-start.2 = ((f32[128,1,1,512]{3,2,1,0:T(1,128)}), f32[128,1,1,512]{3,2,1,0:T(1,128)S(1)}, u32[]{:S(2)}, u32[]{:S(2)}) async-start(f32[128,1,1,512]{3,2,1,0:T(1,128)} %reshape_transpose_transpose_reshape_reshape_reshape.25), calls=%async_computation.2 | async-start | bytes 524288 | tf_op jit(solution)/shard_map/all_to_all | solution.py:37
  97.2 27.4 %copy-start.2 = (f32[6,8,512]{2,1,0:T(8,128)}, f32[6,8,512]{2,1,0:T(8,128)S(1)}, u32[]{:S(2)}) copy-start(f32[6,8,512]{2,1,0:T(8,128)S(1)} %multiply_add_fusion.1) | copy-start | bytes 294916
  117.5 18.2 %copy-start.30 = (s32[128]{0:T(128)S(1)}, s32[128]{0:T(128)}, u32[]{:S(2)}) copy-start(s32[128]{0:T(128)} %get-tuple-element.148) | copy-start | bytes 1540
  117.5 18.2 %copy-start.33 = (s32[128]{0:T(128)S(1)}, s32[128]{0:T(128)}, u32[]{:S(2)}) copy-start(s32[128]{0:T(128)} %get-tuple-element.149) | copy-start | bytes 1540
  119.8 14.1 %all-to-all-start.3 = ((f32[128,1,1,64]{3,2,1,0:T(1,128)}), f32[128,1,1,64]{3,2,1,0:T(1,128)S(1)}, u32[]{:S(2)}, u32[]{:S(2)}) async-start(f32[128,1,1,64]{3,2,1,0:T(1,128)} %bitcast.42), calls=%async_computation.3 | async-start | bytes 131072 | tf_op jit(solution)/shard_map/all_to_all | solution.py:37
  136.9 12.1 %collective-permute-start.4 = (f32[9,2,16,256]{3,2,1,0:T(8,128)}, f32[9,2,16,256]{3,2,1,0:T(8,128)S(1)}, u32[]{:S(2)}, u32[]{:S(2)}) collective-permute-start(f32[9,2,16,256]{3,2,1,0:T(8,128)} %get-tuple-element.119), channel_id=1, source_target_pairs={{0,8},{8,16},{16,24},{24,32},{32,40},{40,48},{48,56},{56,64},{64,7... | collective-permute-start | bytes 884744 | tf_op jit(solution)/shard_map/ppermute | solution.py:49
  137.8 11.2 %collective-permute-start.5 = (f32[9,2,16,256]{3,2,1,0:T(8,128)S(1)}, f32[9,2,16,256]{3,2,1,0:T(8,128)S(1)}, u32[]{:S(2)}, u32[]{:S(2)}) collective-permute-start(f32[9,2,16,256]{3,2,1,0:T(8,128)S(1)} %get-tuple-element.120), channel_id=1, source_target_pairs={{8,0},{16,8},{24,16},{32,24},{40,32},{48,40},{56,48},{64,56},{72,6... | collective-permute-start | bytes 884744 | tf_op jit(solution)/shard_map/ppermute | solution.py:50
  149.2 6.6 %collective-permute-start.6 = (f32[9,12,2,256]{3,2,1,0:T(2,128)S(1)}, f32[9,12,2,256]{3,2,1,0:T(2,128)S(1)}, u32[]{:S(2)}, u32[]{:S(2)}) collective-permute-start(f32[9,12,2,256]{3,2,1,0:T(2,128)S(1)} %get-tuple-element.113), channel_id=1, source_target_pairs={{0,1},{1,2},{2,3},{3,4},{4,5},{5,6},{6,7},{7,0},{8,9},{9,10},{10,1... | collective-permute-start | bytes 663560 | tf_op jit(solution)/shard_map/ppermute | solution.py:49
  149.2 6.6 %collective-permute-start.7 = (f32[9,12,2,256]{3,2,1,0:T(2,128)S(1)}, f32[9,12,2,256]{3,2,1,0:T(2,128)S(1)}, u32[]{:S(2)}, u32[]{:S(2)}) collective-permute-start(f32[9,12,2,256]{3,2,1,0:T(2,128)S(1)} %get-tuple-element.114), channel_id=1, source_target_pairs={{1,0},{2,1},{3,2},{4,3},{5,4},{6,5},{7,6},{0,7},{9,8},{10,9},{11,1... | collective-permute-start | bytes 663560 | tf_op jit(solution)/shard_map/ppermute | solution.py:50
  165.4 23.3 %copy-start.28 = (s32[512]{0:T(512)S(1)}, s32[512]{0:T(512)}, u32[]{:S(2)}) copy-start(s32[512]{0:T(512)} %param.13) | copy-start | bytes 6148
  167.5 20.3 %all-to-all-start.4 = ((f32[128,1,1,512]{3,2,1,0:T(1,128)}), f32[128,1,1,512]{3,2,1,0:T(1,128)S(1)}, u32[]{:S(2)}, u32[]{:S(2)}) async-start(f32[128,1,1,512]{3,2,1,0:T(1,128)} %reshape_transpose_transpose_reshape_reshape_reshape.26), calls=%async_computation.4 | async-start | bytes 524288 | tf_op jit(solution)/shard_map/all_to_all | solution.py:37
  197.4 18.2 %copy-start.31 = (s32[128]{0:T(128)S(1)}, s32[128]{0:T(128)}, u32[]{:S(2)}) copy-start(s32[128]{0:T(128)} %get-tuple-element.148) | copy-start | bytes 1540
  197.4 18.2 %copy-start.34 = (s32[128]{0:T(128)S(1)}, s32[128]{0:T(128)}, u32[]{:S(2)}) copy-start(s32[128]{0:T(128)} %get-tuple-element.149) | copy-start | bytes 1540
  199.6 14.1 %all-to-all-start.5 = ((f32[128,1,1,64]{3,2,1,0:T(1,128)}), f32[128,1,1,64]{3,2,1,0:T(1,128)S(1)}, u32[]{:S(2)}, u32[]{:S(2)}) async-start(f32[128,1,1,64]{3,2,1,0:T(1,128)} %bitcast.65), calls=%async_computation.5 | async-start | bytes 131072 | tf_op jit(solution)/shard_map/all_to_all | solution.py:37
  216.1 11.9 %collective-permute-start.8 = (f32[9,2,16,256]{3,2,1,0:T(8,128)S(1)}, f32[9,2,16,256]{3,2,1,0:T(8,128)S(1)}, u32[]{:S(2)}, u32[]{:S(2)}) collective-permute-start(f32[9,2,16,256]{3,2,1,0:T(8,128)S(1)} %get-tuple-element.117), channel_id=1, source_target_pairs={{0,8},{8,16},{16,24},{24,32},{32,40},{40,48},{48,56},{56,64},{64,7... | collective-permute-start | bytes 884744 | tf_op jit(solution)/shard_map/ppermute | solution.py:49
  217.0 11.0 %collective-permute-start.9 = (f32[9,2,16,256]{3,2,1,0:T(8,128)S(1)}, f32[9,2,16,256]{3,2,1,0:T(8,128)S(1)}, u32[]{:S(2)}, u32[]{:S(2)}) collective-permute-start(f32[9,2,16,256]{3,2,1,0:T(8,128)S(1)} %get-tuple-element.118), channel_id=1, source_target_pairs={{8,0},{16,8},{24,16},{32,24},{40,32},{48,40},{56,48},{64,56},{72,6... | collective-permute-start | bytes 884744 | tf_op jit(solution)/shard_map/ppermute | solution.py:50
  228.2 3.5 %collective-permute-start.11 = (f32[9,12,2,256]{3,2,1,0:T(2,128)S(1)}, f32[9,12,2,256]{3,2,1,0:T(2,128)S(1)}, u32[]{:S(2)}, u32[]{:S(2)}) collective-permute-start(f32[9,12,2,256]{3,2,1,0:T(2,128)S(1)} %get-tuple-element.111), channel_id=1, source_target_pairs={{1,0},{2,1},{3,2},{4,3},{5,4},{6,5},{7,6},{0,7},{9,8},{10,9},{11,1... | collective-permute-start | bytes 663560 | tf_op jit(solution)/shard_map/ppermute | solution.py:50
  228.2 6.6 %collective-permute-start.10 = (f32[9,12,2,256]{3,2,1,0:T(2,128)S(1)}, f32[9,12,2,256]{3,2,1,0:T(2,128)S(1)}, u32[]{:S(2)}, u32[]{:S(2)}) collective-permute-start(f32[9,12,2,256]{3,2,1,0:T(2,128)S(1)} %get-tuple-element.112), channel_id=1, source_target_pairs={{0,1},{1,2},{2,3},{3,4},{4,5},{5,6},{6,7},{7,0},{8,9},{9,10},{10,1... | collective-permute-start | bytes 663560 | tf_op jit(solution)/shard_map/ppermute | solution.py:49
  (21 other events, 160.9 us)
where the time goes:
time: 248 us; the launch traced here: 244 us
  waiting for transfers between devices  89.3 us (36%)
  starting transfers between devices  63.5 us (26%)
  matrix products  33.5 us (14%)
  other arithmetic  30.2 us (12%)
  local copies, waits for them, and re-layouts  24.4 us (10%)
  between operations  3.04 us (1%)
    all_to_all x6, waiting for transfers between devices, exchange_both(): parts = lax.all_to_all(parts, axis, split_axis=0, concat_axis=0, tiled=True)  56.8 us
    all_to_all x6, starting transfers between devices, exchange_both(): parts = lax.all_to_all(parts, axis, split_axis=0, concat_axis=0, tiled=True)  42.8 us
    ppermute x6, waiting for transfers between devices, padded_2(): before = lax.ppermute(last, axis, up)  25.9 us
    ppermute x6, starting transfers between devices, padded_2(): after = lax.ppermute(first, axis, down)  17.1 us
    sub x4, other arithmetic, phase_update(): return center - TIME_STEP * mobility[:, None, None, None] * driving  13.4 us
    dot_general x3, matrix products, shards(): lax.dot_general(inbox, element_pick, (((0,), (1,)), ((), ())), precision=...  6.97 us
    ppermute x6, waiting for transfers between devices, padded_2(): after = lax.ppermute(first, axis, down)  6.73 us
    dot_general x3, matrix products, mechanics(): jnp.dot(latent_hardening, jnp.abs(slip_amount), precision=HIGHEST, prefer...  6.38 us
  transfers between devices with their start and end apart: 18, of which 14 were waited for; matrix products, arithmetic and copies ran while one was open for 2% of the time, Pallas kernels for 0%

commit v1 on v0

v1 whole, which is shorter than its diff:
```python
import functools

import jax
import jax.numpy as jnp
from jax import lax
from jax.experimental import pallas as pl
from jax.experimental.pallas import tpu as pltpu
from jax.sharding import PartitionSpec as P

ITERS = 4
STEPS = 3
SUB = 2

CROSS_TERM = 1.5
DRIVE_SCALE = 6.0
TIME_STEP = 0.02
SLIP_RATE = 0.1
HARDENING = 0.5
LANES = 128
BF16 = jnp.bfloat16
F32 = jnp.float32
VMEM_BYTES = 24 << 20


def two_terms(value):
    high = value.astype(BF16)
    low = (value - high.astype(F32)).astype(BF16)
    return high, low


def two_terms_outside(value):
    high = lax.reduce_precision(value, 8, 7)
    low = lax.reduce_precision(value - high, 8, 7)
    return high.astype(BF16), low.astype(BF16)


def product(left, right):
    return lax.dot_general(
        left, right, (((1,), (0,)), ((), ())), preferred_element_type=F32
    )


def product_rows(left, right):
    return lax.dot_general(
        left, right, (((1,), (1,)), ((), ())), preferred_element_type=F32
    )


def call(kernel, shapes, scratch=(), **options):
    return pl.pallas_call(
        kernel,
        out_shape=shapes,
        scratch_shapes=list(scratch),
        compiler_params=pltpu.CompilerParams(vmem_limit_bytes=VMEM_BYTES),
        **options,
    )


def shape(*dims):
    return jax.ShapeDtypeStruct(dims, F32)


def into_slots(slots_row, values, slots_all):
    items = values.shape[1]
    slot = lax.broadcasted_iota(jnp.int32, (slots_all, items), 0)
    hit = (slot == slots_row).astype(F32).astype(BF16)
    high, low = two_terms(values)
    return product_rows(hit, high) + product_rows(hit, low)


def out_of_slots(slots_col, mail):
    items = slots_col.shape[0]
    slots_all = mail.shape[0]
    lane = lax.broadcasted_iota(jnp.int32, (items, LANES), 1)
    hit = jnp.concatenate(
        [
            (lane + start == slots_col).astype(F32).astype(BF16)
            for start in range(0, slots_all, LANES)
        ],
        axis=1,
    )
    high, low = two_terms(mail)
    return jnp.transpose(product(hit, high) + product(hit, low))


def pack_state_kernel(anchor, strain, stress, resist, active, out):
    rows = strain.shape[0] + stress.shape[0] + resist.shape[0] + active.shape[0]
    values = jnp.concatenate(
        [
            strain[...],
            stress[...],
            resist[...],
            active[...].astype(F32),
            jnp.zeros((out.shape[1] - rows, strain.shape[1]), F32),
        ],
        axis=0,
    )
    out[...] = into_slots(anchor[...], values, out.shape[0])


def unpack_state_kernel(mailbox, mail, strain, stress, resist, active):
    values = out_of_slots(mailbox[...], mail[...])
    start = 0
    for part in (strain, stress, resist, active):
        part[...] = values[start : start + part.shape[0]]
        start += part.shape[0]


def pack_result_kernel(mailbox, stress, resist, out):
    rows = stress.shape[0] + resist.shape[0]
    values = jnp.concatenate(
        [
            stress[...],
            resist[...],
            jnp.zeros((out.shape[1] - rows, stress.shape[1]), F32),
        ],
        axis=0,
    )
    out[...] = into_slots(mailbox[...], values, out.shape[0])


def unpack_result_kernel(anchor, mail, stress, resist):
    values = out_of_slots(anchor[...], mail[...])
    stress[...] = values[: stress.shape[0]]
    resist[...] = values[stress.shape[0] : stress.shape[0] + resist.shape[0]]


def routed(packed):
    count = lax.axis_size(("gx", "gz"))
    slots, feature = packed.shape
    sent = packed.reshape(count, slots // count, feature)
    got = lax.all_to_all(sent, ("gx", "gz"), split_axis=0, concat_axis=0, tiled=True)
    return got.reshape(slots, feature)


def bits(index, *sizes):
    found = []
    for size in reversed(sizes):
        found.append(index % size)
        index = index // size
    return list(reversed(found))


def row_map():
    to_half, to_i, to_bx, to_pair, to_qx, to_qz, _ = bits(
        jnp.arange(128, dtype=jnp.int32)[:, None], 2, 2, 2, 2, 2, 2, 2
    )
    i, bx, qx, pair, half, qz, _ = bits(
        jnp.arange(128, dtype=jnp.int32)[None, :], 2, 2, 2, 2, 2, 2, 2
    )
    same = (
        (to_half == half)
        & (to_i == i)
        & (to_bx == bx)
        & (to_pair == pair)
        & (to_qx == qx)
        & (to_qz == qz)
    )
    half_map = jnp.where(same, 0.125, 0.0)
    return jnp.concatenate([half_map, half_map], axis=1).astype(BF16)


def lane_map(size_y):
    by, qy, _ = bits(jnp.arange(size_y, dtype=jnp.int32)[:, None], size_y // 4, 2, 2)
    to_qy, to_half, to_by = bits(
        jnp.arange(size_y, dtype=jnp.int32)[None, :], 2, 2, size_y // 4
    )
    found = (by == to_by) & (qy == to_qy)
    maps = [jnp.where(found & (to_half == half), 1.0, 0.0) for half in range(2)]
    return jnp.concatenate(maps + maps, axis=0).astype(BF16)


def spread_map(size_y):
    by, qy, _ = bits(jnp.arange(size_y, dtype=jnp.int32)[None, :], size_y // 4, 2, 2)
    of_qy, _, of_by = bits(jnp.arange(size_y, dtype=jnp.int32)[:, None], 2, 2, size_y // 4)
    found = jnp.where((by == of_by) & (qy == of_qy), 1.0, 0.0)
    return jnp.concatenate([found, found], axis=0).astype(BF16)


def repeat_map():
    to_qy, to_qx, _, to_qz, _ = bits(
        jnp.arange(32, dtype=jnp.int32)[:, None], 2, 2, 2, 2, 2
    )
    qx, qz, qy = bits(jnp.arange(8, dtype=jnp.int32)[None, :], 2, 2, 2)
    found = jnp.where((to_qy == qy) & (to_qx == qx) & (to_qz == qz), 1.0, 0.0)
    return jnp.concatenate([found, found], axis=1).astype(BF16)


def restrict_kernel(grains, rows, lanes, weights):
    orders, size_x, size_z, size_y = grains.shape
    lefts = []
    for pair in range(orders // 2):
        parts = []
        for order in (2 * pair, 2 * pair + 1):
            for coarse in range(size_x // 2):
                low = grains[order, 2 * coarse]
                high = grains[order, 2 * coarse + 1]
                parts.append(low * low + high * high)
        summed = jnp.concatenate(parts, axis=0)
        moved = product(rows[...], jnp.concatenate(two_terms(summed), axis=0))
        high, low = two_terms(moved)
        lefts.append(
            jnp.concatenate([high[:64], high[64:], low[:64], low[64:]], axis=1)
        )
    found = product(jnp.concatenate(lefts, axis=0), lanes[...])
    row = lax.broadcasted_iota(jnp.int32, (found.shape[0], LANES), 0)
    picked = jnp.where(row % 2 == 0, found[:, :LANES], found[:, LANES:])
    for order in range(orders):
        for tile in range(4):
            start = (order * 4 + tile) * 8
            weights[order * 8 : order * 8 + 8, tile * LANES : (tile + 1) * LANES] = picked[
                start : start + 8
            ]


def prolonged(stored, repeat, spread, energy):
    high, low = two_terms(stored)
    rows = product(repeat, jnp.concatenate([high, low], axis=0))
    row = lax.broadcasted_iota(jnp.int32, rows.shape, 0)
    lane = lax.broadcasted_iota(jnp.int32, rows.shape, 1)
    rows = jnp.where((row // 4) % 2 == (lane // 64) % 2, rows, 0.0)
    tiles = [
        jnp.concatenate(
            [rows[:16, t * LANES : (t + 1) * LANES], rows[16:, t * LANES : (t + 1) * LANES]],
            axis=1,
        )
        for t in range(4)
    ]
    left = jnp.concatenate(two_terms(jnp.concatenate(tiles, axis=0)), axis=1)
    cells = product(left, spread)
    for bx in range(2):
        for pair in range(2):
            for qx in range(2):
                start = ((bx * 2 + pair) * 2 + qx) * 8
                energy[bx * 2 + qx, pair * 8 : pair * 8 + 8] = cells[start : start + 8]


def mechanics_kernel(
    weights,
    strain,
    stress,
    resist,
    active,
    tensor_map,
    harden_map,
    active_map,
    repeat,
    spread,
    stress_out,
    resist_out,
    energy,
    tensor,
    rates,
    amounts,
):
    systems = active.shape[0]
    points = resist.shape[0] // systems
    items = weights.shape[1]
    high, low = two_terms(weights[...])
    tensor[...] = product(tensor_map[...], jnp.concatenate([high, low, high], axis=0))
    rates[...] = product(active_map[...], active[...].astype(BF16)) * SLIP_RATE

    def tile_step(tile, carry):
        lanes = pl.ds(pl.multiple_of(tile * LANES, LANES), LANES)
        trial = [
            stress[points * c : points * (c + 1), lanes]
            + 2.0 * strain[points * c : points * (c + 1), lanes]
            for c in range(6)
        ]

        def sweep(_, now):
            sums = [jnp.zeros((points, LANES), F32) for _ in range(6)]
            for a in range(systems):
                rows = pl.ds(a * points, points)
                parts = [tensor[pl.ds((a * 6 + c) * points, points), lanes] for c in range(6)]
                resolved = (
                    (parts[0] * now[0] + parts[1] * now[1])
                    + (parts[2] * now[2] + parts[3] * now[3])
                    + (parts[4] * now[4] + parts[5] * now[5])
                )
                slip = rates[rows, lanes] * resolved / (resist[rows, lanes] + jnp.abs(resolved))
                amounts[rows, lanes] = jnp.abs(slip)
                sums = [sums[c] + parts[c] * slip for c in range(6)]
            return tuple(trial[c] - 2.0 * sums[c] for c in range(6))

        now = lax.fori_loop(0, ITERS, sweep, tuple(trial))
        for c in range(6):
            stress_out[points * c : points * (c + 1), lanes] = now[c]
        return carry

    lax.fori_loop(0, items // LANES, tile_step, 0)
    amount = amounts[...]
    high, low = two_terms(amount)
    harden = product(harden_map[...], jnp.concatenate([high, low, high], axis=0))
    grown = resist[...] + HARDENING * harden
    resist_out[...] = grown
    work = grown * amount
    stored = work[:points]
    for a in range(1, systems):
        stored = stored + work[points * a : points * (a + 1)]
    prolonged(stored, repeat[...], spread[...], energy)


def phase_kernel(
    grains,
    x_before,
    x_after,
    z_before,
    z_after,
    energy,
    mobility,
    grain_state,
    out,
    x_first,
    x_last,
    z_first,
    z_last,
):
    orders, size_x, size_z, size_y = grains.shape
    row = lax.broadcasted_iota(jnp.int32, (size_z, size_y), 0)
    for x in range(size_x):
        center = [grains[order, x] for order in range(orders)]
        squares = [value * value for value in center]
        total = squares[0]
        for order in range(1, orders):
            total = total + squares[order]
        shared = 2.0 * CROSS_TERM * total + 5.0
        cell = energy[x // 2]
        for order in range(orders):
            value = center[order]
            lower = grains[order, x - 1] if x > 0 else x_before[order]
            upper = grains[order, x + 1] if x < size_x - 1 else x_after[order]
            below = jnp.where(
                row == 0, z_before[order, x : x + 1], pltpu.roll(value, 1, 0)
            )
            above = jnp.where(
                row == size_z - 1,
                z_after[order, x : x + 1],
                pltpu.roll(value, size_z - 1, 0),
            )
            around = (
                (lower + upper)
                + (below + above)
                + (pltpu.roll(value, 1, 1) + pltpu.roll(value, size_y - 1, 1))
            )
            share = 2.0 * DRIVE_SCALE * (1.0 - grain_state[order])
            factor = shared + share * cell - 2.0 * squares[order]
            new = value + (TIME_STEP * mobility[order]) * (around - value * factor)
            out[order, x] = new
            if x == 0:
                x_first[order] = new
            if x == size_x - 1:
                x_last[order] = new
            z_first[order, x : x + 1] = new[:1]
            z_last[order, x : x + 1] = new[size_z - 1 :]


def neighbours(first, last, axis):
    size = lax.axis_size(axis)
    up = [(i, (i + 1) % size) for i in range(size)]
    down = [(j, i) for i, j in up]
    return lax.ppermute(last, axis, up), lax.ppermute(first, axis, down)


def pair_rank(owners, count_all):
    onehot = (owners[:, None] == jnp.arange(count_all, dtype=jnp.int32)[None, :]).astype(jnp.int32)
    before = jnp.cumsum(onehot, axis=0) - onehot
    return jnp.sum(before * onehot, axis=1)


def over_points(matrix, points):
    rows, columns = matrix.shape
    same = jnp.eye(points, dtype=F32)
    spread = matrix[:, None, :, None] * same[None, :, None, :]
    return spread.reshape(rows * points, columns * points)


def shards(
    grains,
    block_owner,
    element_anchor,
    strain_step,
    stress,
    resistance,
    slip_active,
    orientation_schmid,
    latent_hardening,
    mobility,
    grain_state,
):
    count_all = lax.axis_size(("gx", "gz"))
    owners = block_owner.reshape(-1)
    per_dev = owners.shape[0]
    capacity = 2 * per_dev // count_all
    slots_all = count_all * capacity
    orders, size_x, size_z, size_y = grains.shape
    points = stress.shape[1]
    systems = resistance.shape[0]
    tensors, forces = 6 * points, systems * points
    wide = -(-(2 * tensors + forces + systems) // LANES) * LANES
    narrow = -(-(tensors + forces) // LANES) * LANES

    outbox = call(pack_state_kernel, shape(slots_all, wide))(
        element_anchor.reshape(1, per_dev),
        strain_step.reshape(tensors, per_dev),
        stress.reshape(tensors, per_dev),
        resistance.reshape(forces, per_dev),
        slip_active,
    )
    inbox = routed(outbox)

    mailbox = owners * capacity + pair_rank(owners, count_all)
    mailbox_col = jnp.broadcast_to(mailbox[:, None], (per_dev, LANES))
    anchor_col = jnp.broadcast_to(element_anchor[:, None], (per_dev, LANES))
    schmid = orientation_schmid.reshape(orders, systems * 6).T
    schmid_high, schmid_low = two_terms_outside(schmid)
    tensor_map = jnp.concatenate(
        [over_points(part, points).astype(BF16) for part in (schmid_high, schmid_high, schmid_low)],
        axis=1,
    )
    harden_high, harden_low = two_terms_outside(latent_hardening)
    harden_map = jnp.concatenate(
        [over_points(part, points).astype(BF16) for part in (harden_high, harden_high, harden_low)],
        axis=1,
    )
    active_map = jnp.repeat(jnp.eye(systems, dtype=F32), points, axis=0).astype(BF16)
    rows, lanes = row_map(), lane_map(size_y)
    repeat, spread = repeat_map(), spread_map(size_y)

    edges = (grains[:, 0], grains[:, size_x - 1], grains[:, :, 0], grains[:, :, size_z - 1])
    strain_h = stress_h = resist_h = active_h = None
    scalars = pl.BlockSpec(memory_space=pltpu.SMEM)
    whole = pl.BlockSpec(memory_space=pltpu.VMEM)
    for cycle in range(STEPS):
        x_before, x_after = neighbours(edges[0], edges[1], "gx")
        z_before, z_after = neighbours(edges[2], edges[3], "gz")
        weights = call(restrict_kernel, shape(orders * points, per_dev))(grains, rows, lanes)
        if cycle == 0:
            strain_h, stress_h, resist_h, active_h = call(
                unpack_state_kernel,
                (
                    shape(tensors, per_dev),
                    shape(tensors, per_dev),
                    shape(forces, per_dev),
                    shape(systems, per_dev),
                ),
            )(mailbox_col, inbox)
        stress_h, resist_h, energy = call(
            mechanics_kernel,
            (
                shape(tensors, per_dev),
                shape(forces, per_dev),
                shape(size_x // 2, size_z, size_y),
            ),
            scratch=(
                pltpu.VMEM((6 * forces, per_dev), F32),
                pltpu.VMEM((forces, per_dev), F32),
                pltpu.VMEM((forces, per_dev), F32),
            ),
        )(
            weights,
            strain_h,
            stress_h,
            resist_h,
            active_h,
            tensor_map,
            harden_map,
            active_map,
            repeat,
            spread,
        )
        for inner in range(SUB):
            if inner > 0:
                x_before, x_after = neighbours(edges[0], edges[1], "gx")
                z_before, z_after = neighbours(edges[2], edges[3], "gz")
            grains, *edges = call(
                phase_kernel,
                (
                    shape(orders, size_x, size_z, size_y),
                    shape(orders, size_z, size_y),
                    shape(orders, size_z, size_y),
                    shape(orders, size_x, size_y),
                    shape(orders, size_x, size_y),
                ),
                in_specs=[whole] * 6 + [scalars] * 2,
            )(grains, x_before, x_after, z_before, z_after, energy, mobility, grain_state)
    outbox = call(pack_result_kernel, shape(slots_all, narrow))(
        mailbox.reshape(1, per_dev), stress_h, resist_h
    )
    inbox = routed(outbox)
    stress, resistance = call(
        unpack_result_kernel, (shape(tensors, per_dev), shape(forces, per_dev))
    )(anchor_col, inbox)
    return (
        grains,
        stress.reshape(6, points, per_dev),
        resistance.reshape(systems, points, per_dev),
    )


def solution(mesh):
    return jax.shard_map(
        shards,
        mesh=mesh,
        in_specs=(
            P(None, "gx", "gz", None),
            P("gx", "gz", None),
            P(("gx", "gz")),
            P(None, None, ("gx", "gz")),
            P(None, None, ("gx", "gz")),
            P(None, None, ("gx", "gz")),
            P(None, ("gx", "gz")),
            P(),
            P(),
            P(),
            P(),
        ),
        out_specs=(
            P(None, "gx", "gz", None),
            P(None, None, ("gx", "gz")),
            P(None, None, ("gx", "gz")),
        ),
        check_vma=False,
    )
```

time: 248 us -> 151 us (0.61)
  waiting for transfers between devices: 89.3 us -> 17.9 us
  matrix products: 33.5 us -> 0 us
  Pallas kernels: 0 us -> 29 us
  other arithmetic: 30.2 us -> 7.22 us
  local copies, waits for them, and re-layouts: 24.4 us -> 27.4 us
  starting transfers between devices: 63.5 us -> 66.5 us
    all_to_all x6 -> x2, waiting for transfers between devices: 56.8 us -> 0.01 us  [routed(): lax.all_to_all(sent, ('gx', 'gz'), split_axis=0, concat_axis=0, tiled=True)]
    dot_general x24 -> x0, matrix products: 33.5 us -> none  [the longest x3 6.97 us: shards(): lax.dot_general(inbox, element_pick, (((0,), (1,)), ((), ())), precision=...]
    ppermute x12 -> x24, starting transfers between devices: 20.7 us -> 50.1 us  [neighbours(): return (lax.ppermute(last, axis, up), lax.ppermute(first, axis, down))]
    pallas_call x0 -> x16, Pallas kernels: none -> 29 us  [the longest x3 10.3 us: shards(): call(mechanics_kernel, (shape(tensors, per_dev), shape(forces, per_dev),...]
    all_to_all x6 -> x2, starting transfers between devices: 42.8 us -> 16.5 us  [routed(): lax.all_to_all(sent, ('gx', 'gz'), split_axis=0, concat_axis=0, tiled=True)]
    ppermute x12 -> x24, waiting for transfers between devices: 32.6 us -> 17.9 us  [neighbours(): return (lax.ppermute(last, axis, up), lax.ppermute(first, axis, down))]
    sub x59 -> x0, other arithmetic: 13.8 us -> none  [the longest x4 13.4 us: phase_update(): return center - TIME_STEP * mobility[:, None, None, None] * driving]
    convert_element_type x0 -> x8, local copies, waits for them, and re-layouts: none -> 12.1 us  [the longest x6 12 us: shards(): over_points(part, points).astype(BF16)]
  transfers between devices with their start and end apart: 18 -> 26, of which waited for: 14 -> 5; matrix products, arithmetic and copies ran while one was open for 2% -> 16% of each run, Pallas kernels for 0% -> 9%
where the time goes in v1:
time: 151 us; the launch traced here: 149 us
  starting transfers between devices  66.5 us (44%)
  Pallas kernels  29 us (19%)
  local copies, waits for them, and re-layouts  27.4 us (18%)
  waiting for transfers between devices  17.9 us (12%)
  other arithmetic  7.22 us (5%)
    ppermute x24, starting transfers between devices, neighbours(): return (lax.ppermute(last, axis, up), lax.ppermute(first, axis, down))  50.1 us
    ppermute x24, waiting for transfers between devices, neighbours(): return (lax.ppermute(last, axis, up), lax.ppermute(first, axis, down))  17.9 us
    all_to_all x2, starting transfers between devices, routed(): lax.all_to_all(sent, ('gx', 'gz'), split_axis=0, concat_axis=0, tiled=True)  16.5 us
    convert_element_type x6, local copies, waits for them, and re-layouts, shards(): over_points(part, points).astype(BF16)  12 us
    unnamed x64, local copies, waits for them, and re-layouts  11.6 us
    pallas_call x3, Pallas kernels, shards(): call(mechanics_kernel, (shape(tensors, per_dev), shape(forces, per_dev),...  10.3 us
    pallas_call x6, Pallas kernels, shards(): call(phase_kernel, (shape(orders, size_x, size_z, size_y), shape(orders,...  10.2 us
    convert_element_type x2, other arithmetic, shards(): over_points(part, points).astype(BF16)  4.37 us
  transfers between devices with their start and end apart: 26, of which 5 were waited for; matrix products, arithmetic and copies ran while one was open for 16% of the time, Pallas kernels for 9%

profile of v1, /device:TPU:0, one launch (start us, length us, event | category | flops | bytes accessed | tf_op | source)
XLA Modules:
  0.0 149.3 jit_solution(10814837684117858645)
XLA Ops:
  4.9 2.4 %shard_map.131 = f32[1024,384]{1,0:T(8,128)} custom-call(s32[1,512]{1,0:T(1,128)S(1)} %bitcast.64, f32[48,512]{1,0:T(8,128)S(1)} %bitcast.62, f32[48,512]{1,0:T(8,128)S(1)} %bitcast.63, f32[192,512]{1,0:T(8,128)S(1)} %bitcast.61, s32[24,512]{1,0:T(8,128)S(1)} %copy-done.13), custom_call_target="tpu_custom_call" | custom-call | tf_op jit(solution)/shard_map/pallas_call | solution.py:403
  7.3 11.2 %all-to-all-start = ((f32[128,8,384]{2,1,0:T(8,128)}), f32[128,8,384]{2,1,0:T(8,128)S(1)}, u32[]{:S(2)}, u32[]{:S(2)}) async-start(f32[128,8,384]{2,1,0:T(8,128)} %bitcast.11), calls=%async_computation | async-start | bytes 3145728 | tf_op jit(solution)/shard_map/all_to_all | solution.py:132
  18.5 1.7 %slice_bitcast_fusion = (f32[8,16,256]{2,1,0:T(8,128)}, f32[8,16,256]{2,1,0:T(8,128)}) fusion(f32[8,8,16,256]{3,2,1,0:T(8,128)} %grains.3), kind=kLoop, calls=%fused_computation.21 | loop fusion | bytes 524288 | tf_op jit(solution)/shard_map/squeeze | solution.py:430
  21.3 4.3 %collective-permute-start.1 = (f32[8,16,256]{2,1,0:T(8,128)}, f32[8,16,256]{2,1,0:T(8,128)}, u32[]{:S(2)}, u32[]{:S(2)}) collective-permute-start(f32[8,16,256]{2,1,0:T(8,128)} %get-tuple-element.87), channel_id=1, source_target_pairs={{8,0},{16,8},{24,16},{32,24},{40,32},{48,40},{56,48},{64,56},{72,6... | collective-permute-start | bytes 393224 | tf_op jit(solution)/shard_map/ppermute | solution.py:362
  28.1 3.0 %collective-permute-start.3 = (f32[8,8,256]{2,1,0:T(8,128)}, f32[8,8,256]{2,1,0:T(8,128)}, u32[]{:S(2)}, u32[]{:S(2)}) collective-permute-start(f32[8,8,256]{2,1,0:T(8,128)} %bitcast.54), channel_id=1, source_target_pairs={{1,0},{2,1},{3,2},{4,3},{5,4},{6,5},{7,6},{0,7},{9,8},{10,9},{11,1... | collective-permute-start | bytes 196616 | tf_op jit(solution)/shard_map/ppermute | solution.py:362
  31.8 2.9 %multiply_convert_fusion.1 = (bf16[144,8,8,8]{1,0,3,2:T(8,128)(2,1)}, bf16[144,8,8,8]{1,0,3,2:T(8,128)(2,1)}) fusion(f32[8,8]{0,1:T(8,128)S(1)} %copy.26, f32[144,8]{0,1:T(8,128)S(1)} %get-tuple-element.91, f32[144,8]{0,1:T(8,128)S(1)} %get-tuple-element.92), kind=kLoop, calls=%fused_computation.1 | loop fusion | flops 294912 | bytes 304384 | tf_op jit(solution)/shard_map/convert_element_type | solution.py:418
  34.7 3.7 %convert_element_type.111 = bf16[1152,64]{0,1:T(8,128)(2,1)S(1)} reshape(bf16[144,8,8,8]{1,0,3,2:T(8,128)(2,1)} %get-tuple-element.98) | data formatting | bytes 294912 | tf_op jit(solution)/shard_map/convert_element_type | solution.py:418
  39.3 3.7 %convert_element_type.115 = bf16[1152,64]{0,1:T(8,128)(2,1)S(1)} reshape(bf16[144,8,8,8]{1,0,3,2:T(8,128)(2,1)} %get-tuple-element.99) | data formatting | bytes 294912 | tf_op jit(solution)/shard_map/convert_element_type | solution.py:418
  45.3 2.2 %convert_element_type.119 = bf16[192,192]{1,0:T(8,128)(2,1)S(1)} reshape(bf16[24,8,24,8]{3,2,1,0:T(8,128)(2,1)} %get-tuple-element.96) | data formatting | bytes 147456 | tf_op jit(solution)/shard_map/convert_element_type | solution.py:423
  53.5 3.4 %shard_map.133 = (f32[48,512]{1,0:T(8,128)S(1)}, f32[192,512]{1,0:T(8,128)S(1)}, f32[4,16,256]{2,1,0:T(8,128)S(1)}) custom-call(f32[64,512]{1,0:T(8,128)S(1)} %shard_map.130.weights, f32[48,512]{1,0:T(8,128)S(1)} %get-tuple-element.44.strain, f32[48,512]{1,0:T(8,128)S(1)} %get-tuple-element.45.stress, f32[192,512]{1,0:T(8,128)S(1)} %get-tuple-element.46.resist, ...), custom_call_target="tpu_custom_call" | custom-call | tf_op jit(solution)/shard_map/pallas_call | solution.py:448
  57.0 1.9 %shard_map.134 = (f32[8,8,16,256]{3,2,1,0:T(8,128)S(1)}, f32[8,16,256]{2,1,0:T(8,128)S(1)}, f32[8,16,256]{2,1,0:T(8,128)S(1)}, f32[8,8,256]{2,1,0:T(8,128)S(1)}, f32[8,8,256]{2,1,0:T(8,128)S(1)}) custom-call(f32[8,8,16,256]{3,2,1,0:T(8,128)S(1)} %copy-done.1, f32[8,16,256]{2,1,0:T(8,128)} %collective-permute-done.x_before, ...), custom_call_target="tpu_custom_call" | custom-call | tf_op jit(solution)/shard_map/pallas_call | solution.py:476
  59.0 5.3 %collective-permute-start.5 = (f32[8,16,256]{2,1,0:T(8,128)S(1)}, f32[8,16,256]{2,1,0:T(8,128)S(1)}, u32[]{:S(2)}, u32[]{:S(2)}) collective-permute-start(f32[8,16,256]{2,1,0:T(8,128)S(1)} %get-tuple-element.51), channel_id=1, source_target_pairs={{8,0},{16,8},{24,16},{32,24},{40,32},{48,40},{56,48},{64,56},{72,6... | collective-permute-start | bytes 393224 | tf_op jit(solution)/shard_map/ppermute | solution.py:362
  64.3 3.0 %collective-permute-start.7 = (f32[8,8,256]{2,1,0:T(8,128)S(1)}, f32[8,8,256]{2,1,0:T(8,128)S(1)}, u32[]{:S(2)}, u32[]{:S(2)}) collective-permute-start(f32[8,8,256]{2,1,0:T(8,128)S(1)} %get-tuple-element.53), channel_id=1, source_target_pairs={{1,0},{2,1},{3,2},{4,3},{5,4},{6,5},{7,6},{0,7},{9,8},{10,9},{11,1... | collective-permute-start | bytes 196616 | tf_op jit(solution)/shard_map/ppermute | solution.py:362
  67.3 1.9 %collective-permute-done.6.z_before = f32[8,8,256]{2,1,0:T(8,128)S(1)} collective-permute-done((f32[8,8,256]{2,1,0:T(8,128)S(1)}, f32[8,8,256]{2,1,0:T(8,128)S(1)}, u32[]{:S(2)}, u32[]{:S(2)}) %collective-permute-start.6) | collective-permute-done | bytes 65568 | tf_op jit(solution)/shard_map/ppermute | solution.py:362
  70.8 5.3 %collective-permute-start.9 = (f32[8,16,256]{2,1,0:T(8,128)S(1)}, f32[8,16,256]{2,1,0:T(8,128)S(1)}, u32[]{:S(2)}, u32[]{:S(2)}) collective-permute-start(f32[8,16,256]{2,1,0:T(8,128)S(1)} %get-tuple-element.56), channel_id=1, source_target_pairs={{8,0},{16,8},{24,16},{32,24},{40,32},{48,40},{56,48},{64,56},{72,6... | collective-permute-start | bytes 393224 | tf_op jit(solution)/shard_map/ppermute | solution.py:362
  76.1 3.0 %collective-permute-start.11 = (f32[8,8,256]{2,1,0:T(8,128)S(1)}, f32[8,8,256]{2,1,0:T(8,128)S(1)}, u32[]{:S(2)}, u32[]{:S(2)}) collective-permute-start(f32[8,8,256]{2,1,0:T(8,128)S(1)} %get-tuple-element.58), channel_id=1, source_target_pairs={{1,0},{2,1},{3,2},{4,3},{5,4},{6,5},{7,6},{0,7},{9,8},{10,9},{11,1... | collective-permute-start | bytes 196616 | tf_op jit(solution)/shard_map/ppermute | solution.py:362
  79.6 3.4 %shard_map.137 = (f32[48,512]{1,0:T(8,128)S(1)}, f32[192,512]{1,0:T(8,128)S(1)}, f32[4,16,256]{2,1,0:T(8,128)S(1)}) custom-call(f32[64,512]{1,0:T(8,128)S(1)} %shard_map.136.weights, f32[48,512]{1,0:T(8,128)S(1)} %get-tuple-element.44.strain, f32[48,512]{1,0:T(8,128)S(1)} %get-tuple-element.59.stress, f32[192,512]{1,0:T(8,128)S(1)} %get-tuple-element.60.resist, ...), custom_call_target="tpu_custom_call" | custom-call | tf_op jit(solution)/shard_map/pallas_call | solution.py:448
  86.9 5.3 %collective-permute-start.13 = (f32[8,16,256]{2,1,0:T(8,128)S(1)}, f32[8,16,256]{2,1,0:T(8,128)S(1)}, u32[]{:S(2)}, u32[]{:S(2)}) collective-permute-start(f32[8,16,256]{2,1,0:T(8,128)S(1)} %get-tuple-element.64), channel_id=1, source_target_pairs={{8,0},{16,8},{24,16},{32,24},{40,32},{48,40},{56,48},{64,56},{72,6... | collective-permute-start | bytes 393224 | tf_op jit(solution)/shard_map/ppermute | solution.py:362
  92.2 3.0 %collective-permute-start.15 = (f32[8,8,256]{2,1,0:T(8,128)S(1)}, f32[8,8,256]{2,1,0:T(8,128)S(1)}, u32[]{:S(2)}, u32[]{:S(2)}) collective-permute-start(f32[8,8,256]{2,1,0:T(8,128)S(1)} %get-tuple-element.66), channel_id=1, source_target_pairs={{1,0},{2,1},{3,2},{4,3},{5,4},{6,5},{7,6},{0,7},{9,8},{10,9},{11,1... | collective-permute-start | bytes 196616 | tf_op jit(solution)/shard_map/ppermute | solution.py:362
  95.3 1.8 %collective-permute-done.14.z_before = f32[8,8,256]{2,1,0:T(8,128)S(1)} collective-permute-done((f32[8,8,256]{2,1,0:T(8,128)S(1)}, f32[8,8,256]{2,1,0:T(8,128)S(1)}, u32[]{:S(2)}, u32[]{:S(2)}) %collective-permute-start.14) | collective-permute-done | bytes 65568 | tf_op jit(solution)/shard_map/ppermute | solution.py:362
  102.4 3.4 %shard_map.141 = (f32[48,512]{1,0:T(8,128)S(1)}, f32[192,512]{1,0:T(8,128)S(1)}, f32[4,16,256]{2,1,0:T(8,128)S(1)}) custom-call(f32[64,512]{1,0:T(8,128)S(1)} %shard_map.140.weights, f32[48,512]{1,0:T(8,128)S(1)} %get-tuple-element.44.strain, f32[48,512]{1,0:T(8,128)S(1)} %copy-done.12, f32[192,512]{1,0:T(8,128)S(1)} %copy-done.8, f32[24,512]{1,0:T(8,128)S(1)} %copy-done.5, ...), custom_call_target="tpu_custom_call" | custom-call | tf_op jit(solution)/shard_map/pallas_call | solution.py:448
  105.8 1.7 %shard_map.144 = f32[1024,256]{1,0:T(8,128)} custom-call(s32[1,512]{1,0:T(1,128)S(1)} %add.615.mailbox, f32[48,512]{1,0:T(8,128)S(1)} %get-tuple-element.81.stress, f32[192,512]{1,0:T(8,128)S(1)} %get-tuple-element.82.resist), custom_call_target="tpu_custom_call" | custom-call | tf_op jit(solution)/shard_map/pallas_call | solution.py:487
  107.6 5.3 %all-to-all-start.1 = ((f32[128,8,256]{2,1,0:T(8,128)}), f32[128,8,256]{2,1,0:T(8,128)S(1)}, u32[]{:S(2)}, u32[]{:S(2)}) async-start(f32[128,8,256]{2,1,0:T(8,128)} %bitcast.16), calls=%async_computation.1 | async-start | bytes 2097152 | tf_op jit(solution)/shard_map/all_to_all | solution.py:132
  114.0 4.3 %collective-permute-start.17 = (f32[8,16,256]{2,1,0:T(8,128)S(1)}, f32[8,16,256]{2,1,0:T(8,128)S(1)}, u32[]{:S(2)}, u32[]{:S(2)}) collective-permute-start(f32[8,16,256]{2,1,0:T(8,128)S(1)} %copy-done.19), channel_id=1, source_target_pairs={{8,0},{16,8},{24,16},{32,24},{40,32},{48,40},{56,48},{64,56},{72,6... | collective-permute-start | bytes 393224 | tf_op jit(solution)/shard_map/ppermute | solution.py:362
  118.3 3.0 %collective-permute-start.19 = (f32[8,8,256]{2,1,0:T(8,128)}, f32[8,8,256]{2,1,0:T(8,128)S(1)}, u32[]{:S(2)}, u32[]{:S(2)}) collective-permute-start(f32[8,8,256]{2,1,0:T(8,128)} %copy-done.21), channel_id=1, source_target_pairs={{1,0},{2,1},{3,2},{4,3},{5,4},{6,5},{7,6},{0,7},{9,8},{10,9},{11,1... | collective-permute-start | bytes 196616 | tf_op jit(solution)/shard_map/ppermute | solution.py:362
  121.3 4.7 %collective-permute-done.18.z_before = f32[8,8,256]{2,1,0:T(8,128)S(1)} collective-permute-done((f32[8,8,256]{2,1,0:T(8,128)S(1)}, f32[8,8,256]{2,1,0:T(8,128)S(1)}, u32[]{:S(2)}, u32[]{:S(2)}) %collective-permute-start.18) | collective-permute-done | bytes 65568 | tf_op jit(solution)/shard_map/ppermute | solution.py:362
  126.0 7.3 %collective-permute-done.16.x_before = f32[8,16,256]{2,1,0:T(8,128)S(1)} collective-permute-done((f32[8,16,256]{2,1,0:T(8,128)}, f32[8,16,256]{2,1,0:T(8,128)S(1)}, u32[]{:S(2)}, u32[]{:S(2)}) %collective-permute-start.16) | collective-permute-done | bytes 131104 | tf_op jit(solution)/shard_map/ppermute | solution.py:362
  134.9 5.3 %collective-permute-start.21 = (f32[8,16,256]{2,1,0:T(8,128)S(1)}, f32[8,16,256]{2,1,0:T(8,128)S(1)}, u32[]{:S(2)}, u32[]{:S(2)}) collective-permute-start(f32[8,16,256]{2,1,0:T(8,128)S(1)} %get-tuple-element.77), channel_id=1, source_target_pairs={{8,0},{16,8},{24,16},{32,24},{40,32},{48,40},{56,48},{64,56},{72,6... | collective-permute-start | bytes 393224 | tf_op jit(solution)/shard_map/ppermute | solution.py:362
  140.2 3.0 %collective-permute-start.23 = (f32[8,8,256]{2,1,0:T(8,128)S(1)}, f32[8,8,256]{2,1,0:T(8,128)S(1)}, u32[]{:S(2)}, u32[]{:S(2)}) collective-permute-start(f32[8,8,256]{2,1,0:T(8,128)S(1)} %get-tuple-element.79), channel_id=1, source_target_pairs={{1,0},{2,1},{3,2},{4,3},{5,4},{6,5},{7,6},{0,7},{9,8},{10,9},{11,1... | collective-permute-start | bytes 196616 | tf_op jit(solution)/shard_map/ppermute | solution.py:362
  143.2 1.9 %collective-permute-done.22.z_before = f32[8,8,256]{2,1,0:T(8,128)S(1)} collective-permute-done((f32[8,8,256]{2,1,0:T(8,128)S(1)}, f32[8,8,256]{2,1,0:T(8,128)S(1)}, u32[]{:S(2)}, u32[]{:S(2)}) %collective-permute-start.22) | collective-permute-done | bytes 65568 | tf_op jit(solution)/shard_map/ppermute | solution.py:362
  145.1 2.5 %shard_map.143 = (f32[8,8,16,256]{3,2,1,0:T(8,128)}, f32[8,16,256]{2,1,0:T(8,128)}, f32[8,16,256]{2,1,0:T(8,128)}, f32[8,8,256]{2,1,0:T(8,128)}, f32[8,8,256]{2,1,0:T(8,128)}) custom-call(f32[8,8,16,256]{3,2,1,0:T(8,128)S(1)} %get-tuple-element.75.grains, f32[8,16,256]{2,1,0:T(8,128)S(1)} %collective-permute-done.20.x_before, ...), custom_call_target="tpu_custom_call" | custom-call | tf_op jit(solution)/shard_map/pallas_call | solution.py:476
  147.7 1.5 %shard_map.145 = (f32[48,512]{1,0:T(8,128)}, f32[192,512]{1,0:T(8,128)}) custom-call(s32[512,128]{1,0:T(8,128)S(1)} %broadcast_in_dim.76.anchor, f32[1024,256]{1,0:T(8,128)S(1)} %bitcast.60), custom_call_target="tpu_custom_call" | custom-call | tf_op jit(solution)/shard_map/pallas_call | solution.py:491
  (152 shorter events, 31.6 us)
Async XLA Ops:
  7.3 23.9 %copy-start.24 = (s32[2,4,64]{2,1,0:T(4,128)S(1)}, s32[2,4,64]{2,1,0:T(4,128)}, u32[]{:S(2)}) copy-start(s32[2,4,64]{2,1,0:T(4,128)} %param.12) | copy-start | bytes 6148
  7.3 24.1 %copy-start.26 = (f32[8,24,6]{1,0,2:T(8,128)S(1)}, f32[8,24,6]{1,0,2:T(8,128)}, u32[]{:S(2)}) copy-start(f32[8,24,6]{1,0,2:T(8,128)} %param.18) | copy-start | bytes 13828
  7.3 44.6 %all-to-all-start = ((f32[128,8,384]{2,1,0:T(8,128)}), f32[128,8,384]{2,1,0:T(8,128)S(1)}, u32[]{:S(2)}, u32[]{:S(2)}) async-start(f32[128,8,384]{2,1,0:T(8,128)} %bitcast.11), calls=%async_computation | async-start | bytes 3145728 | tf_op jit(solution)/shard_map/all_to_all | solution.py:132
  20.2 36.7 %collective-permute-start = (f32[8,16,256]{2,1,0:T(8,128)}, f32[8,16,256]{2,1,0:T(8,128)}, u32[]{:S(2)}, u32[]{:S(2)}) collective-permute-start(f32[8,16,256]{2,1,0:T(8,128)} %get-tuple-element.88), channel_id=1, source_target_pairs={{0,8},{8,16},{16,24},{24,32},{32,40},{40,48},{48,56},{56,64},{64,7... | collective-permute-start | bytes 393224 | tf_op jit(solution)/shard_map/ppermute | solution.py:362
  21.3 35.7 %collective-permute-start.1 = (f32[8,16,256]{2,1,0:T(8,128)}, f32[8,16,256]{2,1,0:T(8,128)}, u32[]{:S(2)}, u32[]{:S(2)}) collective-permute-start(f32[8,16,256]{2,1,0:T(8,128)} %get-tuple-element.87), channel_id=1, source_target_pairs={{8,0},{16,8},{24,16},{32,24},{40,32},{48,40},{56,48},{64,56},{72,6... | collective-permute-start | bytes 393224 | tf_op jit(solution)/shard_map/ppermute | solution.py:362
  27.5 29.4 %collective-permute-start.2 = (f32[8,8,256]{2,1,0:T(8,128)}, f32[8,8,256]{2,1,0:T(8,128)}, u32[]{:S(2)}, u32[]{:S(2)}) collective-permute-start(f32[8,8,256]{2,1,0:T(8,128)} %bitcast.55), channel_id=1, source_target_pairs={{0,1},{1,2},{2,3},{3,4},{4,5},{5,6},{6,7},{7,0},{8,9},{9,10},{10,1... | collective-permute-start | bytes 196616 | tf_op jit(solution)/shard_map/ppermute | solution.py:362
  28.1 28.8 %collective-permute-start.3 = (f32[8,8,256]{2,1,0:T(8,128)}, f32[8,8,256]{2,1,0:T(8,128)}, u32[]{:S(2)}, u32[]{:S(2)}) collective-permute-start(f32[8,8,256]{2,1,0:T(8,128)} %bitcast.54), channel_id=1, source_target_pairs={{1,0},{2,1},{3,2},{4,3},{5,4},{6,5},{7,6},{0,7},{9,8},{10,9},{11,1... | collective-permute-start | bytes 196616 | tf_op jit(solution)/shard_map/ppermute | solution.py:362
  53.4 26.1 %copy-start.4 = (f32[24,512]{1,0:T(8,128)}, f32[24,512]{1,0:T(8,128)S(1)}, u32[]{:S(2)}) copy-start(f32[24,512]{1,0:T(8,128)S(1)} %get-tuple-element.47.active) | copy-start | bytes 147460
  58.9 10.3 %collective-permute-start.4 = (f32[8,16,256]{2,1,0:T(8,128)S(1)}, f32[8,16,256]{2,1,0:T(8,128)S(1)}, u32[]{:S(2)}, u32[]{:S(2)}) collective-permute-start(f32[8,16,256]{2,1,0:T(8,128)S(1)} %get-tuple-element.50), channel_id=1, source_target_pairs={{0,8},{8,16},{16,24},{24,32},{32,40},{40,48},{48,56},{56,64},{64,7... | collective-permute-start | bytes 393224 | tf_op jit(solution)/shard_map/ppermute | solution.py:362
  59.0 10.2 %collective-permute-start.5 = (f32[8,16,256]{2,1,0:T(8,128)S(1)}, f32[8,16,256]{2,1,0:T(8,128)S(1)}, u32[]{:S(2)}, u32[]{:S(2)}) collective-permute-start(f32[8,16,256]{2,1,0:T(8,128)S(1)} %get-tuple-element.51), channel_id=1, source_target_pairs={{8,0},{16,8},{24,16},{32,24},{40,32},{48,40},{56,48},{64,56},{72,6... | collective-permute-start | bytes 393224 | tf_op jit(solution)/shard_map/ppermute | solution.py:362
  64.3 4.9 %collective-permute-start.6 = (f32[8,8,256]{2,1,0:T(8,128)S(1)}, f32[8,8,256]{2,1,0:T(8,128)S(1)}, u32[]{:S(2)}, u32[]{:S(2)}) collective-permute-start(f32[8,8,256]{2,1,0:T(8,128)S(1)} %get-tuple-element.52), channel_id=1, source_target_pairs={{0,1},{1,2},{2,3},{3,4},{4,5},{5,6},{6,7},{7,0},{8,9},{9,10},{10,1... | collective-permute-start | bytes 196616 | tf_op jit(solution)/shard_map/ppermute | solution.py:362
  64.3 4.9 %collective-permute-start.7 = (f32[8,8,256]{2,1,0:T(8,128)S(1)}, f32[8,8,256]{2,1,0:T(8,128)S(1)}, u32[]{:S(2)}, u32[]{:S(2)}) collective-permute-start(f32[8,8,256]{2,1,0:T(8,128)S(1)} %get-tuple-element.53), channel_id=1, source_target_pairs={{1,0},{2,1},{3,2},{4,3},{5,4},{6,5},{7,6},{0,7},{9,8},{10,9},{11,1... | collective-permute-start | bytes 196616 | tf_op jit(solution)/shard_map/ppermute | solution.py:362
  70.7 13.7 %collective-permute-start.8 = (f32[8,16,256]{2,1,0:T(8,128)S(1)}, f32[8,16,256]{2,1,0:T(8,128)S(1)}, u32[]{:S(2)}, u32[]{:S(2)}) collective-permute-start(f32[8,16,256]{2,1,0:T(8,128)S(1)} %get-tuple-element.55), channel_id=1, source_target_pairs={{0,8},{8,16},{16,24},{24,32},{32,40},{40,48},{48,56},{56,64},{64,7... | collective-permute-start | bytes 393224 | tf_op jit(solution)/shard_map/ppermute | solution.py:362
  70.8 13.6 %collective-permute-start.9 = (f32[8,16,256]{2,1,0:T(8,128)S(1)}, f32[8,16,256]{2,1,0:T(8,128)S(1)}, u32[]{:S(2)}, u32[]{:S(2)}) collective-permute-start(f32[8,16,256]{2,1,0:T(8,128)S(1)} %get-tuple-element.56), channel_id=1, source_target_pairs={{8,0},{16,8},{24,16},{32,24},{40,32},{48,40},{56,48},{64,56},{72,6... | collective-permute-start | bytes 393224 | tf_op jit(solution)/shard_map/ppermute | solution.py:362
  76.1 8.3 %collective-permute-start.10 = (f32[8,8,256]{2,1,0:T(8,128)S(1)}, f32[8,8,256]{2,1,0:T(8,128)S(1)}, u32[]{:S(2)}, u32[]{:S(2)}) collective-permute-start(f32[8,8,256]{2,1,0:T(8,128)S(1)} %get-tuple-element.57), channel_id=1, source_target_pairs={{0,1},{1,2},{2,3},{3,4},{4,5},{5,6},{6,7},{7,0},{8,9},{9,10},{10,1... | collective-permute-start | bytes 196616 | tf_op jit(solution)/shard_map/ppermute | solution.py:362
  76.1 8.3 %collective-permute-start.11 = (f32[8,8,256]{2,1,0:T(8,128)S(1)}, f32[8,8,256]{2,1,0:T(8,128)S(1)}, u32[]{:S(2)}, u32[]{:S(2)}) collective-permute-start(f32[8,8,256]{2,1,0:T(8,128)S(1)} %get-tuple-element.58), channel_id=1, source_target_pairs={{1,0},{2,1},{3,2},{4,3},{5,4},{6,5},{7,6},{0,7},{9,8},{10,9},{11,1... | collective-permute-start | bytes 196616 | tf_op jit(solution)/shard_map/ppermute | solution.py:362
  79.1 16.1 %copy-start.25 = (s32[2,4,64]{2,1,0:T(4,128)S(1)}, s32[2,4,64]{2,1,0:T(4,128)}, u32[]{:S(2)}) copy-start(s32[2,4,64]{2,1,0:T(4,128)} %param.12) | copy-start | bytes 6148
  79.1 16.2 %copy-start.28 = (s32[512]{0:T(512)S(1)}, s32[512]{0:T(512)}, u32[]{:S(2)}) copy-start(s32[512]{0:T(512)} %copy-done.27) | copy-start | bytes 6148
  86.9 10.3 %collective-permute-start.12 = (f32[8,16,256]{2,1,0:T(8,128)S(1)}, f32[8,16,256]{2,1,0:T(8,128)S(1)}, u32[]{:S(2)}, u32[]{:S(2)}) collective-permute-start(f32[8,16,256]{2,1,0:T(8,128)S(1)} %get-tuple-element.63), channel_id=1, source_target_pairs={{0,8},{8,16},{16,24},{24,32},{32,40},{40,48},{48,56},{56,64},{64,7... | collective-permute-start | bytes 393224 | tf_op jit(solution)/shard_map/ppermute | solution.py:362
  86.9 10.3 %collective-permute-start.13 = (f32[8,16,256]{2,1,0:T(8,128)S(1)}, f32[8,16,256]{2,1,0:T(8,128)S(1)}, u32[]{:S(2)}, u32[]{:S(2)}) collective-permute-start(f32[8,16,256]{2,1,0:T(8,128)S(1)} %get-tuple-element.64), channel_id=1, source_target_pairs={{8,0},{16,8},{24,16},{32,24},{40,32},{48,40},{56,48},{64,56},{72,6... | collective-permute-start | bytes 393224 | tf_op jit(solution)/shard_map/ppermute | solution.py:362
  92.2 4.9 %collective-permute-start.14 = (f32[8,8,256]{2,1,0:T(8,128)S(1)}, f32[8,8,256]{2,1,0:T(8,128)S(1)}, u32[]{:S(2)}, u32[]{:S(2)}) collective-permute-start(f32[8,8,256]{2,1,0:T(8,128)S(1)} %get-tuple-element.65), channel_id=1, source_target_pairs={{0,1},{1,2},{2,3},{3,4},{4,5},{5,6},{6,7},{7,0},{8,9},{9,10},{10,1... | collective-permute-start | bytes 196616 | tf_op jit(solution)/shard_map/ppermute | solution.py:362
  92.2 4.9 %collective-permute-start.15 = (f32[8,8,256]{2,1,0:T(8,128)S(1)}, f32[8,8,256]{2,1,0:T(8,128)S(1)}, u32[]{:S(2)}, u32[]{:S(2)}) collective-permute-start(f32[8,8,256]{2,1,0:T(8,128)S(1)} %get-tuple-element.66), channel_id=1, source_target_pairs={{1,0},{2,1},{3,2},{4,3},{5,4},{6,5},{7,6},{0,7},{9,8},{10,9},{11,1... | collective-permute-start | bytes 196616 | tf_op jit(solution)/shard_map/ppermute | solution.py:362
  107.6 40.0 %copy-start.17 = (s32[512]{0:T(512)S(1)}, s32[512]{0:T(512)}, u32[]{:S(2)}) copy-start(s32[512]{0:T(512)} %param.13) | copy-start | bytes 6148
  107.6 40.0 %all-to-all-start.1 = ((f32[128,8,256]{2,1,0:T(8,128)}), f32[128,8,256]{2,1,0:T(8,128)S(1)}, u32[]{:S(2)}, u32[]{:S(2)}) async-start(f32[128,8,256]{2,1,0:T(8,128)} %bitcast.16), calls=%async_computation.1 | async-start | bytes 2097152 | tf_op jit(solution)/shard_map/all_to_all | solution.py:132
  112.9 20.4 %collective-permute-start.16 = (f32[8,16,256]{2,1,0:T(8,128)}, f32[8,16,256]{2,1,0:T(8,128)S(1)}, u32[]{:S(2)}, u32[]{:S(2)}) collective-permute-start(f32[8,16,256]{2,1,0:T(8,128)} %copy-done.20), channel_id=1, source_target_pairs={{0,8},{8,16},{16,24},{24,32},{32,40},{40,48},{48,56},{56,64},{64,7... | collective-permute-start | bytes 393224 | tf_op jit(solution)/shard_map/ppermute | solution.py:362
  114.0 19.3 %collective-permute-start.17 = (f32[8,16,256]{2,1,0:T(8,128)S(1)}, f32[8,16,256]{2,1,0:T(8,128)S(1)}, u32[]{:S(2)}, u32[]{:S(2)}) collective-permute-start(f32[8,16,256]{2,1,0:T(8,128)S(1)} %copy-done.19), channel_id=1, source_target_pairs={{8,0},{16,8},{24,16},{32,24},{40,32},{48,40},{56,48},{64,56},{72,6... | collective-permute-start | bytes 393224 | tf_op jit(solution)/shard_map/ppermute | solution.py:362
  118.3 7.7 %collective-permute-start.18 = (f32[8,8,256]{2,1,0:T(8,128)S(1)}, f32[8,8,256]{2,1,0:T(8,128)S(1)}, u32[]{:S(2)}, u32[]{:S(2)}) collective-permute-start(f32[8,8,256]{2,1,0:T(8,128)S(1)} %copy-done.23), channel_id=1, source_target_pairs={{0,1},{1,2},{2,3},{3,4},{4,5},{5,6},{6,7},{7,0},{8,9},{9,10},{10,1... | collective-permute-start | bytes 196616 | tf_op jit(solution)/shard_map/ppermute | solution.py:362
  118.3 7.7 %collective-permute-start.19 = (f32[8,8,256]{2,1,0:T(8,128)}, f32[8,8,256]{2,1,0:T(8,128)S(1)}, u32[]{:S(2)}, u32[]{:S(2)}) collective-permute-start(f32[8,8,256]{2,1,0:T(8,128)} %copy-done.21), channel_id=1, source_target_pairs={{1,0},{2,1},{3,2},{4,3},{5,4},{6,5},{7,6},{0,7},{9,8},{10,9},{11,1... | collective-permute-start | bytes 196616 | tf_op jit(solution)/shard_map/ppermute | solution.py:362
  134.8 10.3 %collective-permute-start.20 = (f32[8,16,256]{2,1,0:T(8,128)S(1)}, f32[8,16,256]{2,1,0:T(8,128)S(1)}, u32[]{:S(2)}, u32[]{:S(2)}) collective-permute-start(f32[8,16,256]{2,1,0:T(8,128)S(1)} %get-tuple-element.76), channel_id=1, source_target_pairs={{0,8},{8,16},{16,24},{24,32},{32,40},{40,48},{48,56},{56,64},{64,7... | collective-permute-start | bytes 393224 | tf_op jit(solution)/shard_map/ppermute | solution.py:362
  134.9 10.2 %collective-permute-start.21 = (f32[8,16,256]{2,1,0:T(8,128)S(1)}, f32[8,16,256]{2,1,0:T(8,128)S(1)}, u32[]{:S(2)}, u32[]{:S(2)}) collective-permute-start(f32[8,16,256]{2,1,0:T(8,128)S(1)} %get-tuple-element.77), channel_id=1, source_target_pairs={{8,0},{16,8},{24,16},{32,24},{40,32},{48,40},{56,48},{64,56},{72,6... | collective-permute-start | bytes 393224 | tf_op jit(solution)/shard_map/ppermute | solution.py:362
  140.2 4.9 %collective-permute-start.22 = (f32[8,8,256]{2,1,0:T(8,128)S(1)}, f32[8,8,256]{2,1,0:T(8,128)S(1)}, u32[]{:S(2)}, u32[]{:S(2)}) collective-permute-start(f32[8,8,256]{2,1,0:T(8,128)S(1)} %get-tuple-element.78), channel_id=1, source_target_pairs={{0,1},{1,2},{2,3},{3,4},{4,5},{5,6},{6,7},{7,0},{8,9},{9,10},{10,1... | collective-permute-start | bytes 196616 | tf_op jit(solution)/shard_map/ppermute | solution.py:362
  140.2 4.9 %collective-permute-start.23 = (f32[8,8,256]{2,1,0:T(8,128)S(1)}, f32[8,8,256]{2,1,0:T(8,128)S(1)}, u32[]{:S(2)}, u32[]{:S(2)}) collective-permute-start(f32[8,8,256]{2,1,0:T(8,128)S(1)} %get-tuple-element.79), channel_id=1, source_target_pairs={{1,0},{2,1},{3,2},{4,3},{5,4},{6,5},{7,6},{0,7},{9,8},{10,9},{11,1... | collective-permute-start | bytes 196616 | tf_op jit(solution)/shard_map/ppermute | solution.py:362
  (24 other events, 91.2 us)

commit v2 on v1

v2 whole, which is shorter than its diff:
```python
import functools

import jax
import jax.numpy as jnp
from jax import lax
from jax.experimental import pallas as pl
from jax.experimental.pallas import tpu as pltpu
from jax.sharding import PartitionSpec as P

ITERS = 4
STEPS = 3
SUB = 2

CROSS_TERM = 1.5
DRIVE_SCALE = 6.0
TIME_STEP = 0.02
SLIP_RATE = 0.1
HARDENING = 0.5
LANES = 128
BF16 = jnp.bfloat16
F32 = jnp.float32


def two_terms(value):
    high = value.astype(BF16)
    low = (value - high.astype(F32)).astype(BF16)
    return high, low


def product(left, right):
    return lax.dot_general(
        left, right, (((1,), (0,)), ((), ())), preferred_element_type=F32
    )


def product_rows(left, right):
    return lax.dot_general(
        left, right, (((1,), (1,)), ((), ())), preferred_element_type=F32
    )


def call(kernel, shapes, limit, scratch=(), **options):
    return pl.pallas_call(
        kernel,
        out_shape=shapes,
        scratch_shapes=list(scratch),
        compiler_params=pltpu.CompilerParams(vmem_limit_bytes=limit and limit << 20),
        **options,
    )


def shape(*dims):
    return jax.ShapeDtypeStruct(dims, F32)


def hit_rows(slots_row, slot):
    return (slot == slots_row).astype(F32).astype(BF16)


def into_slots(hit, values):
    high, low = two_terms(values)
    return product_rows(hit, high) + product_rows(hit, low)


def hit_columns(slots_col, count):
    lane = lax.broadcasted_iota(jnp.int32, (slots_col.shape[0], LANES), 1)
    return jnp.concatenate(
        [
            (lane + start == slots_col).astype(F32).astype(BF16)
            for start in range(0, count, LANES)
        ],
        axis=1,
    )


def out_of_slots(hit, mail):
    high, low = two_terms(mail)
    return product(hit, high) + product(hit, low)


def pack_state_kernel(
    anchor, strain, stress, resist, active, out, values, flags, wide_mail, rest_mail, sems
):
    tensors, forces = strain.shape[0], resist.shape[0]
    copies = [
        pltpu.make_async_copy(resist, values.at[2 * tensors : 2 * tensors + forces], sems.at[0]),
        pltpu.make_async_copy(strain, values.at[:tensors], sems.at[1]),
        pltpu.make_async_copy(stress, values.at[tensors : 2 * tensors], sems.at[2]),
        pltpu.make_async_copy(active, flags, sems.at[3]),
    ]
    for copy in copies:
        copy.start()
    items = values.shape[1]
    slots_all = wide_mail.shape[0]
    slots_row = anchor[...]
    slot = lax.broadcasted_iota(jnp.int32, (slots_all, items), 0)
    hit = hit_rows(slots_row, slot)
    row = lax.broadcasted_iota(jnp.int32, (slots_all // 2, items), 0)
    lower = (row >> 2) * 8 + (row & 3)
    sides = jnp.concatenate([hit_rows(slots_row, lower), hit_rows(slots_row, lower + 4)], axis=1)
    for copy in copies:
        copy.wait()
    wide_mail[...] = into_slots(hit, values[: 2 * LANES])
    total = 2 * tensors + forces
    rest = jnp.concatenate(
        [values[2 * LANES : total], flags[...].astype(F32), jnp.zeros((8, items), F32)], axis=0
    )
    empty = jnp.zeros_like(rest)
    both = jnp.concatenate(
        [jnp.concatenate([rest, empty], axis=1), jnp.concatenate([empty, rest], axis=1)], axis=0
    )
    rest_mail[...] = into_slots(sides, both)
    upper = lax.broadcasted_iota(jnp.int32, (8, LANES), 0) < 4
    for pair in range(slots_all // 16):
        start = 16 * pair
        left = pltpu.roll(wide_mail[start + 8 : start + 16, :LANES], 4, 0)
        right = pltpu.roll(wide_mail[start + 8 : start + 16, LANES:], 4, 0)
        side = rest_mail[8 * pair : 8 * pair + 8]
        out[40 * pair : 40 * pair + 8] = wide_mail[start : start + 8, :LANES]
        out[40 * pair + 8 : 40 * pair + 16] = wide_mail[start : start + 8, LANES:]
        out[40 * pair + 16 : 40 * pair + 24] = jnp.where(upper, side, left)
        out[40 * pair + 24 : 40 * pair + 32] = jnp.where(upper, left, right)
        out[40 * pair + 32 : 40 * pair + 40] = jnp.where(upper, right, side)


def unpack_state_kernel(
    mailbox, mail, strain, stress, resist, active, wide_mail, rest_mail
):
    slots_all = wide_mail.shape[0]
    upper = lax.broadcasted_iota(jnp.int32, (8, LANES), 0) < 4
    for pair in range(slots_all // 16):
        start = 16 * pair
        third, fourth, fifth = (
            mail[40 * pair + 8 * k : 40 * pair + 8 * k + 8] for k in (2, 3, 4)
        )
        wide_mail[start : start + 8, :LANES] = mail[40 * pair : 40 * pair + 8]
        wide_mail[start : start + 8, LANES:] = mail[40 * pair + 8 : 40 * pair + 16]
        wide_mail[start + 8 : start + 16, :LANES] = pltpu.roll(
            jnp.where(upper, fourth, third), 4, 0
        )
        wide_mail[start + 8 : start + 16, LANES:] = pltpu.roll(
            jnp.where(upper, fifth, fourth), 4, 0
        )
        rest_mail[8 * pair : 8 * pair + 8] = jnp.where(upper, third, fifth)
    slots = mailbox[...]
    wide = out_of_slots(hit_columns(slots, slots_all), wide_mail[...])
    row = (slots >> 3) * 4 + (slots & 3)
    rest = out_of_slots(hit_columns(row, slots_all // 2), rest_mail[...])
    rest = jnp.where((slots & 4) > 0, pltpu.roll(rest, LANES // 2, 1), rest)
    values = jnp.transpose(jnp.concatenate([wide, rest], axis=1))
    start = 0
    for part in (strain, stress, resist, active):
        part[...] = values[start : start + part.shape[0]]
        start += part.shape[0]


def pack_result_kernel(mailbox, stress, resist, out):
    rows = stress.shape[0] + resist.shape[0]
    values = jnp.concatenate(
        [
            stress[...],
            resist[...],
            jnp.zeros((out.shape[1] - rows, stress.shape[1]), F32),
        ],
        axis=0,
    )
    slot = lax.broadcasted_iota(jnp.int32, (out.shape[0], values.shape[1]), 0)
    out[...] = into_slots(hit_rows(mailbox[...], slot), values)


def unpack_result_kernel(anchor, mail, stress, resist):
    values = jnp.transpose(out_of_slots(hit_columns(anchor[...], mail.shape[0]), mail[...]))
    stress[...] = values[: stress.shape[0]]
    resist[...] = values[stress.shape[0] : stress.shape[0] + resist.shape[0]]


def exchanged(sent):
    return lax.all_to_all(sent, ("gx", "gz"), split_axis=0, concat_axis=0, tiled=True)


def grid_of(rows, columns):
    dims = (rows, columns)
    return lax.broadcasted_iota(jnp.int32, dims, 0), lax.broadcasted_iota(jnp.int32, dims, 1)


def marked(condition, value=1.0):
    return jnp.where(condition, value, 0.0).astype(BF16)


def field(index, low, width):
    return (index >> low) & ((1 << width) - 1)


def row_map():
    to, index = grid_of(128, 256)
    same = (
        (field(to, 6, 1) == field(index, 2, 1))
        & (field(to, 5, 1) == field(index, 6, 1))
        & (field(to, 4, 1) == field(index, 5, 1))
        & (field(to, 3, 1) == field(index, 3, 1))
        & (field(to, 2, 1) == field(index, 4, 1))
        & (field(to, 1, 1) == field(index, 1, 1))
    )
    return marked(same, 0.125)


def lane_map():
    index, to = grid_of(1024, 256)
    y = field(index, 0, 8)
    return marked(
        ((y >> 2) == field(to, 0, 6))
        & (field(y, 1, 1) == field(to, 7, 1))
        & (field(index, 8, 1) == field(to, 6, 1))
    )


def spread_map():
    index, y = grid_of(512, 256)
    return marked(((y >> 2) == field(index, 0, 6)) & (field(y, 1, 1) == field(index, 7, 1)))


def repeat_map():
    to, index = grid_of(32, 16)
    return marked(
        (field(to, 4, 1) == field(index, 0, 1))
        & (field(to, 3, 1) == field(index, 2, 1))
        & (field(to, 1, 1) == field(index, 1, 1))
    )


def over_points(matrix):
    rows, columns = matrix.shape
    wide = columns * 8
    high, low = two_terms(matrix)
    index, to = grid_of(columns, 3 * wide)
    source = (to >> 3) - jnp.where(to >= wide, columns, 0) - jnp.where(to >= 2 * wide, columns, 0)
    same = index == source
    spread = product(high, marked(same & (to < 2 * wide))) + product(
        low, marked(same & (to >= 2 * wide))
    )
    to, index = grid_of(rows * 8, rows)
    tall = product(marked((to >> 3) == index), spread.astype(BF16))
    row, column = grid_of(rows * 8, 3 * wide)
    return jnp.where((row & 7) == (column & 7), tall, 0.0).astype(BF16)


def column_of(row):
    tall = jnp.broadcast_to(row.astype(F32), (LANES, row.shape[1]))
    return jnp.transpose(tall).astype(jnp.int32)


def prepare_kernel(
    owner,
    anchor,
    schmid,
    latent,
    mailbox_row,
    mailbox_col,
    anchor_col,
    tensor_map,
    harden_map,
    active_map,
    rows,
    lanes,
    repeat,
    spread,
):
    owners = jnp.concatenate(
        [owner[i, j : j + 1] for i in range(owner.shape[0]) for j in range(owner.shape[1])],
        axis=1,
    )
    items = owners.shape[1]
    device = lax.broadcasted_iota(jnp.int32, (128, items), 0)
    onehot = (device == owners).astype(F32)
    index, to = grid_of(items, items)
    before = product(onehot.astype(BF16), marked(index < to))
    rank = jnp.sum(before * onehot, axis=0, keepdims=True).astype(jnp.int32)
    mailbox = owners * 8 + rank
    mailbox_row[...] = mailbox
    mailbox_col[...] = column_of(mailbox)
    anchor_col[...] = column_of(anchor[...])
    tensor_map[...] = over_points(schmid[...])
    harden_map[...] = over_points(latent[...])
    to, index = grid_of(active_map.shape[0], active_map.shape[1])
    active_map[...] = marked((to >> 3) == index)
    rows[...] = row_map()
    lanes[...] = lane_map()
    repeat[...] = repeat_map()
    spread[...] = spread_map()


def restrict_kernel(grains, rows, lanes, weights):
    orders, size_x, size_z, size_y = grains.shape
    lefts = []
    for pair in range(orders // 2):
        parts = []
        for order in (2 * pair, 2 * pair + 1):
            for coarse in range(size_x // 2):
                low = grains[order, 2 * coarse]
                high = grains[order, 2 * coarse + 1]
                parts.append(low * low + high * high)
        summed = jnp.concatenate(parts, axis=0)
        moved = product(rows[...], jnp.concatenate(two_terms(summed), axis=0))
        high, low = two_terms(moved)
        lefts.append(
            jnp.concatenate([high[:64], high[64:], low[:64], low[64:]], axis=1)
        )
    found = product(jnp.concatenate(lefts, axis=0), lanes[...])
    row = lax.broadcasted_iota(jnp.int32, (found.shape[0], LANES), 0)
    picked = jnp.where(row % 2 == 0, found[:, :LANES], found[:, LANES:])
    for order in range(orders):
        for tile in range(4):
            start = (order * 4 + tile) * 8
            weights[order * 8 : order * 8 + 8, tile * LANES : (tile + 1) * LANES] = picked[
                start : start + 8
            ]


def prolonged(stored, repeat, spread, energy):
    high, low = two_terms(stored)
    rows = product(repeat, jnp.concatenate([high, low], axis=0))
    row = lax.broadcasted_iota(jnp.int32, rows.shape, 0)
    lane = lax.broadcasted_iota(jnp.int32, rows.shape, 1)
    rows = jnp.where((row // 4) % 2 == (lane // 64) % 2, rows, 0.0)
    tiles = [
        jnp.concatenate(
            [rows[:16, t * LANES : (t + 1) * LANES], rows[16:, t * LANES : (t + 1) * LANES]],
            axis=1,
        )
        for t in range(4)
    ]
    left = jnp.concatenate(two_terms(jnp.concatenate(tiles, axis=0)), axis=1)
    cells = product(left, spread)
    for bx in range(2):
        for pair in range(2):
            for qx in range(2):
                start = ((bx * 2 + pair) * 2 + qx) * 8
                energy[bx * 2 + qx, pair * 8 : pair * 8 + 8] = cells[start : start + 8]


def mechanics_kernel(
    weights,
    strain,
    stress,
    resist,
    active,
    tensor_map,
    harden_map,
    active_map,
    repeat,
    spread,
    stress_out,
    resist_out,
    energy,
    tensor,
    rates,
    amounts,
):
    systems = active.shape[0]
    points = resist.shape[0] // systems
    items = weights.shape[1]
    high, low = two_terms(weights[...])
    tensor[...] = product(tensor_map[...], jnp.concatenate([high, low, high], axis=0))
    rates[...] = product(active_map[...], active[...].astype(BF16)) * SLIP_RATE

    def tile_step(tile, carry):
        lanes = pl.ds(pl.multiple_of(tile * LANES, LANES), LANES)
        trial = [
            stress[points * c : points * (c + 1), lanes]
            + 2.0 * strain[points * c : points * (c + 1), lanes]
            for c in range(6)
        ]

        def sweep(_, now):
            sums = [jnp.zeros((points, LANES), F32) for _ in range(6)]
            for a in range(systems):
                rows = pl.ds(a * points, points)
                parts = [tensor[pl.ds((a * 6 + c) * points, points), lanes] for c in range(6)]
                resolved = (
                    (parts[0] * now[0] + parts[1] * now[1])
                    + (parts[2] * now[2] + parts[3] * now[3])
                    + (parts[4] * now[4] + parts[5] * now[5])
                )
                slip = rates[rows, lanes] * resolved / (resist[rows, lanes] + jnp.abs(resolved))
                amounts[rows, lanes] = jnp.abs(slip)
                sums = [sums[c] + parts[c] * slip for c in range(6)]
            return tuple(trial[c] - 2.0 * sums[c] for c in range(6))

        now = lax.fori_loop(0, ITERS, sweep, tuple(trial))
        for c in range(6):
            stress_out[points * c : points * (c + 1), lanes] = now[c]
        return carry

    lax.fori_loop(0, items // LANES, tile_step, 0)
    amount = amounts[...]
    high, low = two_terms(amount)
    harden = product(harden_map[...], jnp.concatenate([high, low, high], axis=0))
    grown = resist[...] + HARDENING * harden
    resist_out[...] = grown
    work = grown * amount
    stored = work[:points]
    for a in range(1, systems):
        stored = stored + work[points * a : points * (a + 1)]
    prolonged(stored, repeat[...], spread[...], energy)


def own_and_other(odd, even_value, odd_value):
    return jnp.where(odd > 0, odd_value, even_value)


def new_layer(grains, x, lower, upper, z_pair, z_other, energy, odd_z, mobility, grain_state):
    orders, _, size_z, size_y = grains.shape
    row = lax.broadcasted_iota(jnp.int32, (size_z, size_y), 0)
    center = [grains[order, x] for order in range(orders)]
    squares = [value * value for value in center]
    total = squares[0]
    for order in range(1, orders):
        total = total + squares[order]
    shared = 2.0 * CROSS_TERM * total + 5.0
    cell = energy[x // 2]
    found = []
    for order in range(orders):
        value = center[order]
        z_mate, z_next = z_pair[order, x : x + 1], z_other[order, x : x + 1]
        below = jnp.where(row == 0, own_and_other(odd_z, z_next, z_mate), pltpu.roll(value, 1, 0))
        above = jnp.where(
            row == size_z - 1,
            own_and_other(odd_z, z_mate, z_next),
            pltpu.roll(value, size_z - 1, 0),
        )
        around = (
            (lower(order) + upper(order))
            + (below + above)
            + (pltpu.roll(value, 1, 1) + pltpu.roll(value, size_y - 1, 1))
        )
        share = 2.0 * DRIVE_SCALE * (1.0 - grain_state[order])
        factor = shared + share * cell - 2.0 * squares[order]
        found.append(value + (TIME_STEP * mobility[order]) * (around - value * factor))
    return found


def new_ends(grains, x_pair, x_other, odd_x, *others):
    last = grains.shape[1] - 1
    low = new_layer(
        grains,
        0,
        lambda order: own_and_other(odd_x, x_other[order], x_pair[order]),
        lambda order: grains[order, 1],
        *others,
    )
    high = new_layer(
        grains,
        last,
        lambda order: grains[order, last - 1],
        lambda order: own_and_other(odd_x, x_pair[order], x_other[order]),
        *others,
    )
    return low, high


def new_inner(grains, x, *others):
    return new_layer(
        grains,
        x,
        lambda order: grains[order, x - 1],
        lambda order: grains[order, x + 1],
        *others,
    )


def send_layers(odd_x, order, low, high, x_pair, x_other):
    x_pair[order] = own_and_other(odd_x, high, low)
    x_other[order] = own_and_other(odd_x, low, high)


def send_rows(odd_z, order, x, new, z_pair, z_other):
    size_z = new.shape[0]
    first, last = new[:1], new[size_z - 1 :]
    z_pair[order, x : x + 1] = own_and_other(odd_z, last, first)
    z_other[order, x : x + 1] = own_and_other(odd_z, first, last)


def edges_kernel(grains, odd, x_pair, x_other, z_pair, z_other):
    orders, size_x, _, _ = grains.shape
    for order in range(orders):
        send_layers(
            odd[0], order, grains[order, 0], grains[order, size_x - 1], x_pair, x_other
        )
        for x in range(size_x):
            send_rows(odd[1], order, x, grains[order, x], z_pair, z_other)


def first_ends_kernel(
    grains,
    x_pair,
    x_other,
    z_pair,
    z_other,
    energy,
    odd,
    mobility,
    grain_state,
    x_pair_out,
    x_other_out,
):
    low, high = new_ends(
        grains, x_pair, x_other, odd[0], z_pair, z_other, energy, odd[1], mobility, grain_state
    )
    for order in range(grains.shape[0]):
        send_layers(odd[0], order, low[order], high[order], x_pair_out, x_other_out)


def first_inner_kernel(
    grains,
    z_pair,
    z_other,
    energy,
    x_pair_new,
    x_other_new,
    odd,
    mobility,
    grain_state,
    out,
    z_pair_out,
    z_other_out,
):
    orders, size_x, _, _ = grains.shape
    for order in range(orders):
        low = own_and_other(odd[0], x_other_new[order], x_pair_new[order])
        high = own_and_other(odd[0], x_pair_new[order], x_other_new[order])
        for x, new in ((0, low), (size_x - 1, high)):
            out[order, x] = new
            send_rows(odd[1], order, x, new, z_pair_out, z_other_out)
    for x in range(1, size_x - 1):
        found = new_inner(grains, x, z_pair, z_other, energy, odd[1], mobility, grain_state)
        for order in range(orders):
            out[order, x] = found[order]
            send_rows(odd[1], order, x, found[order], z_pair_out, z_other_out)


def second_inner_kernel(grains, z_pair, z_other, energy, odd, mobility, grain_state, out):
    orders, size_x, _, _ = grains.shape
    for x in range(1, size_x - 1):
        found = new_inner(grains, x, z_pair, z_other, energy, odd[1], mobility, grain_state)
        for order in range(orders):
            out[order, x] = found[order]


def second_ends_kernel(
    grains,
    x_pair,
    x_other,
    z_pair,
    z_other,
    energy,
    inner,
    odd,
    mobility,
    grain_state,
    out,
    x_pair_out,
    x_other_out,
    z_pair_out,
    z_other_out,
):
    orders, size_x, _, _ = grains.shape
    low, high = new_ends(
        grains, x_pair, x_other, odd[0], z_pair, z_other, energy, odd[1], mobility, grain_state
    )
    for order in range(orders):
        send_layers(odd[0], order, low[order], high[order], x_pair_out, x_other_out)
        for x, new in ((0, low[order]), (size_x - 1, high[order])):
            out[order, x] = new
            send_rows(odd[1], order, x, new, z_pair_out, z_other_out)
        for x in range(1, size_x - 1):
            send_rows(odd[1], order, x, inner[order, x], z_pair_out, z_other_out)


def last_inner_kernel(
    grains, z_pair, z_other, energy, odd, mobility, grain_state, out, held, sems
):
    orders, size_x, _, _ = grains.shape
    copies = []
    for x in range(1, size_x - 1):
        found = new_inner(grains, x, z_pair, z_other, energy, odd[1], mobility, grain_state)
        for order in range(orders):
            held[x - 1, order] = found[order]
        copies.append(pltpu.make_async_copy(held.at[x - 1], out.at[:, x], sems.at[x - 1]))
        copies[-1].start()
    for copy in copies:
        copy.wait()


def last_ends_kernel(
    grains,
    x_pair,
    x_other,
    z_pair,
    z_other,
    energy,
    inner,
    odd,
    mobility,
    grain_state,
    out,
    held,
    sems,
):
    orders, size_x, _, _ = grains.shape
    ends = new_ends(
        grains, x_pair, x_other, odd[0], z_pair, z_other, energy, odd[1], mobility, grain_state
    )
    copies = []
    for side, x in ((0, 0), (1, size_x - 1)):
        for order in range(orders):
            held[side, order] = ends[side][order]
        copies.append(pltpu.make_async_copy(held.at[side], out.at[:, x], sems.at[side]))
        copies[-1].start()
    for copy in copies:
        copy.wait()


def swapped(value, axis, first):
    size = lax.axis_size(axis)
    pairs = [(i % size, (i + 1) % size) for i in range(first, size + first, 2)]
    return lax.ppermute(value, axis, pairs + [(j, i) for i, j in pairs])


def halos(edges):
    return (
        swapped(edges[0], "gx", 0),
        swapped(edges[1], "gx", 1),
        swapped(edges[2], "gz", 0),
        swapped(edges[3], "gz", 1),
    )


def shards(
    grains,
    block_owner,
    element_anchor,
    strain_step,
    stress,
    resistance,
    slip_active,
    orientation_schmid,
    latent_hardening,
    mobility,
    grain_state,
):
    count_all = lax.axis_size(("gx", "gz"))
    per_dev = element_anchor.shape[0]
    slots_all = 2 * per_dev
    orders, size_x, size_z, size_y = grains.shape
    points = stress.shape[1]
    systems = resistance.shape[0]
    tensors, forces = 6 * points, systems * points
    narrow = -(-(tensors + forces) // LANES) * LANES
    scalars = pl.BlockSpec(memory_space=pltpu.SMEM)
    whole = pl.BlockSpec(memory_space=pltpu.VMEM)
    far = pl.BlockSpec(memory_space=pltpu.HBM)
    anchor = element_anchor.reshape(1, per_dev)
    message = 5 * slots_all // 2

    outbox = call(
        pack_state_kernel,
        shape(message, LANES),
        limit=None,
        scratch=(
            pltpu.VMEM((2 * tensors + forces, per_dev), F32),
            pltpu.VMEM((systems, per_dev), jnp.int32),
            pltpu.VMEM((slots_all, 2 * LANES), F32),
            pltpu.VMEM((slots_all // 2, LANES), F32),
            pltpu.SemaphoreType.DMA((4,)),
        ),
        in_specs=[whole, far, far, far, far],
    )(
        anchor,
        strain_step.reshape(tensors, per_dev),
        stress.reshape(tensors, per_dev),
        resistance.reshape(forces, per_dev),
        slip_active,
    )
    inbox = exchanged(outbox.reshape(count_all, 5, 4, LANES)).reshape(message, LANES)

    whole_number = functools.partial(jax.ShapeDtypeStruct, dtype=jnp.int32)
    half_wide = functools.partial(jax.ShapeDtypeStruct, dtype=BF16)
    (
        mailbox_row,
        mailbox_col,
        anchor_col,
        tensor_map,
        harden_map,
        active_map,
        rows,
        lanes,
        repeat,
        spread,
    ) = call(
        prepare_kernel,
        (
            whole_number((1, per_dev)),
            whole_number((per_dev, LANES)),
            whole_number((per_dev, LANES)),
            half_wide((6 * forces, 3 * orders * points)),
            half_wide((forces, 3 * forces)),
            half_wide((forces, systems)),
            half_wide((128, 256)),
            half_wide((1024, 256)),
            half_wide((32, 16)),
            half_wide((512, 256)),
        ),
        limit=12,
    )(
        block_owner,
        anchor,
        orientation_schmid.reshape(orders, systems * 6).T,
        latent_hardening,
    )
    odd = jnp.stack([lax.axis_index("gx") % 2, lax.axis_index("gz") % 2]).astype(jnp.int32)
    edge_shapes = (
        shape(orders, size_z, size_y),
        shape(orders, size_z, size_y),
        shape(orders, size_x, size_y),
        shape(orders, size_x, size_y),
    )
    edges = call(edges_kernel, edge_shapes, limit=4, in_specs=[whole, scalars])(grains, odd)
    strain_h = stress_h = resist_h = active_h = None
    for cycle in range(STEPS):
        around = halos(edges)
        weights = call(restrict_kernel, shape(orders * points, per_dev), limit=8)(
            grains, rows, lanes
        )
        if cycle == 0:
            strain_h, stress_h, resist_h, active_h = call(
                unpack_state_kernel,
                (
                    shape(tensors, per_dev),
                    shape(tensors, per_dev),
                    shape(forces, per_dev),
                    shape(systems, per_dev),
                ),
                limit=16,
                scratch=(
                    pltpu.VMEM((slots_all, 2 * LANES), F32),
                    pltpu.VMEM((slots_all // 2, LANES), F32),
                ),
            )(mailbox_col, inbox)
        stress_h, resist_h, energy = call(
            mechanics_kernel,
            (
                shape(tensors, per_dev),
                shape(forces, per_dev),
                shape(size_x // 2, size_z, size_y),
            ),
            limit=12,
            scratch=(
                pltpu.VMEM((6 * forces, per_dev), F32),
                pltpu.VMEM((forces, per_dev), F32),
                pltpu.VMEM((forces, per_dev), F32),
            ),
        )(
            weights,
            strain_h,
            stress_h,
            resist_h,
            active_h,
            tensor_map,
            harden_map,
            active_map,
            repeat,
            spread,
        )
        if cycle == STEPS - 1:
            around, stress_h = lax.optimization_barrier((around, stress_h))
        brick = shape(orders, size_x, size_z, size_y)
        tables = (odd, mobility, grain_state)
        x_pair, x_other = call(
            first_ends_kernel, edge_shapes[:2], limit=4, in_specs=[whole] * 6 + [scalars] * 3
        )(grains, *around, energy, *tables)
        grains, z_pair, z_other = call(
            first_inner_kernel,
            (brick,) + edge_shapes[2:],
            limit=4,
            in_specs=[whole] * 6 + [scalars] * 3,
        )(grains, *around[2:], energy, x_pair, x_other, *tables)
        around = halos((x_pair, x_other, z_pair, z_other))
        if cycle < STEPS - 1:
            inner = call(
                second_inner_kernel, brick, limit=4, in_specs=[whole] * 4 + [scalars] * 3
            )(grains, *around[2:], energy, *tables)
            grains, *edges = call(
                second_ends_kernel,
                (brick,) + edge_shapes,
                limit=4,
                in_specs=[whole] * 7 + [scalars] * 3,
                input_output_aliases={6: 0},
            )(grains, *around, energy, inner, *tables)
        else:
            inner = call(
                last_inner_kernel,
                brick,
                limit=6,
                in_specs=[whole] * 4 + [scalars] * 3,
                out_specs=far,
                scratch=(
                    pltpu.VMEM((size_x - 2, orders, size_z, size_y), F32),
                    pltpu.SemaphoreType.DMA((size_x - 2,)),
                ),
            )(grains, *around[2:], energy, *tables)
            last = (grains, *around, energy, inner, *tables)
    outbox = call(pack_result_kernel, shape(slots_all, narrow), limit=12)(
        mailbox_row, stress_h, resist_h
    )
    inbox = exchanged(outbox.reshape(count_all, slots_all // count_all, narrow))
    stress, resistance = call(
        unpack_result_kernel, (shape(tensors, per_dev), shape(forces, per_dev)), limit=12
    )(anchor_col, inbox.reshape(slots_all, narrow))
    last, stress, resistance = lax.optimization_barrier((last, stress, resistance))
    grains = call(
        last_ends_kernel,
        brick,
        limit=4,
        in_specs=[whole] * 6 + [far] + [scalars] * 3,
        out_specs=far,
        scratch=(
            pltpu.VMEM((2, orders, size_z, size_y), F32),
            pltpu.SemaphoreType.DMA((2,)),
        ),
        input_output_aliases={6: 0},
    )(*last)
    return (
        grains,
        stress.reshape(6, points, per_dev),
        resistance.reshape(systems, points, per_dev),
    )


def solution(mesh):
    return jax.shard_map(
        shards,
        mesh=mesh,
        in_specs=(
            P(None, "gx", "gz", None),
            P("gx", "gz", None),
            P(("gx", "gz")),
            P(None, None, ("gx", "gz")),
            P(None, None, ("gx", "gz")),
            P(None, None, ("gx", "gz")),
            P(None, ("gx", "gz")),
            P(),
            P(),
            P(),
            P(),
        ),
        out_specs=(
            P(None, "gx", "gz", None),
            P(None, None, ("gx", "gz")),
            P(None, None, ("gx", "gz")),
        ),
        check_vma=False,
    )
```

time: 151 us -> 119 us (0.79)
  starting transfers between devices: 66.5 us -> 48.6 us
  local copies, waits for them, and re-layouts: 27.4 us -> 10.4 us
  Pallas kernels: 29 us -> 39.5 us
  other arithmetic: 7.22 us -> 0.08 us
    ppermute x24, starting transfers between devices: 50.1 us -> 31.9 us  [swapped(): return lax.ppermute(value, axis, pairs + [(j, i) for i, j in pairs])]
    convert_element_type x8 -> x0, local copies, waits for them, and re-layouts: 12.1 us -> none  [the longest x6 12 us: shards(): over_points(part, points).astype(BF16)]
    pallas_call x11 -> x19, Pallas kernels: 15.7 us -> 26.2 us  [the longest x3 4.83 us: shards(): call(first_inner_kernel, (brick,) + edge_shapes[2:], limit=4, in_specs=[w...]
    all_to_all x2, waiting for transfers between devices: 0.01 us -> 5.94 us  [exchanged(): lax.all_to_all(sent, ('gx', 'gz'), split_axis=0, concat_axis=0, tiled=True)]
    ppermute x24, waiting for transfers between devices: 17.9 us -> 12.7 us  [swapped(): return lax.ppermute(value, axis, pairs + [(j, i) for i, j in pairs])]
    convert_element_type x6 -> x0, other arithmetic: 4.39 us -> none  [the longest x2 4.37 us: shards(): over_points(part, points).astype(BF16)]
    unnamed x64 -> x54, local copies, waits for them, and re-layouts: 11.6 us -> 9.65 us
    squeeze x1 -> x0, local copies, waits for them, and re-layouts: 1.68 us -> none  [shards(): grains[:, 0]]
  transfers between devices with their start and end apart: 26 -> 26, of which waited for: 5 -> 8; matrix products, arithmetic and copies ran while one was open for 16% -> 1% of each run, Pallas kernels for 9% -> 23%
where the time goes in v2:
time: 119 us; the launch traced here: 118 us
  starting transfers between devices  48.6 us (41%)
  Pallas kernels  39.5 us (33%)
  waiting for transfers between devices  18.7 us (16%)
  local copies, waits for them, and re-layouts  10.4 us (9%)
  between operations  1.28 us (1%)
    ppermute x24, starting transfers between devices, swapped(): return lax.ppermute(value, axis, pairs + [(j, i) for i, j in pairs])  31.9 us
    all_to_all x2, starting transfers between devices, exchanged(): lax.all_to_all(sent, ('gx', 'gz'), split_axis=0, concat_axis=0, tiled=True)  16.6 us
    ppermute x24, waiting for transfers between devices, swapped(): return lax.ppermute(value, axis, pairs + [(j, i) for i, j in pairs])  12.7 us
    pallas_call x3, Pallas kernels, shards(): call(mechanics_kernel, (shape(tensors, per_dev), shape(forces, per_dev),...  10.4 us
    unnamed x54, local copies, waits for them, and re-layouts  9.65 us
    all_to_all x2, waiting for transfers between devices, exchanged(): lax.all_to_all(sent, ('gx', 'gz'), split_axis=0, concat_axis=0, tiled=True)  5.94 us
    pallas_call x3, Pallas kernels, shards(): call(first_inner_kernel, (brick,) + edge_shapes[2:], limit=4, in_specs=[w...  4.83 us
    pallas_call x1, Pallas kernels, shards(): call(pack_state_kernel, shape(message, LANES), limit=None, scratch=(pltpu...  4.14 us
  transfers between devices with their start and end apart: 26, of which 8 were waited for; matrix products, arithmetic and copies ran while one was open for 1% of the time, Pallas kernels for 23%

profile of v2, /device:TPU:0, one launch (start us, length us, event | category | flops | bytes accessed | tf_op | source)
XLA Modules:
  0.0 118.5 jit_solution(14632829043747075050)
XLA Ops:
  0.6 4.1 %shard_map.133 = f32[2560,128]{1,0:T(8,128)} custom-call(s32[1,512]{1,0:T(1,128)} %bitcast.18, f32[48,512]{1,0:T(8,128)} %bitcast.22, f32[48,512]{1,0:T(8,128)} %bitcast.23, f32[192,512]{1,0:T(8,128)} %bitcast.21, s32[24,512]{1,0:T(8,128)} %active.1), custom_call_target="tpu_custom_call" | custom-call | tf_op jit(solution)/shard_map/pallas_call | solution.py:665
  4.8 11.2 %all-to-all-start = ((f32[128,5,4,128]{3,2,1,0:T(4,128)}), f32[128,5,4,128]{3,2,1,0:T(4,128)S(1)}, u32[]{:S(2)}, u32[]{:S(2)}) async-start(f32[128,5,4,128]{3,2,1,0:T(4,128)} %bitcast.20), calls=%async_computation | async-start | bytes 2621440 | tf_op jit(solution)/shard_map/all_to_all | solution.py:178
  16.1 1.4 %shard_map.130 = (f32[8,16,256]{2,1,0:T(8,128)}, f32[8,16,256]{2,1,0:T(8,128)}, f32[8,8,256]{2,1,0:T(8,128)}, f32[8,8,256]{2,1,0:T(8,128)}) custom-call(f32[8,8,16,256]{3,2,1,0:T(8,128)S(1)} %copy-done, s32[2]{0:T(128)S(1)} %pad_add_fusion.odd), custom_call_target="tpu_custom_call" | custom-call | tf_op jit(solution)/shard_map/pallas_call | solution.py:727
  18.5 4.5 %collective-permute-start.3 = (f32[8,16,256]{2,1,0:T(8,128)}, f32[8,16,256]{2,1,0:T(8,128)}, u32[]{:S(2)}, u32[]{:S(2)}) collective-permute-start(f32[8,16,256]{2,1,0:T(8,128)} %get-tuple-element.90), channel_id=1, source_target_pairs={{8,16},{24,32},{40,48},{56,64},{72,80},{88,96},{104,112},{120,0},{... | collective-permute-start | bytes 393224 | tf_op jit(solution)/shard_map/ppermute | solution.py:626
  23.0 3.0 %collective-permute-start.1 = (f32[8,8,256]{2,1,0:T(8,128)}, f32[8,8,256]{2,1,0:T(8,128)}, u32[]{:S(2)}, u32[]{:S(2)}) collective-permute-start(f32[8,8,256]{2,1,0:T(8,128)} %get-tuple-element.75), channel_id=1, source_target_pairs={{1,2},{3,4},{5,6},{7,0},{2,1},{4,3},{6,5},{0,7},{9,10},{11,12},{13... | collective-permute-start | bytes 196616 | tf_op jit(solution)/shard_map/ppermute | solution.py:626
  35.3 3.8 %all-to-all-done = f32[128,5,4,128]{3,2,1,0:T(4,128)S(1)} async-done(((f32[128,5,4,128]{3,2,1,0:T(4,128)}), f32[128,5,4,128]{3,2,1,0:T(4,128)S(1)}, u32[]{:S(2)}, u32[]{:S(2)}) %all-to-all-start) | async-done | bytes 1310752 | tf_op jit(solution)/shard_map/all_to_all | solution.py:178
  40.2 1.4 %shard_map.134 = (f32[48,512]{1,0:T(8,128)S(1)}, f32[48,512]{1,0:T(8,128)S(1)}, f32[192,512]{1,0:T(8,128)S(1)}, f32[24,512]{1,0:T(8,128)S(1)}) custom-call(s32[512,128]{1,0:T(8,128)S(1)} %copy-done.17, f32[2560,128]{1,0:T(8,128)S(1)} %bitcast.15), custom_call_target="tpu_custom_call" | custom-call | tf_op jit(solution)/shard_map/pallas_call | solution.py:735
  41.7 3.5 %shard_map.135 = (f32[48,512]{1,0:T(8,128)S(1)}, f32[192,512]{1,0:T(8,128)S(1)}, f32[4,16,256]{2,1,0:T(8,128)S(1)}) custom-call(f32[64,512]{1,0:T(8,128)S(1)} %copy-done.6, f32[48,512]{1,0:T(8,128)S(1)} %get-tuple-element.79.strain, f32[48,512]{1,0:T(8,128)S(1)} %get-tuple-element.80.stress, f32[192,512]{1,0:T(8,128)S(1)} %get-tuple-element.81.resist, ...), custom_call_target="tpu_custom_call" | custom-call | tf_op jit(solution)/shard_map/pallas_call | solution.py:749
  45.2 1.3 %shard_map.136 = (f32[8,16,256]{2,1,0:T(8,128)S(1)}, f32[8,16,256]{2,1,0:T(8,128)S(1)}) custom-call(f32[8,8,16,256]{3,2,1,0:T(8,128)S(1)} %copy-done, f32[8,16,256]{2,1,0:T(8,128)} %collective-permute-done.2.x_pair, f32[8,16,256]{2,1,0:T(8,128)} %collective-permute-done.3.x_other, f32[8,8,256]{2,1,0:T(8,128)} %collective-permute-done.z_pair, ...), custom_call_target="tpu_custom_call" | custom-call | tf_op jit(solution)/shard_map/pallas_call | solution.py:778
  46.9 1.7 %shard_map.137 = (f32[8,8,16,256]{3,2,1,0:T(8,128)S(1)}, f32[8,8,256]{2,1,0:T(8,128)S(1)}, f32[8,8,256]{2,1,0:T(8,128)S(1)}) custom-call(f32[8,8,16,256]{3,2,1,0:T(8,128)S(1)} %copy-done, f32[8,8,256]{2,1,0:T(8,128)} %collective-permute-done.z_pair, f32[8,8,256]{2,1,0:T(8,128)} %collective-permute-done.1.z_other, ...), custom_call_target="tpu_custom_call" | custom-call | tf_op jit(solution)/shard_map/pallas_call | solution.py:781
  48.7 1.4 %collective-permute-start.7 = (f32[8,8,256]{2,1,0:T(8,128)S(1)}, f32[8,8,256]{2,1,0:T(8,128)S(1)}, u32[]{:S(2)}, u32[]{:S(2)}) collective-permute-start(f32[8,8,256]{2,1,0:T(8,128)S(1)} %get-tuple-element.95), channel_id=1, source_target_pairs={{1,2},{3,4},{5,6},{7,0},{2,1},{4,3},{6,5},{0,7},{9,10},{11,12},{13... | collective-permute-start | bytes 196616 | tf_op jit(solution)/shard_map/ppermute | solution.py:626
  50.2 3.5 %collective-permute-done.7.z_other = f32[8,8,256]{2,1,0:T(8,128)S(1)} collective-permute-done((f32[8,8,256]{2,1,0:T(8,128)S(1)}, f32[8,8,256]{2,1,0:T(8,128)S(1)}, u32[]{:S(2)}, u32[]{:S(2)}) %collective-permute-start.7) | collective-permute-done | bytes 65568 | tf_op jit(solution)/shard_map/ppermute | solution.py:626
  55.9 1.7 %collective-permute-start.10 = (f32[8,16,256]{2,1,0:T(8,128)S(1)}, f32[8,16,256]{2,1,0:T(8,128)S(1)}, u32[]{:S(2)}, u32[]{:S(2)}) collective-permute-start(f32[8,16,256]{2,1,0:T(8,128)S(1)} %get-tuple-element.102), channel_id=1, source_target_pairs={{0,8},{16,24},{32,40},{48,56},{64,72},{80,88},{96,104},{112,120},{... | collective-permute-start | bytes 393224 | tf_op jit(solution)/shard_map/ppermute | solution.py:626
  57.6 3.5 %collective-permute-start.11 = (f32[8,16,256]{2,1,0:T(8,128)S(1)}, f32[8,16,256]{2,1,0:T(8,128)S(1)}, u32[]{:S(2)}, u32[]{:S(2)}) collective-permute-start(f32[8,16,256]{2,1,0:T(8,128)S(1)} %get-tuple-element.103), channel_id=1, source_target_pairs={{8,16},{24,32},{40,48},{56,64},{72,80},{88,96},{104,112},{120,0},{... | collective-permute-start | bytes 393224 | tf_op jit(solution)/shard_map/ppermute | solution.py:626
  61.6 3.5 %shard_map.141 = (f32[48,512]{1,0:T(8,128)S(1)}, f32[192,512]{1,0:T(8,128)S(1)}, f32[4,16,256]{2,1,0:T(8,128)S(1)}) custom-call(f32[64,512]{1,0:T(8,128)S(1)} %shard_map.140.weights, f32[48,512]{1,0:T(8,128)S(1)} %get-tuple-element.79.strain, f32[48,512]{1,0:T(8,128)S(1)} %get-tuple-element.99.stress, f32[192,512]{1,0:T(8,128)S(1)} %get-tuple-element.100.resist, ...), custom_call_target="tpu_custom_call" | custom-call | tf_op jit(solution)/shard_map/pallas_call | solution.py:749
  66.9 3.5 %collective-permute-start.13 = (f32[8,16,256]{2,1,0:T(8,128)S(1)}, f32[8,16,256]{2,1,0:T(8,128)S(1)}, u32[]{:S(2)}, u32[]{:S(2)}) collective-permute-start(f32[8,16,256]{2,1,0:T(8,128)S(1)} %get-tuple-element.105.x_other_new), channel_id=1, source_target_pairs={{8,16},{24,32},{40,48},{56,64},{72,80},{88,96},{104,112},{120,0},{... | collective-permute-start | bytes 393224 | tf_op jit(solution)/shard_map/ppermute | solution.py:626
  70.4 1.4 %shard_map.143 = (f32[8,8,16,256]{3,2,1,0:T(8,128)S(1)}, f32[8,8,256]{2,1,0:T(8,128)S(1)}, f32[8,8,256]{2,1,0:T(8,128)S(1)}) custom-call(f32[8,8,16,256]{3,2,1,0:T(8,128)S(1)} %get-tuple-element.96.grains, f32[8,8,256]{2,1,0:T(8,128)S(1)} %collective-permute-done.8.z_pair, f32[8,8,256]{2,1,0:T(8,128)S(1)} %collective-permute-done.9.z_other, ...), custom_call_target="tpu_custom_call" | custom-call | tf_op jit(solution)/shard_map/pallas_call | solution.py:781
  73.1 3.7 %collective-permute-done.15.z_other = f32[8,8,256]{2,1,0:T(8,128)S(1)} collective-permute-done((f32[8,8,256]{2,1,0:T(8,128)S(1)}, f32[8,8,256]{2,1,0:T(8,128)S(1)}, u32[]{:S(2)}, u32[]{:S(2)}) %collective-permute-start.15) | collective-permute-done | bytes 65568 | tf_op jit(solution)/shard_map/ppermute | solution.py:626
  79.1 2.1 %collective-permute-start.17 = (f32[8,16,256]{2,1,0:T(8,128)S(1)}, f32[8,16,256]{2,1,0:T(8,128)S(1)}, u32[]{:S(2)}, u32[]{:S(2)}) collective-permute-start(f32[8,16,256]{2,1,0:T(8,128)S(1)} %get-tuple-element.111), channel_id=1, source_target_pairs={{8,16},{24,32},{40,48},{56,64},{72,80},{88,96},{104,112},{120,0},{... | collective-permute-start | bytes 393224 | tf_op jit(solution)/shard_map/ppermute | solution.py:626
  81.2 1.5 %collective-permute-start.19 = (f32[8,8,256]{2,1,0:T(8,128)S(1)}, f32[8,8,256]{2,1,0:T(8,128)S(1)}, u32[]{:S(2)}, u32[]{:S(2)}) collective-permute-start(f32[8,8,256]{2,1,0:T(8,128)S(1)} %get-tuple-element.113), channel_id=1, source_target_pairs={{1,2},{3,4},{5,6},{7,0},{2,1},{4,3},{6,5},{0,7},{9,10},{11,12},{13... | collective-permute-start | bytes 196616 | tf_op jit(solution)/shard_map/ppermute | solution.py:626
  83.1 3.5 %shard_map.147 = (f32[48,512]{1,0:T(8,128)S(1)}, f32[192,512]{1,0:T(8,128)S(1)}, f32[4,16,256]{2,1,0:T(8,128)S(1)}) custom-call(f32[64,512]{1,0:T(8,128)S(1)} %shard_map.146.weights, f32[48,512]{1,0:T(8,128)S(1)} %get-tuple-element.79.strain, f32[48,512]{1,0:T(8,128)S(1)} %get-tuple-element.114.stress, f32[192,512]{1,0:T(8,128)S(1)} %get-tuple-element.115.resist, ...), custom_call_target="tpu_custom_call" | custom-call | tf_op jit(solution)/shard_map/pallas_call | solution.py:749
  87.5 1.8 %shard_map.151 = f32[1024,256]{1,0:T(8,128)} custom-call(s32[1,512]{1,0:T(1,128)S(1)} %copy-done.25, f32[48,512]{1,0:T(8,128)S(1)} %get-tuple-element.129.stress, f32[192,512]{1,0:T(8,128)S(1)} %get-tuple-element.130.resist), custom_call_target="tpu_custom_call" | custom-call | tf_op jit(solution)/shard_map/pallas_call | solution.py:812
  89.3 5.4 %all-to-all-start.1 = ((f32[128,8,256]{2,1,0:T(8,128)}), f32[128,8,256]{2,1,0:T(8,128)S(1)}, u32[]{:S(2)}, u32[]{:S(2)}) async-start(f32[128,8,256]{2,1,0:T(8,128)} %bitcast.9), calls=%async_computation.1 | async-start | bytes 2097152 | tf_op jit(solution)/shard_map/all_to_all | solution.py:178
  94.7 1.4 %shard_map.148 = (f32[8,16,256]{2,1,0:T(8,128)}, f32[8,16,256]{2,1,0:T(8,128)S(1)}) custom-call(f32[8,8,16,256]{3,2,1,0:T(8,128)S(1)} %get-tuple-element.109.grains, f32[8,16,256]{2,1,0:T(8,128)S(1)} %collective-permute-done.16.x_pair, f32[8,16,256]{2,1,0:T(8,128)S(1)} %collective-permute-done.17.x_other, f32[8,8,256]{2,1,0:T(8,128)S(1)} %collective-permute-done.18.z_pair, ...), custom_call_target="tpu_custom_call" | custom-call | tf_op jit(solution)/shard_map/pallas_call | solution.py:778
  97.3 4.5 %collective-permute-start.21 = (f32[8,16,256]{2,1,0:T(8,128)S(1)}, f32[8,16,256]{2,1,0:T(8,128)}, u32[]{:S(2)}, u32[]{:S(2)}) collective-permute-start(f32[8,16,256]{2,1,0:T(8,128)S(1)} %get-tuple-element.123.x_other_new), channel_id=1, source_target_pairs={{8,16},{24,32},{40,48},{56,64},{72,80},{88,96},{104,112},{120,0},{... | collective-permute-start | bytes 393224 | tf_op jit(solution)/shard_map/ppermute | solution.py:626
  103.4 1.7 %shard_map.149 = (f32[8,8,16,256]{3,2,1,0:T(8,128)S(1)}, f32[8,8,256]{2,1,0:T(8,128)S(1)}, f32[8,8,256]{2,1,0:T(8,128)S(1)}) custom-call(f32[8,8,16,256]{3,2,1,0:T(8,128)S(1)} %get-tuple-element.109.grains, f32[8,8,256]{2,1,0:T(8,128)S(1)} %copy-done.13, f32[8,8,256]{2,1,0:T(8,128)S(1)} %copy-done.15, f32[4,16,256]{2,1,0:T(8,128)S(1)} %get-tuple-element.138.energy, ...), custom_call_target="tpu_custom_call" | custom-call | tf_op jit(solution)/shard_map/pallas_call | solution.py:781
  105.3 3.0 %collective-permute-start.23 = (f32[8,8,256]{2,1,0:T(8,128)S(1)}, f32[8,8,256]{2,1,0:T(8,128)S(1)}, u32[]{:S(2)}, u32[]{:S(2)}) collective-permute-start(f32[8,8,256]{2,1,0:T(8,128)S(1)} %get-tuple-element.126), channel_id=1, source_target_pairs={{1,2},{3,4},{5,6},{7,0},{2,1},{4,3},{6,5},{0,7},{9,10},{11,12},{13... | collective-permute-start | bytes 196616 | tf_op jit(solution)/shard_map/ppermute | solution.py:626
  108.3 2.7 %collective-permute-done.23.z_other = f32[8,8,256]{2,1,0:T(8,128)S(1)} collective-permute-done((f32[8,8,256]{2,1,0:T(8,128)S(1)}, f32[8,8,256]{2,1,0:T(8,128)S(1)}, u32[]{:S(2)}, u32[]{:S(2)}) %collective-permute-start.23) | collective-permute-done | bytes 65568 | tf_op jit(solution)/shard_map/ppermute | solution.py:626
  110.9 1.9 %shard_map.150.inner = f32[8,8,16,256]{3,2,1,0:T(8,128)} custom-call(f32[8,8,16,256]{3,2,1,0:T(8,128)S(1)} %get-tuple-element.133.grains, f32[8,8,256]{2,1,0:T(8,128)S(1)} %collective-permute-done.22.z_pair, f32[8,8,256]{2,1,0:T(8,128)S(1)} %collective-permute-done.23.z_other, f32[4,16,256]{2,1,0:T(8,128)S(1)} %get-tuple-element.138.energy, ...), custom_call_target="tpu_custom_call" | custom-call | tf_op jit(solution)/shard_map/pallas_call | solution.py:800
  112.8 2.1 %all-to-all-done.1 = f32[128,8,256]{2,1,0:T(8,128)S(1)} async-done(((f32[128,8,256]{2,1,0:T(8,128)}), f32[128,8,256]{2,1,0:T(8,128)S(1)}, u32[]{:S(2)}, u32[]{:S(2)}) %all-to-all-start.1) | async-done | bytes 1048608 | tf_op jit(solution)/shard_map/all_to_all | solution.py:178
  115.0 1.5 %shard_map.152 = (f32[48,512]{1,0:T(8,128)}, f32[192,512]{1,0:T(8,128)}) custom-call(s32[512,128]{1,0:T(8,128)S(1)} %copy-done.11, f32[1024,256]{1,0:T(8,128)S(1)} %bitcast.16), custom_call_target="tpu_custom_call" | custom-call | tf_op jit(solution)/shard_map/pallas_call | solution.py:816
  116.5 1.8 %shard_map.153 = f32[8,8,16,256]{3,2,1,0:T(8,128)} custom-call(f32[8,8,16,256]{3,2,1,0:T(8,128)S(1)} %get-tuple-element.133.grains, f32[8,16,256]{2,1,0:T(8,128)S(1)} %collective-permute-done.20.x_pair, f32[8,16,256]{2,1,0:T(8,128)} %collective-permute-done.21.x_other, ...), custom_call_target="tpu_custom_call", output_to_operand_aliasing={{}: (6, {})} | custom-call | tf_op jit(solution)/shard_map/pallas_call | solution.py:820
  (101 shorter events, 24.3 us)
Async XLA Ops:
  4.8 11.3 %copy-start = (f32[8,8,16,256]{3,2,1,0:T(8,128)S(1)}, f32[8,8,16,256]{3,2,1,0:T(8,128)}, u32[]{:S(2)}) copy-start(f32[8,8,16,256]{3,2,1,0:T(8,128)} %grains.7) | copy-start | bytes 3145732
  4.8 21.2 %copy-start.26 = (f32[8,24,6]{1,0,2:T(8,128)S(1)}, f32[8,24,6]{1,0,2:T(8,128)}, u32[]{:S(2)}) copy-start(f32[8,24,6]{1,0,2:T(8,128)} %param.18) | copy-start | bytes 13828
  4.8 34.3 %all-to-all-start = ((f32[128,5,4,128]{3,2,1,0:T(4,128)}), f32[128,5,4,128]{3,2,1,0:T(4,128)S(1)}, u32[]{:S(2)}, u32[]{:S(2)}) async-start(f32[128,5,4,128]{3,2,1,0:T(4,128)} %bitcast.20), calls=%async_computation | async-start | bytes 2621440 | tf_op jit(solution)/shard_map/all_to_all | solution.py:178
  16.0 10.8 %copy-start.22 = (s32[512]{0:T(512)S(1)}, s32[512]{0:T(512)}, u32[]{:S(2)}) copy-start(s32[512]{0:T(512)} %param.13) | copy-start | bytes 6148
  17.5 27.7 %collective-permute-start.2 = (f32[8,16,256]{2,1,0:T(8,128)}, f32[8,16,256]{2,1,0:T(8,128)}, u32[]{:S(2)}, u32[]{:S(2)}) collective-permute-start(f32[8,16,256]{2,1,0:T(8,128)} %get-tuple-element.89), channel_id=1, source_target_pairs={{0,8},{16,24},{32,40},{48,56},{64,72},{80,88},{96,104},{112,120},{... | collective-permute-start | bytes 393224 | tf_op jit(solution)/shard_map/ppermute | solution.py:626
  18.5 26.6 %collective-permute-start.3 = (f32[8,16,256]{2,1,0:T(8,128)}, f32[8,16,256]{2,1,0:T(8,128)}, u32[]{:S(2)}, u32[]{:S(2)}) collective-permute-start(f32[8,16,256]{2,1,0:T(8,128)} %get-tuple-element.90), channel_id=1, source_target_pairs={{8,16},{24,32},{40,48},{56,64},{72,80},{88,96},{104,112},{120,0},{... | collective-permute-start | bytes 393224 | tf_op jit(solution)/shard_map/ppermute | solution.py:626
  23.0 22.1 %collective-permute-start = (f32[8,8,256]{2,1,0:T(8,128)}, f32[8,8,256]{2,1,0:T(8,128)}, u32[]{:S(2)}, u32[]{:S(2)}) collective-permute-start(f32[8,8,256]{2,1,0:T(8,128)} %get-tuple-element.74), channel_id=1, source_target_pairs={{0,1},{2,3},{4,5},{6,7},{1,0},{3,2},{5,4},{7,6},{8,9},{10,11},{12,... | collective-permute-start | bytes 196616 | tf_op jit(solution)/shard_map/ppermute | solution.py:626
  23.0 22.1 %collective-permute-start.1 = (f32[8,8,256]{2,1,0:T(8,128)}, f32[8,8,256]{2,1,0:T(8,128)}, u32[]{:S(2)}, u32[]{:S(2)}) collective-permute-start(f32[8,8,256]{2,1,0:T(8,128)} %get-tuple-element.75), channel_id=1, source_target_pairs={{1,2},{3,4},{5,6},{7,0},{2,1},{4,3},{6,5},{0,7},{9,10},{11,12},{13... | collective-permute-start | bytes 196616 | tf_op jit(solution)/shard_map/ppermute | solution.py:626
  46.5 8.5 %collective-permute-start.4 = (f32[8,16,256]{2,1,0:T(8,128)S(1)}, f32[8,16,256]{2,1,0:T(8,128)S(1)}, u32[]{:S(2)}, u32[]{:S(2)}) collective-permute-start(f32[8,16,256]{2,1,0:T(8,128)S(1)} %get-tuple-element.91.x_pair_new), channel_id=1, source_target_pairs={{0,8},{16,24},{32,40},{48,56},{64,72},{80,88},{96,104},{112,120},{... | collective-permute-start | bytes 393224 | tf_op jit(solution)/shard_map/ppermute | solution.py:626
  46.6 8.4 %collective-permute-start.5 = (f32[8,16,256]{2,1,0:T(8,128)S(1)}, f32[8,16,256]{2,1,0:T(8,128)S(1)}, u32[]{:S(2)}, u32[]{:S(2)}) collective-permute-start(f32[8,16,256]{2,1,0:T(8,128)S(1)} %get-tuple-element.92.x_other_new), channel_id=1, source_target_pairs={{8,16},{24,32},{40,48},{56,64},{72,80},{88,96},{104,112},{120,0},{... | collective-permute-start | bytes 393224 | tf_op jit(solution)/shard_map/ppermute | solution.py:626
  48.6 1.5 %collective-permute-start.6 = (f32[8,8,256]{2,1,0:T(8,128)S(1)}, f32[8,8,256]{2,1,0:T(8,128)S(1)}, u32[]{:S(2)}, u32[]{:S(2)}) collective-permute-start(f32[8,8,256]{2,1,0:T(8,128)S(1)} %get-tuple-element.94), channel_id=1, source_target_pairs={{0,1},{2,3},{4,5},{6,7},{1,0},{3,2},{5,4},{7,6},{8,9},{10,11},{12,... | collective-permute-start | bytes 196616 | tf_op jit(solution)/shard_map/ppermute | solution.py:626
  48.7 5.0 %collective-permute-start.7 = (f32[8,8,256]{2,1,0:T(8,128)S(1)}, f32[8,8,256]{2,1,0:T(8,128)S(1)}, u32[]{:S(2)}, u32[]{:S(2)}) collective-permute-start(f32[8,8,256]{2,1,0:T(8,128)S(1)} %get-tuple-element.95), channel_id=1, source_target_pairs={{1,2},{3,4},{5,6},{7,0},{2,1},{4,3},{6,5},{0,7},{9,10},{11,12},{13... | collective-permute-start | bytes 196616 | tf_op jit(solution)/shard_map/ppermute | solution.py:626
  55.9 10.1 %collective-permute-start.10 = (f32[8,16,256]{2,1,0:T(8,128)S(1)}, f32[8,16,256]{2,1,0:T(8,128)S(1)}, u32[]{:S(2)}, u32[]{:S(2)}) collective-permute-start(f32[8,16,256]{2,1,0:T(8,128)S(1)} %get-tuple-element.102), channel_id=1, source_target_pairs={{0,8},{16,24},{32,40},{48,56},{64,72},{80,88},{96,104},{112,120},{... | collective-permute-start | bytes 393224 | tf_op jit(solution)/shard_map/ppermute | solution.py:626
  57.6 8.4 %collective-permute-start.11 = (f32[8,16,256]{2,1,0:T(8,128)S(1)}, f32[8,16,256]{2,1,0:T(8,128)S(1)}, u32[]{:S(2)}, u32[]{:S(2)}) collective-permute-start(f32[8,16,256]{2,1,0:T(8,128)S(1)} %get-tuple-element.103), channel_id=1, source_target_pairs={{8,16},{24,32},{40,48},{56,64},{72,80},{88,96},{104,112},{120,0},{... | collective-permute-start | bytes 393224 | tf_op jit(solution)/shard_map/ppermute | solution.py:626
  61.1 3.9 %collective-permute-start.8 = (f32[8,8,256]{2,1,0:T(8,128)S(1)}, f32[8,8,256]{2,1,0:T(8,128)S(1)}, u32[]{:S(2)}, u32[]{:S(2)}) collective-permute-start(f32[8,8,256]{2,1,0:T(8,128)S(1)} %get-tuple-element.97), channel_id=1, source_target_pairs={{0,1},{2,3},{4,5},{6,7},{1,0},{3,2},{5,4},{7,6},{8,9},{10,11},{12,... | collective-permute-start | bytes 196616 | tf_op jit(solution)/shard_map/ppermute | solution.py:626
  61.1 4.9 %collective-permute-start.9 = (f32[8,8,256]{2,1,0:T(8,128)S(1)}, f32[8,8,256]{2,1,0:T(8,128)S(1)}, u32[]{:S(2)}, u32[]{:S(2)}) collective-permute-start(f32[8,8,256]{2,1,0:T(8,128)S(1)} %get-tuple-element.98), channel_id=1, source_target_pairs={{1,2},{3,4},{5,6},{7,0},{2,1},{4,3},{6,5},{0,7},{9,10},{11,12},{13... | collective-permute-start | bytes 196616 | tf_op jit(solution)/shard_map/ppermute | solution.py:626
  66.8 11.2 %collective-permute-start.12 = (f32[8,16,256]{2,1,0:T(8,128)S(1)}, f32[8,16,256]{2,1,0:T(8,128)S(1)}, u32[]{:S(2)}, u32[]{:S(2)}) collective-permute-start(f32[8,16,256]{2,1,0:T(8,128)S(1)} %get-tuple-element.104.x_pair_new), channel_id=1, source_target_pairs={{0,8},{16,24},{32,40},{48,56},{64,72},{80,88},{96,104},{112,120},{... | collective-permute-start | bytes 393224 | tf_op jit(solution)/shard_map/ppermute | solution.py:626
  66.9 11.1 %collective-permute-start.13 = (f32[8,16,256]{2,1,0:T(8,128)S(1)}, f32[8,16,256]{2,1,0:T(8,128)S(1)}, u32[]{:S(2)}, u32[]{:S(2)}) collective-permute-start(f32[8,16,256]{2,1,0:T(8,128)S(1)} %get-tuple-element.105.x_other_new), channel_id=1, source_target_pairs={{8,16},{24,32},{40,48},{56,64},{72,80},{88,96},{104,112},{120,0},{... | collective-permute-start | bytes 393224 | tf_op jit(solution)/shard_map/ppermute | solution.py:626
  71.8 1.3 %collective-permute-start.14 = (f32[8,8,256]{2,1,0:T(8,128)S(1)}, f32[8,8,256]{2,1,0:T(8,128)S(1)}, u32[]{:S(2)}, u32[]{:S(2)}) collective-permute-start(f32[8,8,256]{2,1,0:T(8,128)S(1)} %get-tuple-element.107), channel_id=1, source_target_pairs={{0,1},{2,3},{4,5},{6,7},{1,0},{3,2},{5,4},{7,6},{8,9},{10,11},{12,... | collective-permute-start | bytes 196616 | tf_op jit(solution)/shard_map/ppermute | solution.py:626
  71.9 5.0 %collective-permute-start.15 = (f32[8,8,256]{2,1,0:T(8,128)S(1)}, f32[8,8,256]{2,1,0:T(8,128)S(1)}, u32[]{:S(2)}, u32[]{:S(2)}) collective-permute-start(f32[8,8,256]{2,1,0:T(8,128)S(1)} %get-tuple-element.108), channel_id=1, source_target_pairs={{1,2},{3,4},{5,6},{7,0},{2,1},{4,3},{6,5},{0,7},{9,10},{11,12},{13... | collective-permute-start | bytes 196616 | tf_op jit(solution)/shard_map/ppermute | solution.py:626
  79.0 7.6 %collective-permute-start.16 = (f32[8,16,256]{2,1,0:T(8,128)S(1)}, f32[8,16,256]{2,1,0:T(8,128)S(1)}, u32[]{:S(2)}, u32[]{:S(2)}) collective-permute-start(f32[8,16,256]{2,1,0:T(8,128)S(1)} %get-tuple-element.110), channel_id=1, source_target_pairs={{0,8},{16,24},{32,40},{48,56},{64,72},{80,88},{96,104},{112,120},{... | collective-permute-start | bytes 393224 | tf_op jit(solution)/shard_map/ppermute | solution.py:626
  79.1 8.4 %collective-permute-start.17 = (f32[8,16,256]{2,1,0:T(8,128)S(1)}, f32[8,16,256]{2,1,0:T(8,128)S(1)}, u32[]{:S(2)}, u32[]{:S(2)}) collective-permute-start(f32[8,16,256]{2,1,0:T(8,128)S(1)} %get-tuple-element.111), channel_id=1, source_target_pairs={{8,16},{24,32},{40,48},{56,64},{72,80},{88,96},{104,112},{120,0},{... | collective-permute-start | bytes 393224 | tf_op jit(solution)/shard_map/ppermute | solution.py:626
  81.2 5.4 %collective-permute-start.18 = (f32[8,8,256]{2,1,0:T(8,128)S(1)}, f32[8,8,256]{2,1,0:T(8,128)S(1)}, u32[]{:S(2)}, u32[]{:S(2)}) collective-permute-start(f32[8,8,256]{2,1,0:T(8,128)S(1)} %get-tuple-element.112), channel_id=1, source_target_pairs={{0,1},{2,3},{4,5},{6,7},{1,0},{3,2},{5,4},{7,6},{8,9},{10,11},{12,... | collective-permute-start | bytes 196616 | tf_op jit(solution)/shard_map/ppermute | solution.py:626
  81.2 5.4 %collective-permute-start.19 = (f32[8,8,256]{2,1,0:T(8,128)S(1)}, f32[8,8,256]{2,1,0:T(8,128)S(1)}, u32[]{:S(2)}, u32[]{:S(2)}) collective-permute-start(f32[8,8,256]{2,1,0:T(8,128)S(1)} %get-tuple-element.113), channel_id=1, source_target_pairs={{1,2},{3,4},{5,6},{7,0},{2,1},{4,3},{6,5},{0,7},{9,10},{11,12},{13... | collective-permute-start | bytes 196616 | tf_op jit(solution)/shard_map/ppermute | solution.py:626
  86.6 8.1 %copy-start.12 = (f32[8,8,256]{2,1,0:T(8,128)}, f32[8,8,256]{2,1,0:T(8,128)S(1)}, u32[]{:S(2)}) copy-start(f32[8,8,256]{2,1,0:T(8,128)S(1)} %collective-permute-done.18.z_pair) | copy-start | bytes 196612
  86.6 8.1 %copy-start.14 = (f32[8,8,256]{2,1,0:T(8,128)}, f32[8,8,256]{2,1,0:T(8,128)S(1)}, u32[]{:S(2)}) copy-start(f32[8,8,256]{2,1,0:T(8,128)S(1)} %collective-permute-done.19.z_other) | copy-start | bytes 196612
  89.3 25.7 %all-to-all-start.1 = ((f32[128,8,256]{2,1,0:T(8,128)}), f32[128,8,256]{2,1,0:T(8,128)S(1)}, u32[]{:S(2)}, u32[]{:S(2)}) async-start(f32[128,8,256]{2,1,0:T(8,128)} %bitcast.9), calls=%async_computation.1 | async-start | bytes 2097152 | tf_op jit(solution)/shard_map/all_to_all | solution.py:178
  96.2 20.3 %collective-permute-start.20 = (f32[8,16,256]{2,1,0:T(8,128)}, f32[8,16,256]{2,1,0:T(8,128)S(1)}, u32[]{:S(2)}, u32[]{:S(2)}) collective-permute-start(f32[8,16,256]{2,1,0:T(8,128)} %get-tuple-element.122.x_pair_new), channel_id=1, source_target_pairs={{0,8},{16,24},{32,40},{48,56},{64,72},{80,88},{96,104},{112,120},{... | collective-permute-start | bytes 393224 | tf_op jit(solution)/shard_map/ppermute | solution.py:626
  97.3 19.2 %collective-permute-start.21 = (f32[8,16,256]{2,1,0:T(8,128)S(1)}, f32[8,16,256]{2,1,0:T(8,128)}, u32[]{:S(2)}, u32[]{:S(2)}) collective-permute-start(f32[8,16,256]{2,1,0:T(8,128)S(1)} %get-tuple-element.123.x_other_new), channel_id=1, source_target_pairs={{8,16},{24,32},{40,48},{56,64},{72,80},{88,96},{104,112},{120,0},{... | collective-permute-start | bytes 393224 | tf_op jit(solution)/shard_map/ppermute | solution.py:626
  105.2 9.8 %copy-start.11 = (s32[512,128]{1,0:T(8,128)S(1)}, s32[512,128]{1,0:T(8,128)}, u32[]{:S(2)}) copy-start(s32[512,128]{1,0:T(8,128)} %copy-done.10) | copy-start | bytes 786436
  105.2 3.1 %collective-permute-start.22 = (f32[8,8,256]{2,1,0:T(8,128)S(1)}, f32[8,8,256]{2,1,0:T(8,128)S(1)}, u32[]{:S(2)}, u32[]{:S(2)}) collective-permute-start(f32[8,8,256]{2,1,0:T(8,128)S(1)} %get-tuple-element.125), channel_id=1, source_target_pairs={{0,1},{2,3},{4,5},{6,7},{1,0},{3,2},{5,4},{7,6},{8,9},{10,11},{12,... | collective-permute-start | bytes 196616 | tf_op jit(solution)/shard_map/ppermute | solution.py:626
  105.3 5.6 %collective-permute-start.23 = (f32[8,8,256]{2,1,0:T(8,128)S(1)}, f32[8,8,256]{2,1,0:T(8,128)S(1)}, u32[]{:S(2)}, u32[]{:S(2)}) collective-permute-start(f32[8,8,256]{2,1,0:T(8,128)S(1)} %get-tuple-element.126), channel_id=1, source_target_pairs={{1,2},{3,4},{5,6},{7,0},{2,1},{4,3},{6,5},{0,7},{9,10},{11,12},{13... | collective-permute-start | bytes 196616 | tf_op jit(solution)/shard_map/ppermute | solution.py:626
  (21 other events, 36.6 us)

commit v3 on v2

--- a/solution.py
+++ b/solution.py
@@ -17,6 +17,8 @@
 SLIP_RATE = 0.1
 HARDENING = 0.5
 LANES = 128
+WIDE = 256
+CHUNKS = 4
 BF16 = jnp.bfloat16
 F32 = jnp.float32
 
@@ -79,7 +81,7 @@
 
 
 def pack_state_kernel(
-    anchor, strain, stress, resist, active, out, values, flags, wide_mail, rest_mail, sems
+    anchor, strain, stress, resist, active, out, values, flags, wide_mail, rest_mail, mail, sems
 ):
     tensors, forces = strain.shape[0], resist.shape[0]
     copies = [
@@ -95,37 +97,50 @@
     slots_row = anchor[...]
     slot = lax.broadcasted_iota(jnp.int32, (slots_all, items), 0)
     hit = hit_rows(slots_row, slot)
-    row = lax.broadcasted_iota(jnp.int32, (slots_all // 2, items), 0)
-    lower = (row >> 2) * 8 + (row & 3)
-    sides = jnp.concatenate([hit_rows(slots_row, lower), hit_rows(slots_row, lower + 4)], axis=1)
     for copy in copies:
         copy.wait()
-    wide_mail[...] = into_slots(hit, values[: 2 * LANES])
     total = 2 * tensors + forces
     rest = jnp.concatenate(
         [values[2 * LANES : total], flags[...].astype(F32), jnp.zeros((8, items), F32)], axis=0
     )
-    empty = jnp.zeros_like(rest)
-    both = jnp.concatenate(
-        [jnp.concatenate([rest, empty], axis=1), jnp.concatenate([empty, rest], axis=1)], axis=0
-    )
-    rest_mail[...] = into_slots(sides, both)
+    rest = jnp.concatenate(two_terms(rest), axis=0)
+    wide = two_terms(values[: 2 * LANES])
     upper = lax.broadcasted_iota(jnp.int32, (8, LANES), 0) < 4
-    for pair in range(slots_all // 16):
-        start = 16 * pair
-        left = pltpu.roll(wide_mail[start + 8 : start + 16, :LANES], 4, 0)
-        right = pltpu.roll(wide_mail[start + 8 : start + 16, LANES:], 4, 0)
-        side = rest_mail[8 * pair : 8 * pair + 8]
-        out[40 * pair : 40 * pair + 8] = wide_mail[start : start + 8, :LANES]
-        out[40 * pair + 8 : 40 * pair + 16] = wide_mail[start : start + 8, LANES:]
-        out[40 * pair + 16 : 40 * pair + 24] = jnp.where(upper, side, left)
-        out[40 * pair + 24 : 40 * pair + 32] = jnp.where(upper, left, right)
-        out[40 * pair + 32 : 40 * pair + 40] = jnp.where(upper, right, side)
+    near = lax.broadcasted_iota(jnp.int32, (8, LANES), 1) < LANES // 2
+    part = slots_all // CHUNKS
+    sent = []
+    for chunk in range(CHUNKS):
+        rows = slice(chunk * part, (chunk + 1) * part)
+        wide_mail[rows] = product_rows(hit[rows], wide[0]) + product_rows(hit[rows], wide[1])
+        terms = product_rows(hit[rows], rest)
+        rest_mail[rows] = terms + pltpu.roll(terms, LANES // 2, 1)
+        for pair in range(chunk * part // 16, (chunk + 1) * part // 16):
+            start = 16 * pair
+            left = pltpu.roll(wide_mail[start + 8 : start + 16, :LANES], 4, 0)
+            right = pltpu.roll(wide_mail[start + 8 : start + 16, LANES:], 4, 0)
+            one, two = rest_mail[start : start + 8], rest_mail[start + 8 : start + 16]
+            side = jnp.where(
+                upper,
+                jnp.where(near, one, pltpu.roll(one, 4, 0)),
+                jnp.where(near, pltpu.roll(two, 4, 0), two),
+            )
+            mail[40 * pair : 40 * pair + 8] = wide_mail[start : start + 8, :LANES]
+            mail[40 * pair + 8 : 40 * pair + 16] = wide_mail[start : start + 8, LANES:]
+            mail[40 * pair + 16 : 40 * pair + 24] = jnp.where(upper, side, left)
+            mail[40 * pair + 24 : 40 * pair + 32] = jnp.where(upper, left, right)
+            mail[40 * pair + 32 : 40 * pair + 40] = jnp.where(upper, right, side)
+        rows = slice(chunk * part * 5 // 2, (chunk + 1) * part * 5 // 2)
+        sent.append(pltpu.make_async_copy(mail.at[rows], out.at[rows], sems.at[4 + chunk]))
+        sent[-1].start()
+    for copy in sent:
+        copy.wait()
 
 
 def unpack_state_kernel(
-    mailbox, mail, strain, stress, resist, active, wide_mail, rest_mail
+    mailbox, mail, strain, stress, resist, active, wide_mail, rest_mail, slots_row, sem
 ):
+    fetch = pltpu.make_async_copy(mailbox, slots_row, sem)
+    fetch.start()
     slots_all = wide_mail.shape[0]
     upper = lax.broadcasted_iota(jnp.int32, (8, LANES), 0) < 4
     for pair in range(slots_all // 16):
@@ -142,10 +157,15 @@
             jnp.where(upper, fifth, fourth), 4, 0
         )
         rest_mail[8 * pair : 8 * pair + 8] = jnp.where(upper, third, fifth)
-    slots = mailbox[...]
-    wide = out_of_slots(hit_columns(slots, slots_all), wide_mail[...])
+    wide_terms, rest_terms = two_terms(wide_mail[...]), two_terms(rest_mail[...])
+    fetch.wait()
+    slots = column_of(slots_row[...])
+    hit = hit_columns(slots, slots_all)
+    wide = product(hit, wide_terms[0]) + product(hit, wide_terms[1])
     row = (slots >> 3) * 4 + (slots & 3)
-    rest = out_of_slots(hit_columns(row, slots_all // 2), rest_mail[...])
+    hit = hit_columns(row, slots_all // 2)
+    rest = product(hit, jnp.concatenate(rest_terms, axis=1))
+    rest = rest[:, :LANES] + rest[:, LANES:]
     rest = jnp.where((slots & 4) > 0, pltpu.roll(rest, LANES // 2, 1), rest)
     values = jnp.transpose(jnp.concatenate([wide, rest], axis=1))
     start = 0
@@ -154,7 +174,7 @@
         start += part.shape[0]
 
 
-def pack_result_kernel(mailbox, stress, resist, out):
+def pack_result_kernel(mailbox, stress, resist, out, mail, sems):
     rows = stress.shape[0] + resist.shape[0]
     values = jnp.concatenate(
         [
@@ -164,12 +184,23 @@
         ],
         axis=0,
     )
-    slot = lax.broadcasted_iota(jnp.int32, (out.shape[0], values.shape[1]), 0)
-    out[...] = into_slots(hit_rows(mailbox[...], slot), values)
+    high, low = two_terms(values)
+    part = out.shape[0] // CHUNKS
+    slot = lax.broadcasted_iota(jnp.int32, (part, values.shape[1]), 0)
+    sent = []
+    for chunk in range(CHUNKS):
+        rows = slice(chunk * part, (chunk + 1) * part)
+        hit = hit_rows(mailbox[...] - chunk * part, slot)
+        mail[rows] = product_rows(hit, high) + product_rows(hit, low)
+        sent.append(pltpu.make_async_copy(mail.at[rows], out.at[rows], sems.at[chunk]))
+        sent[-1].start()
+    for copy in sent:
+        copy.wait()
 
 
 def unpack_result_kernel(anchor, mail, stress, resist):
-    values = jnp.transpose(out_of_slots(hit_columns(anchor[...], mail.shape[0]), mail[...]))
+    hit = hit_columns(column_of(anchor[...]), mail.shape[0])
+    values = jnp.transpose(out_of_slots(hit, mail[...]))
     stress[...] = values[: stress.shape[0]]
     resist[...] = values[stress.shape[0] : stress.shape[0] + resist.shape[0]]
 
@@ -205,7 +236,7 @@
 
 
 def lane_map():
-    index, to = grid_of(1024, 256)
+    index, to = grid_of(512, 256)
     y = field(index, 0, 8)
     return marked(
         ((y >> 2) == field(to, 0, 6))
@@ -215,7 +246,7 @@
 
 
 def spread_map():
-    index, y = grid_of(512, 256)
+    index, y = grid_of(256, 256)
     return marked(((y >> 2) == field(index, 0, 6)) & (field(y, 1, 1) == field(index, 7, 1)))
 
 
@@ -251,12 +282,10 @@
 
 def prepare_kernel(
     owner,
-    anchor,
     schmid,
     latent,
+    places,
     mailbox_row,
-    mailbox_col,
-    anchor_col,
     tensor_map,
     harden_map,
     active_map,
@@ -264,7 +293,9 @@
     lanes,
     repeat,
     spread,
+    table,
 ):
+    table[...] = jnp.broadcast_to(places[...], table.shape)
     owners = jnp.concatenate(
         [owner[i, j : j + 1] for i in range(owner.shape[0]) for j in range(owner.shape[1])],
         axis=1,
@@ -277,8 +308,6 @@
     rank = jnp.sum(before * onehot, axis=0, keepdims=True).astype(jnp.int32)
     mailbox = owners * 8 + rank
     mailbox_row[...] = mailbox
-    mailbox_col[...] = column_of(mailbox)
-    anchor_col[...] = column_of(anchor[...])
     tensor_map[...] = over_points(schmid[...])
     harden_map[...] = over_points(latent[...])
     to, index = grid_of(active_map.shape[0], active_map.shape[1])
@@ -291,7 +320,7 @@
 
 def restrict_kernel(grains, rows, lanes, weights):
     orders, size_x, size_z, size_y = grains.shape
-    lefts = []
+    lefts = ([], [])
     for pair in range(orders // 2):
         parts = []
         for order in (2 * pair, 2 * pair + 1):
@@ -301,11 +330,10 @@
                 parts.append(low * low + high * high)
         summed = jnp.concatenate(parts, axis=0)
         moved = product(rows[...], jnp.concatenate(two_terms(summed), axis=0))
-        high, low = two_terms(moved)
-        lefts.append(
-            jnp.concatenate([high[:64], high[64:], low[:64], low[64:]], axis=1)
-        )
-    found = product(jnp.concatenate(lefts, axis=0), lanes[...])
+        for left, part in zip(lefts, two_terms(moved)):
+            left.append(jnp.concatenate([part[:64], part[64:]], axis=1))
+    found = product(jnp.concatenate(lefts[0], axis=0), lanes[...])
+    found = found + product(jnp.concatenate(lefts[1], axis=0), lanes[...])
     row = lax.broadcasted_iota(jnp.int32, (found.shape[0], LANES), 0)
     picked = jnp.where(row % 2 == 0, found[:, :LANES], found[:, LANES:])
     for order in range(orders):
@@ -329,8 +357,8 @@
         )
         for t in range(4)
     ]
-    left = jnp.concatenate(two_terms(jnp.concatenate(tiles, axis=0)), axis=1)
-    cells = product(left, spread)
+    high, low = two_terms(jnp.concatenate(tiles, axis=0))
+    cells = product(high, spread) + product(low, spread)
     for bx in range(2):
         for pair in range(2):
             for qx in range(2):
@@ -364,7 +392,7 @@
     rates[...] = product(active_map[...], active[...].astype(BF16)) * SLIP_RATE
 
     def tile_step(tile, carry):
-        lanes = pl.ds(pl.multiple_of(tile * LANES, LANES), LANES)
+        lanes = pl.ds(pl.multiple_of(tile * WIDE, WIDE), WIDE)
         trial = [
             stress[points * c : points * (c + 1), lanes]
             + 2.0 * strain[points * c : points * (c + 1), lanes]
@@ -372,7 +400,7 @@
         ]
 
         def sweep(_, now):
-            sums = [jnp.zeros((points, LANES), F32) for _ in range(6)]
+            sums = [jnp.zeros((points, WIDE), F32) for _ in range(6)]
             for a in range(systems):
                 rows = pl.ds(a * points, points)
                 parts = [tensor[pl.ds((a * 6 + c) * points, points), lanes] for c in range(6)]
@@ -391,7 +419,7 @@
             stress_out[points * c : points * (c + 1), lanes] = now[c]
         return carry
 
-    lax.fori_loop(0, items // LANES, tile_step, 0)
+    lax.fori_loop(0, items // WIDE, tile_step, 0)
     amount = amounts[...]
     high, low = two_terms(amount)
     harden = product(harden_map[...], jnp.concatenate([high, low, high], axis=0))
@@ -405,10 +433,24 @@
 
 
 def own_and_other(odd, even_value, odd_value):
-    return jnp.where(odd > 0, odd_value, even_value)
-
-
-def new_layer(grains, x, lower, upper, z_pair, z_other, energy, odd_z, mobility, grain_state):
+    return jnp.where(odd > 0.0, odd_value, even_value)
+
+
+def odd_x_of(table):
+    return table[16:17]
+
+
+def odd_z_of(table):
+    return table[17:18]
+
+
+def z_rows(table, order, x, z_pair, z_other):
+    odd_z = odd_z_of(table)
+    mate, other = z_pair[order, x : x + 1], z_other[order, x : x + 1]
+    return own_and_other(odd_z, other, mate), own_and_other(odd_z, mate, other)
+
+
+def new_layer(grains, x, lower, upper, z_pair, z_other, energy, table):
     orders, _, size_z, size_y = grains.shape
     row = lax.broadcasted_iota(jnp.int32, (size_z, size_y), 0)
     center = [grains[order, x] for order in range(orders)]
@@ -421,21 +463,18 @@
     found = []
     for order in range(orders):
         value = center[order]
-        z_mate, z_next = z_pair[order, x : x + 1], z_other[order, x : x + 1]
-        below = jnp.where(row == 0, own_and_other(odd_z, z_next, z_mate), pltpu.roll(value, 1, 0))
-        above = jnp.where(
-            row == size_z - 1,
-            own_and_other(odd_z, z_mate, z_next),
-            pltpu.roll(value, size_z - 1, 0),
-        )
+        first, last = 0.0, 0.0
+        if z_pair is not None:
+            first, last = z_rows(table, order, x, z_pair, z_other)
+        below = jnp.where(row == 0, first, pltpu.roll(value, 1, 0))
+        above = jnp.where(row == size_z - 1, last, pltpu.roll(value, size_z - 1, 0))
         around = (
             (lower(order) + upper(order))
             + (below + above)
             + (pltpu.roll(value, 1, 1) + pltpu.roll(value, size_y - 1, 1))
         )
-        share = 2.0 * DRIVE_SCALE * (1.0 - grain_state[order])
-        factor = shared + share * cell - 2.0 * squares[order]
-        found.append(value + (TIME_STEP * mobility[order]) * (around - value * factor))
+        factor = shared + table[8 + order : 9 + order] * cell - 2.0 * squares[order]
+        found.append(value + table[order : order + 1] * (around - value * factor))
     return found
 
 
@@ -480,34 +519,32 @@
     z_other[order, x : x + 1] = own_and_other(odd_z, first, last)
 
 
-def edges_kernel(grains, odd, x_pair, x_other, z_pair, z_other):
+def edges_kernel(grains, table, x_pair, x_other, z_pair, z_other):
     orders, size_x, _, _ = grains.shape
     for order in range(orders):
         send_layers(
-            odd[0], order, grains[order, 0], grains[order, size_x - 1], x_pair, x_other
+            odd_x_of(table), order, grains[order, 0], grains[order, size_x - 1], x_pair, x_other
         )
         for x in range(size_x):
-            send_rows(odd[1], order, x, grains[order, x], z_pair, z_other)
-
-
-def first_ends_kernel(
+            send_rows(odd_z_of(table), order, x, grains[order, x], z_pair, z_other)
+
+
+def ends_kernel(
     grains,
     x_pair,
     x_other,
     z_pair,
     z_other,
     energy,
-    odd,
-    mobility,
-    grain_state,
+    table,
     x_pair_out,
     x_other_out,
 ):
     low, high = new_ends(
-        grains, x_pair, x_other, odd[0], z_pair, z_other, energy, odd[1], mobility, grain_state
+        grains, x_pair, x_other, odd_x_of(table), z_pair, z_other, energy, table
     )
     for order in range(grains.shape[0]):
-        send_layers(odd[0], order, low[order], high[order], x_pair_out, x_other_out)
+        send_layers(odd_x_of(table), order, low[order], high[order], x_pair_out, x_other_out)
 
 
 def first_inner_kernel(
@@ -517,102 +554,84 @@
     energy,
     x_pair_new,
     x_other_new,
-    odd,
-    mobility,
-    grain_state,
+    table,
     out,
     z_pair_out,
     z_other_out,
 ):
     orders, size_x, _, _ = grains.shape
     for order in range(orders):
-        low = own_and_other(odd[0], x_other_new[order], x_pair_new[order])
-        high = own_and_other(odd[0], x_pair_new[order], x_other_new[order])
+        low = own_and_other(odd_x_of(table), x_other_new[order], x_pair_new[order])
+        high = own_and_other(odd_x_of(table), x_pair_new[order], x_other_new[order])
         for x, new in ((0, low), (size_x - 1, high)):
             out[order, x] = new
-            send_rows(odd[1], order, x, new, z_pair_out, z_other_out)
+            send_rows(odd_z_of(table), order, x, new, z_pair_out, z_other_out)
     for x in range(1, size_x - 1):
-        found = new_inner(grains, x, z_pair, z_other, energy, odd[1], mobility, grain_state)
+        found = new_inner(grains, x, z_pair, z_other, energy, table)
         for order in range(orders):
             out[order, x] = found[order]
-            send_rows(odd[1], order, x, found[order], z_pair_out, z_other_out)
-
-
-def second_inner_kernel(grains, z_pair, z_other, energy, odd, mobility, grain_state, out):
+            send_rows(odd_z_of(table), order, x, found[order], z_pair_out, z_other_out)
+
+
+def second_inner_kernel(grains, energy, table, out):
     orders, size_x, _, _ = grains.shape
     for x in range(1, size_x - 1):
-        found = new_inner(grains, x, z_pair, z_other, energy, odd[1], mobility, grain_state)
+        found = new_inner(grains, x, None, None, energy, table)
         for order in range(orders):
             out[order, x] = found[order]
 
 
-def second_ends_kernel(
-    grains,
-    x_pair,
-    x_other,
-    z_pair,
-    z_other,
-    energy,
-    inner,
-    odd,
-    mobility,
-    grain_state,
-    out,
-    x_pair_out,
-    x_other_out,
-    z_pair_out,
-    z_other_out,
+def end_rows(inner, order, x, z_pair, z_other, table):
+    size_z = inner.shape[2]
+    first, last = z_rows(table, order, x, z_pair, z_other)
+    step = table[order : order + 1]
+    return (
+        inner[order, x, :1] + step * first,
+        inner[order, x, size_z - 1 :] + step * last,
+    )
+
+
+def second_rows_kernel(
+    inner, x_pair_new, x_other_new, z_pair, z_other, table, out, z_pair_out, z_other_out
 ):
-    orders, size_x, _, _ = grains.shape
-    low, high = new_ends(
-        grains, x_pair, x_other, odd[0], z_pair, z_other, energy, odd[1], mobility, grain_state
-    )
+    orders, size_x, size_z, _ = inner.shape
+    odd_x, odd_z = odd_x_of(table), odd_z_of(table)
     for order in range(orders):
-        send_layers(odd[0], order, low[order], high[order], x_pair_out, x_other_out)
-        for x, new in ((0, low[order]), (size_x - 1, high[order])):
+        low = own_and_other(odd_x, x_other_new[order], x_pair_new[order])
+        high = own_and_other(odd_x, x_pair_new[order], x_other_new[order])
+        for x, new in ((0, low), (size_x - 1, high)):
             out[order, x] = new
-            send_rows(odd[1], order, x, new, z_pair_out, z_other_out)
+            send_rows(odd_z, order, x, new, z_pair_out, z_other_out)
         for x in range(1, size_x - 1):
-            send_rows(odd[1], order, x, inner[order, x], z_pair_out, z_other_out)
-
-
-def last_inner_kernel(
-    grains, z_pair, z_other, energy, odd, mobility, grain_state, out, held, sems
+            first, last = end_rows(inner, order, x, z_pair, z_other, table)
+            out[order, x, :1] = first
+            out[order, x, size_z - 1 :] = last
+            z_pair_out[order, x : x + 1] = own_and_other(odd_z, last, first)
+            z_other_out[order, x : x + 1] = own_and_other(odd_z, first, last)
+
+
+def last_rows_kernel(inner, z_pair, z_other, table, out, held, sem):
+    orders, size_x, size_z, _ = inner.shape
+    for order in range(orders):
+        for x in range(1, size_x - 1):
+            first, last = end_rows(inner, order, x, z_pair, z_other, table)
+            held[order, x] = inner[order, x]
+            held[order, x, :1] = first
+            held[order, x, size_z - 1 :] = last
+    inside = (slice(None), slice(1, size_x - 1))
+    copy = pltpu.make_async_copy(held.at[inside], out.at[inside], sem)
+    copy.start()
+    copy.wait()
+
+
+def last_ends_kernel(
+    grains, x_pair, x_other, z_pair, z_other, energy, table, inner, out, held, sems
 ):
-    orders, size_x, _, _ = grains.shape
-    copies = []
-    for x in range(1, size_x - 1):
-        found = new_inner(grains, x, z_pair, z_other, energy, odd[1], mobility, grain_state)
-        for order in range(orders):
-            held[x - 1, order] = found[order]
-        copies.append(pltpu.make_async_copy(held.at[x - 1], out.at[:, x], sems.at[x - 1]))
-        copies[-1].start()
-    for copy in copies:
-        copy.wait()
-
-
-def last_ends_kernel(
-    grains,
-    x_pair,
-    x_other,
-    z_pair,
-    z_other,
-    energy,
-    inner,
-    odd,
-    mobility,
-    grain_state,
-    out,
-    held,
-    sems,
-):
-    orders, size_x, _, _ = grains.shape
-    ends = new_ends(
-        grains, x_pair, x_other, odd[0], z_pair, z_other, energy, odd[1], mobility, grain_state
-    )
+    size_x = grains.shape[1]
+    ends = new_ends(grains, x_pair, x_other, odd_x_of(table), z_pair, z_other, energy, table)
     copies = []
     for side, x in ((0, 0), (1, size_x - 1)):
-        for order in range(orders):
+        for order in range(grains.shape[0]):
             held[side, order] = ends[side][order]
         copies.append(pltpu.make_async_copy(held.at[side], out.at[:, x], sems.at[side]))
         copies[-1].start()
@@ -627,12 +646,11 @@
 
 
 def halos(edges):
-    return (
-        swapped(edges[0], "gx", 0),
-        swapped(edges[1], "gx", 1),
-        swapped(edges[2], "gz", 0),
-        swapped(edges[3], "gz", 1),
-    )
+    x_other = swapped(edges[1], "gx", 1)
+    z_other = swapped(edges[3], "gz", 1)
+    x_pair = swapped(edges[0], "gx", 0)
+    z_pair = swapped(edges[2], "gz", 0)
+    return x_pair, x_other, z_pair, z_other
 
 
 def shards(
@@ -656,7 +674,6 @@
     systems = resistance.shape[0]
     tensors, forces = 6 * points, systems * points
     narrow = -(-(tensors + forces) // LANES) * LANES
-    scalars = pl.BlockSpec(memory_space=pltpu.SMEM)
     whole = pl.BlockSpec(memory_space=pltpu.VMEM)
     far = pl.BlockSpec(memory_space=pltpu.HBM)
     anchor = element_anchor.reshape(1, per_dev)
@@ -670,10 +687,12 @@
             pltpu.VMEM((2 * tensors + forces, per_dev), F32),
             pltpu.VMEM((systems, per_dev), jnp.int32),
             pltpu.VMEM((slots_all, 2 * LANES), F32),
-            pltpu.VMEM((slots_all // 2, LANES), F32),
-            pltpu.SemaphoreType.DMA((4,)),
+            pltpu.VMEM((slots_all, LANES), F32),
+            pltpu.VMEM((message, LANES), F32),
+            pltpu.SemaphoreType.DMA((4 + CHUNKS,)),
         ),
         in_specs=[whole, far, far, far, far],
+        out_specs=far,
     )(
         anchor,
         strain_step.reshape(tensors, per_dev),
@@ -683,12 +702,18 @@
     )
     inbox = exchanged(outbox.reshape(count_all, 5, 4, LANES)).reshape(message, LANES)
 
+    places = jnp.concatenate(
+        [
+            TIME_STEP * mobility,
+            2.0 * DRIVE_SCALE * (1.0 - grain_state),
+            jnp.stack([lax.axis_index(name) % 2 for name in ("gx", "gz")]).astype(F32),
+            jnp.zeros((6,), F32),
+        ]
+    ).reshape(24, 1)
     whole_number = functools.partial(jax.ShapeDtypeStruct, dtype=jnp.int32)
     half_wide = functools.partial(jax.ShapeDtypeStruct, dtype=BF16)
     (
         mailbox_row,
-        mailbox_col,
-        anchor_col,
         tensor_map,
         harden_map,
         active_map,
@@ -696,35 +721,34 @@
         lanes,
         repeat,
         spread,
+        table,
     ) = call(
         prepare_kernel,
         (
             whole_number((1, per_dev)),
-            whole_number((per_dev, LANES)),
-            whole_number((per_dev, LANES)),
             half_wide((6 * forces, 3 * orders * points)),
             half_wide((forces, 3 * forces)),
             half_wide((forces, systems)),
             half_wide((128, 256)),
-            half_wide((1024, 256)),
+            half_wide((512, 256)),
             half_wide((32, 16)),
-            half_wide((512, 256)),
+            half_wide((256, 256)),
+            shape(24, size_y),
         ),
         limit=12,
     )(
         block_owner,
-        anchor,
         orientation_schmid.reshape(orders, systems * 6).T,
         latent_hardening,
-    )
-    odd = jnp.stack([lax.axis_index("gx") % 2, lax.axis_index("gz") % 2]).astype(jnp.int32)
+        places,
+    )
     edge_shapes = (
         shape(orders, size_z, size_y),
         shape(orders, size_z, size_y),
         shape(orders, size_x, size_y),
         shape(orders, size_x, size_y),
     )
-    edges = call(edges_kernel, edge_shapes, limit=4, in_specs=[whole, scalars])(grains, odd)
+    edges = call(edges_kernel, edge_shapes, limit=4, in_specs=[whole] * 2)(grains, table)
     strain_h = stress_h = resist_h = active_h = None
     for cycle in range(STEPS):
         around = halos(edges)
@@ -741,11 +765,14 @@
                     shape(systems, per_dev),
                 ),
                 limit=16,
+                in_specs=[far, whole],
                 scratch=(
                     pltpu.VMEM((slots_all, 2 * LANES), F32),
                     pltpu.VMEM((slots_all // 2, LANES), F32),
+                    pltpu.VMEM((1, per_dev), jnp.int32),
+                    pltpu.SemaphoreType.DMA,
                 ),
-            )(mailbox_col, inbox)
+            )(mailbox_row, inbox)
         stress_h, resist_h, energy = call(
             mechanics_kernel,
             (
@@ -774,61 +801,73 @@
         if cycle == STEPS - 1:
             around, stress_h = lax.optimization_barrier((around, stress_h))
         brick = shape(orders, size_x, size_z, size_y)
-        tables = (odd, mobility, grain_state)
         x_pair, x_other = call(
-            first_ends_kernel, edge_shapes[:2], limit=4, in_specs=[whole] * 6 + [scalars] * 3
-        )(grains, *around, energy, *tables)
+            ends_kernel, edge_shapes[:2], limit=4, in_specs=[whole] * 7
+        )(grains, *around, energy, table)
         grains, z_pair, z_other = call(
             first_inner_kernel,
             (brick,) + edge_shapes[2:],
             limit=4,
-            in_specs=[whole] * 6 + [scalars] * 3,
-        )(grains, *around[2:], energy, x_pair, x_other, *tables)
+            in_specs=[whole] * 7,
+        )(grains, *around[2:], energy, x_pair, x_other, table)
         around = halos((x_pair, x_other, z_pair, z_other))
+        inner = call(
+            second_inner_kernel,
+            brick,
+            limit=4,
+            in_specs=[whole] * 3,
+            out_specs=whole,
+        )(grains, energy, table)
         if cycle < STEPS - 1:
-            inner = call(
-                second_inner_kernel, brick, limit=4, in_specs=[whole] * 4 + [scalars] * 3
-            )(grains, *around[2:], energy, *tables)
-            grains, *edges = call(
-                second_ends_kernel,
-                (brick,) + edge_shapes,
+            x_pair, x_other = call(
+                ends_kernel, edge_shapes[:2], limit=4, in_specs=[whole] * 7
+            )(grains, *around, energy, table)
+            grains, z_pair, z_other = call(
+                second_rows_kernel,
+                (brick,) + edge_shapes[2:],
                 limit=4,
-                in_specs=[whole] * 7 + [scalars] * 3,
-                input_output_aliases={6: 0},
-            )(grains, *around, energy, inner, *tables)
-        else:
-            inner = call(
-                last_inner_kernel,
-                brick,
-                limit=6,
-                in_specs=[whole] * 4 + [scalars] * 3,
-                out_specs=far,
-                scratch=(
-                    pltpu.VMEM((size_x - 2, orders, size_z, size_y), F32),
-                    pltpu.SemaphoreType.DMA((size_x - 2,)),
-                ),
-            )(grains, *around[2:], energy, *tables)
-            last = (grains, *around, energy, inner, *tables)
-    outbox = call(pack_result_kernel, shape(slots_all, narrow), limit=12)(
+                in_specs=[whole] * 6,
+                out_specs=[whole] * 3,
+                input_output_aliases={0: 0},
+            )(inner, x_pair, x_other, *around[2:], table)
+            edges = (x_pair, x_other, z_pair, z_other)
+    outbox = call(
+        pack_result_kernel,
+        shape(slots_all, narrow),
+        limit=12,
+        out_specs=far,
+        scratch=(pltpu.VMEM((slots_all, narrow), F32), pltpu.SemaphoreType.DMA((CHUNKS,))),
+    )(
         mailbox_row, stress_h, resist_h
     )
     inbox = exchanged(outbox.reshape(count_all, slots_all // count_all, narrow))
-    stress, resistance = call(
-        unpack_result_kernel, (shape(tensors, per_dev), shape(forces, per_dev)), limit=12
-    )(anchor_col, inbox.reshape(slots_all, narrow))
-    last, stress, resistance = lax.optimization_barrier((last, stress, resistance))
+    inside = call(
+        last_rows_kernel,
+        brick,
+        limit=4,
+        in_specs=[whole] * 4,
+        out_specs=far,
+        scratch=(
+            pltpu.VMEM((orders, size_x, size_z, size_y), F32),
+            pltpu.SemaphoreType.DMA,
+        ),
+    )(inner, *around[2:], table)
     grains = call(
         last_ends_kernel,
         brick,
         limit=4,
-        in_specs=[whole] * 6 + [far] + [scalars] * 3,
+        in_specs=[whole] * 7 + [far],
         out_specs=far,
         scratch=(
             pltpu.VMEM((2, orders, size_z, size_y), F32),
             pltpu.SemaphoreType.DMA((2,)),
         ),
-        input_output_aliases={6: 0},
-    )(*last)
+        input_output_aliases={7: 0},
+    )(grains, *around, energy, table, inside)
+    grains, inbox = lax.optimization_barrier((grains, inbox))
+    stress, resistance = call(
+        unpack_result_kernel, (shape(tensors, per_dev), shape(forces, per_dev)), limit=12
+    )(anchor, inbox.reshape(slots_all, narrow))
     return (
         grains,
         stress.reshape(6, points, per_dev),

time: 119 us -> 112 us (0.941)
  Pallas kernels: 39.5 us -> 29.8 us
  waiting for transfers between devices: 18.7 us -> 27.3 us
  local copies, waits for them, and re-layouts: 10.4 us -> 5.84 us
    ppermute x24, waiting for transfers between devices: 12.7 us -> 20.3 us  [swapped(): return lax.ppermute(value, axis, pairs + [(j, i) for i, j in pairs])]
    pallas_call x12 -> x15, Pallas kernels: 15.8 us -> 9.92 us  [the longest x5 2.31 us: shards(): call(ends_kernel, edge_shapes[:2], limit=4, in_specs=[whole] * 7)]
    unnamed x54 -> x34, local copies, waits for them, and re-layouts: 9.65 us -> 4.41 us
    pallas_call x3, Pallas kernels: 10.4 us -> 8.59 us  [shards(): call(mechanics_kernel, (shape(tensors, per_dev), shape(forces, per_dev),...]
    pallas_call x3, Pallas kernels: 4.83 us -> 3.2 us  [shards(): call(first_inner_kernel, (brick,) + edge_shapes[2:], limit=4, in_specs=[w...]
  transfers between devices with their start and end apart: 26 -> 26, of which waited for: 8 -> 10; matrix products, arithmetic and copies ran while one was open for 1% -> 1% of each run, Pallas kernels for 23% -> 19%
where the time goes in v3:
time: 112 us
  starting transfers between devices  47.6 us (42%)
  Pallas kernels  29.8 us (27%)
  waiting for transfers between devices  27.3 us (24%)
  local copies, waits for them, and re-layouts  5.84 us (5%)
    ppermute x24, starting transfers between devices, swapped(): return lax.ppermute(value, axis, pairs + [(j, i) for i, j in pairs])  31.2 us
    ppermute x24, waiting for transfers between devices, swapped(): return lax.ppermute(value, axis, pairs + [(j, i) for i, j in pairs])  20.3 us
    all_to_all x2, starting transfers between devices, exchanged(): lax.all_to_all(sent, ('gx', 'gz'), split_axis=0, concat_axis=0, tiled=True)  16.4 us
    pallas_call x3, Pallas kernels, shards(): call(mechanics_kernel, (shape(tensors, per_dev), shape(forces, per_dev),...  8.59 us
    all_to_all x2, waiting for transfers between devices, exchanged(): lax.all_to_all(sent, ('gx', 'gz'), split_axis=0, concat_axis=0, tiled=True)  7.02 us
    unnamed x34, local copies, waits for them, and re-layouts  4.41 us
    pallas_call x1, Pallas kernels, shards(): call(pack_state_kernel, shape(message, LANES), limit=None, scratch=(pltpu...  3.6 us
    pallas_call x3, Pallas kernels, shards(): call(first_inner_kernel, (brick,) + edge_shapes[2:], limit=4, in_specs=[w...  3.2 us
  transfers between devices with their start and end apart: 26, of which 10 were waited for; matrix products, arithmetic and copies ran while one was open for 1% of the time, Pallas kernels for 19%

profile of v3, /device:TPU:0, one launch (start us, length us, event | category | flops | bytes accessed | tf_op | source)
XLA Modules:
  0.0 111.8 jit_solution(707063345727111748)
XLA Ops:
  0.6 3.6 %shard_map.133 = f32[2560,128]{1,0:T(8,128)} custom-call(s32[1,512]{1,0:T(1,128)} %bitcast.20, f32[48,512]{1,0:T(8,128)} %bitcast.24, f32[48,512]{1,0:T(8,128)} %bitcast.25, f32[192,512]{1,0:T(8,128)} %bitcast.23, s32[24,512]{1,0:T(8,128)} %active.1), custom_call_target="tpu_custom_call" | custom-call | tf_op jit(solution)/shard_map/pallas_call | solution.py:682
  4.3 11.2 %all-to-all-start = ((f32[128,5,4,128]{3,2,1,0:T(4,128)}), f32[128,5,4,128]{3,2,1,0:T(4,128)S(1)}, u32[]{:S(2)}, u32[]{:S(2)}) async-start(f32[128,5,4,128]{3,2,1,0:T(4,128)} %bitcast.22), calls=%async_computation | async-start | bytes 2621440 | tf_op jit(solution)/shard_map/all_to_all | solution.py:209
  20.1 0.9 shard_map.130
  21.9 1.1 collective-permute-start.2
  23.0 4.5 %collective-permute-start.3 = (f32[8,16,256]{2,1,0:T(8,128)}, f32[8,16,256]{2,1,0:T(8,128)}, u32[]{:S(2)}, u32[]{:S(2)}) collective-permute-start(f32[8,16,256]{2,1,0:T(8,128)} %get-tuple-element.80), channel_id=1, source_target_pairs={{8,16},{24,32},{40,48},{56,64},{72,80},{88,96},{104,112},{120,0},{... | collective-permute-start | bytes 393224 | tf_op jit(solution)/shard_map/ppermute | solution.py:645
  27.5 3.0 %collective-permute-start.1 = (f32[8,8,256]{2,1,0:T(8,128)}, f32[8,8,256]{2,1,0:T(8,128)}, u32[]{:S(2)}, u32[]{:S(2)}) collective-permute-start(f32[8,8,256]{2,1,0:T(8,128)} %get-tuple-element.65), channel_id=1, source_target_pairs={{1,2},{3,4},{5,6},{7,0},{2,1},{4,3},{6,5},{0,7},{9,10},{11,12},{13... | collective-permute-start | bytes 196616 | tf_op jit(solution)/shard_map/ppermute | solution.py:645
  31.6 7.0 %all-to-all-done = f32[128,5,4,128]{3,2,1,0:T(4,128)S(1)} async-done(((f32[128,5,4,128]{3,2,1,0:T(4,128)}), f32[128,5,4,128]{3,2,1,0:T(4,128)S(1)}, u32[]{:S(2)}, u32[]{:S(2)}) %all-to-all-start) | async-done | bytes 1310752 | tf_op jit(solution)/shard_map/all_to_all | solution.py:209
  39.4 1.6 %shard_map.134 = (f32[48,512]{1,0:T(8,128)S(1)}, f32[48,512]{1,0:T(8,128)S(1)}, f32[192,512]{1,0:T(8,128)S(1)}, f32[24,512]{1,0:T(8,128)S(1)}) custom-call(s32[1,512]{1,0:T(1,128)S(1)} %copy-done.12, f32[2560,128]{1,0:T(8,128)S(1)} %bitcast.17), custom_call_target="tpu_custom_call" | custom-call | tf_op jit(solution)/shard_map/pallas_call | solution.py:759
  41.0 2.9 %shard_map.135 = (f32[48,512]{1,0:T(8,128)S(1)}, f32[192,512]{1,0:T(8,128)S(1)}, f32[4,16,256]{2,1,0:T(8,128)S(1)}) custom-call(f32[64,512]{1,0:T(8,128)S(1)} %copy-done.4, f32[48,512]{1,0:T(8,128)S(1)} %get-tuple-element.69.strain, f32[48,512]{1,0:T(8,128)S(1)} %get-tuple-element.70.stress, f32[192,512]{1,0:T(8,128)S(1)} %get-tuple-element.71.resist, ...), custom_call_target="tpu_custom_call" | custom-call | tf_op jit(solution)/shard_map/pallas_call | solution.py:776
  43.9 1.2 %shard_map.136 = (f32[8,16,256]{2,1,0:T(8,128)S(1)}, f32[8,16,256]{2,1,0:T(8,128)S(1)}) custom-call(f32[8,8,16,256]{3,2,1,0:T(8,128)S(1)} %copy-done, f32[8,16,256]{2,1,0:T(8,128)} %collective-permute-done.2.x_pair, f32[8,16,256]{2,1,0:T(8,128)} %collective-permute-done.3.x_other, f32[8,8,256]{2,1,0:T(8,128)} %collective-permute-done.z_pair, ...), custom_call_target="tpu_custom_call" | custom-call | tf_op jit(solution)/shard_map/pallas_call | solution.py:804
  46.0 1.6 %shard_map.137 = (f32[8,8,16,256]{3,2,1,0:T(8,128)S(1)}, f32[8,8,256]{2,1,0:T(8,128)S(1)}, f32[8,8,256]{2,1,0:T(8,128)S(1)}) custom-call(f32[8,8,16,256]{3,2,1,0:T(8,128)S(1)} %copy-done, f32[8,8,256]{2,1,0:T(8,128)} %collective-permute-done.z_pair, f32[8,8,256]{2,1,0:T(8,128)} %collective-permute-done.1.z_other, ...), custom_call_target="tpu_custom_call" | custom-call | tf_op jit(solution)/shard_map/pallas_call | solution.py:807
  47.7 1.3 %collective-permute-start.7 = (f32[8,8,256]{2,1,0:T(8,128)S(1)}, f32[8,8,256]{2,1,0:T(8,128)S(1)}, u32[]{:S(2)}, u32[]{:S(2)}) collective-permute-start(f32[8,8,256]{2,1,0:T(8,128)S(1)} %get-tuple-element.85), channel_id=1, source_target_pairs={{1,2},{3,4},{5,6},{7,0},{2,1},{4,3},{6,5},{0,7},{9,10},{11,12},{13... | collective-permute-start | bytes 196616 | tf_op jit(solution)/shard_map/ppermute | solution.py:645
  49.0 3.7 %collective-permute-done.7.z_other = f32[8,8,256]{2,1,0:T(8,128)S(1)} collective-permute-done((f32[8,8,256]{2,1,0:T(8,128)S(1)}, f32[8,8,256]{2,1,0:T(8,128)S(1)}, u32[]{:S(2)}, u32[]{:S(2)}) %collective-permute-start.7) | collective-permute-done | bytes 65568 | tf_op jit(solution)/shard_map/ppermute | solution.py:645
  52.7 0.9 collective-permute-done.5.x_other
  54.4 3.5 %collective-permute-start.11 = (f32[8,16,256]{2,1,0:T(8,128)S(1)}, f32[8,16,256]{2,1,0:T(8,128)S(1)}, u32[]{:S(2)}, u32[]{:S(2)}) collective-permute-start(f32[8,16,256]{2,1,0:T(8,128)S(1)} %get-tuple-element.87.x_other_new), channel_id=1, source_target_pairs={{8,16},{24,32},{40,48},{56,64},{72,80},{88,96},{104,112},{120,0},{... | collective-permute-start | bytes 393224 | tf_op jit(solution)/shard_map/ppermute | solution.py:645
  59.5 2.8 %shard_map.142 = (f32[48,512]{1,0:T(8,128)S(1)}, f32[192,512]{1,0:T(8,128)S(1)}, f32[4,16,256]{2,1,0:T(8,128)S(1)}) custom-call(f32[64,512]{1,0:T(8,128)S(1)} %shard_map.141.weights, f32[48,512]{1,0:T(8,128)S(1)} %get-tuple-element.69.strain, f32[48,512]{1,0:T(8,128)S(1)} %get-tuple-element.91.stress, f32[192,512]{1,0:T(8,128)S(1)} %get-tuple-element.92.resist, ...), custom_call_target="tpu_custom_call" | custom-call | tf_op jit(solution)/shard_map/pallas_call | solution.py:776
  62.4 1.6 %collective-permute-done.9.z_other = f32[8,8,256]{2,1,0:T(8,128)S(1)} collective-permute-done((f32[8,8,256]{2,1,0:T(8,128)S(1)}, f32[8,8,256]{2,1,0:T(8,128)S(1)}, u32[]{:S(2)}, u32[]{:S(2)}) %collective-permute-start.9) | collective-permute-done | bytes 65568 | tf_op jit(solution)/shard_map/ppermute | solution.py:645
  64.3 2.3 %collective-permute-start.13 = (f32[8,16,256]{2,1,0:T(8,128)S(1)}, f32[8,16,256]{2,1,0:T(8,128)S(1)}, u32[]{:S(2)}, u32[]{:S(2)}) collective-permute-start(f32[8,16,256]{2,1,0:T(8,128)S(1)} %get-tuple-element.95.x_other_new), channel_id=1, source_target_pairs={{8,16},{24,32},{40,48},{56,64},{72,80},{88,96},{104,112},{120,0},{... | collective-permute-start | bytes 393224 | tf_op jit(solution)/shard_map/ppermute | solution.py:645
  68.7 3.7 %collective-permute-done.15.z_other = f32[8,8,256]{2,1,0:T(8,128)S(1)} collective-permute-done((f32[8,8,256]{2,1,0:T(8,128)S(1)}, f32[8,8,256]{2,1,0:T(8,128)S(1)}, u32[]{:S(2)}, u32[]{:S(2)}) %collective-permute-start.15) | collective-permute-done | bytes 65568 | tf_op jit(solution)/shard_map/ppermute | solution.py:645
  73.1 3.0 %collective-permute-start.17 = (f32[8,16,256]{2,1,0:T(8,128)S(1)}, f32[8,16,256]{2,1,0:T(8,128)S(1)}, u32[]{:S(2)}, u32[]{:S(2)}) collective-permute-start(f32[8,16,256]{2,1,0:T(8,128)S(1)} %get-tuple-element.100.x_other_new), channel_id=1, source_target_pairs={{8,16},{24,32},{40,48},{56,64},{72,80},{88,96},{104,112},{120,0},{... | collective-permute-start | bytes 393224 | tf_op jit(solution)/shard_map/ppermute | solution.py:645
  77.0 0.9 collective-permute-start.19
  78.4 2.8 %shard_map.149 = (f32[48,512]{1,0:T(8,128)S(1)}, f32[192,512]{1,0:T(8,128)S(1)}, f32[4,16,256]{2,1,0:T(8,128)S(1)}) custom-call(f32[64,512]{1,0:T(8,128)S(1)} %shard_map.148.weights, f32[48,512]{1,0:T(8,128)S(1)} %get-tuple-element.69.strain, f32[48,512]{1,0:T(8,128)S(1)} %get-tuple-element.104.stress, f32[192,512]{1,0:T(8,128)S(1)} %get-tuple-element.105.resist, ...), custom_call_target="tpu_custom_call" | custom-call | tf_op jit(solution)/shard_map/pallas_call | solution.py:776
  82.0 1.6 %shard_map.155 = f32[1024,256]{1,0:T(8,128)} custom-call(s32[1,512]{1,0:T(1,128)S(1)} %copy-done.12, f32[48,512]{1,0:T(8,128)S(1)} %get-tuple-element.117.stress, f32[192,512]{1,0:T(8,128)S(1)} %get-tuple-element.118.resist), custom_call_target="tpu_custom_call" | custom-call | tf_op jit(solution)/shard_map/pallas_call | solution.py:834
  83.6 5.2 %all-to-all-start.1 = ((f32[128,8,256]{2,1,0:T(8,128)}), f32[128,8,256]{2,1,0:T(8,128)S(1)}, u32[]{:S(2)}, u32[]{:S(2)}) async-start(f32[128,8,256]{2,1,0:T(8,128)} %bitcast.10), calls=%async_computation.1 | async-start | bytes 2097152 | tf_op jit(solution)/shard_map/all_to_all | solution.py:209
  89.1 1.2 %collective-permute-start.20 = (f32[8,16,256]{2,1,0:T(8,128)S(1)}, f32[8,16,256]{2,1,0:T(8,128)S(1)}, u32[]{:S(2)}, u32[]{:S(2)}) collective-permute-start(f32[8,16,256]{2,1,0:T(8,128)S(1)} %get-tuple-element.112.x_pair_new), channel_id=1, source_target_pairs={{0,8},{16,24},{32,40},{48,56},{64,72},{80,88},{96,104},{112,120},{... | collective-permute-start | bytes 393224 | tf_op jit(solution)/shard_map/ppermute | solution.py:645
  90.2 4.5 %collective-permute-start.21 = (f32[8,16,256]{2,1,0:T(8,128)S(1)}, f32[8,16,256]{2,1,0:T(8,128)S(1)}, u32[]{:S(2)}, u32[]{:S(2)}) collective-permute-start(f32[8,16,256]{2,1,0:T(8,128)S(1)} %get-tuple-element.113.x_other_new), channel_id=1, source_target_pairs={{8,16},{24,32},{40,48},{56,64},{72,80},{88,96},{104,112},{120,0},{... | collective-permute-start | bytes 393224 | tf_op jit(solution)/shard_map/ppermute | solution.py:645
  95.6 3.0 %collective-permute-start.23 = (f32[8,8,256]{2,1,0:T(8,128)S(1)}, f32[8,8,256]{2,1,0:T(8,128)S(1)}, u32[]{:S(2)}, u32[]{:S(2)}) collective-permute-start(f32[8,8,256]{2,1,0:T(8,128)S(1)} %get-tuple-element.116), channel_id=1, source_target_pairs={{1,2},{3,4},{5,6},{7,0},{2,1},{4,3},{6,5},{0,7},{9,10},{11,12},{13... | collective-permute-start | bytes 196616 | tf_op jit(solution)/shard_map/ppermute | solution.py:645
  99.2 4.4 %collective-permute-done.23.z_other = f32[8,8,256]{2,1,0:T(8,128)S(1)} collective-permute-done((f32[8,8,256]{2,1,0:T(8,128)S(1)}, f32[8,8,256]{2,1,0:T(8,128)S(1)}, u32[]{:S(2)}, u32[]{:S(2)}) %collective-permute-start.23) | collective-permute-done | bytes 65568 | tf_op jit(solution)/shard_map/ppermute | solution.py:645
  103.6 1.0 shard_map.153.inner
  104.7 4.6 %collective-permute-done.21.x_other = f32[8,16,256]{2,1,0:T(8,128)S(1)} collective-permute-done((f32[8,16,256]{2,1,0:T(8,128)S(1)}, f32[8,16,256]{2,1,0:T(8,128)S(1)}, u32[]{:S(2)}, u32[]{:S(2)}) %collective-permute-start.21) | collective-permute-done | bytes 131104 | tf_op jit(solution)/shard_map/ppermute | solution.py:645
  109.3 0.9 shard_map.154
  110.2 1.6 %shard_map.156 = (f32[48,512]{1,0:T(8,128)}, f32[192,512]{1,0:T(8,128)}) custom-call(s32[1,512]{1,0:T(1,128)S(1)} %bitcast.21, f32[1024,256]{1,0:T(8,128)S(1)} %bitcast.18), custom_call_target="tpu_custom_call" | custom-call | tf_op jit(solution)/shard_map/pallas_call | solution.py:868
  (88 shorter events, 17.4 us)
Async XLA Ops:
  4.2 11.3 %copy-start.15 = (f32[8]{0:T(128)S(1)}, f32[8]{0:T(128)}, u32[]{:S(2)}) copy-start(f32[8]{0:T(128)} %param.21) | copy-start | bytes 100
  4.3 11.3 %copy-start.16 = (f32[8]{0:T(128)S(1)}, f32[8]{0:T(128)}, u32[]{:S(2)}) copy-start(f32[8]{0:T(128)} %param.20) | copy-start | bytes 100
  4.3 12.1 %copy-start.14 = (f32[8,24,6]{1,0,2:T(8,128)S(1)}, f32[8,24,6]{1,0,2:T(8,128)}, u32[]{:S(2)}) copy-start(f32[8,24,6]{1,0,2:T(8,128)} %param.18) | copy-start | bytes 13828
  4.3 16.8 %copy-start = (f32[8,8,16,256]{3,2,1,0:T(8,128)S(1)}, f32[8,8,16,256]{3,2,1,0:T(8,128)}, u32[]{:S(2)}) copy-start(f32[8,8,16,256]{3,2,1,0:T(8,128)} %grains.7) | copy-start | bytes 3145732
  4.3 34.4 %all-to-all-start = ((f32[128,5,4,128]{3,2,1,0:T(4,128)}), f32[128,5,4,128]{3,2,1,0:T(4,128)S(1)}, u32[]{:S(2)}, u32[]{:S(2)}) async-start(f32[128,5,4,128]{3,2,1,0:T(4,128)} %bitcast.22), calls=%async_computation | async-start | bytes 2621440 | tf_op jit(solution)/shard_map/all_to_all | solution.py:209
  21.0 9.4 %copy-start.1 = (bf16[256,256]{1,0:T(8,128)(2,1)}, bf16[256,256]{1,0:T(8,128)(2,1)S(1)}, u32[]{:S(2)}) copy-start(bf16[256,256]{1,0:T(8,128)(2,1)S(1)} %get-tuple-element.77.spread) | copy-start | bytes 393220
  21.1 9.4 %copy-start.5 = (bf16[192,24]{1,0:T(8,128)(2,1)}, bf16[192,24]{1,0:T(8,128)(2,1)S(1)}, u32[]{:S(2)}) copy-start(bf16[192,24]{1,0:T(8,128)(2,1)S(1)} %get-tuple-element.75.active_map) | copy-start | bytes 27652
  21.9 22.0 %collective-permute-start.2 = (f32[8,16,256]{2,1,0:T(8,128)}, f32[8,16,256]{2,1,0:T(8,128)}, u32[]{:S(2)}, u32[]{:S(2)}) collective-permute-start(f32[8,16,256]{2,1,0:T(8,128)} %get-tuple-element.79), channel_id=1, source_target_pairs={{0,8},{16,24},{32,40},{48,56},{64,72},{80,88},{96,104},{112,120},{... | collective-permute-start | bytes 393224 | tf_op jit(solution)/shard_map/ppermute | solution.py:645
  23.0 20.9 %collective-permute-start.3 = (f32[8,16,256]{2,1,0:T(8,128)}, f32[8,16,256]{2,1,0:T(8,128)}, u32[]{:S(2)}, u32[]{:S(2)}) collective-permute-start(f32[8,16,256]{2,1,0:T(8,128)} %get-tuple-element.80), channel_id=1, source_target_pairs={{8,16},{24,32},{40,48},{56,64},{72,80},{88,96},{104,112},{120,0},{... | collective-permute-start | bytes 393224 | tf_op jit(solution)/shard_map/ppermute | solution.py:645
  27.5 16.4 %collective-permute-start = (f32[8,8,256]{2,1,0:T(8,128)}, f32[8,8,256]{2,1,0:T(8,128)}, u32[]{:S(2)}, u32[]{:S(2)}) collective-permute-start(f32[8,8,256]{2,1,0:T(8,128)} %get-tuple-element.64), channel_id=1, source_target_pairs={{0,1},{2,3},{4,5},{6,7},{1,0},{3,2},{5,4},{7,6},{8,9},{10,11},{12,... | collective-permute-start | bytes 196616 | tf_op jit(solution)/shard_map/ppermute | solution.py:645
  27.5 16.4 %collective-permute-start.1 = (f32[8,8,256]{2,1,0:T(8,128)}, f32[8,8,256]{2,1,0:T(8,128)}, u32[]{:S(2)}, u32[]{:S(2)}) collective-permute-start(f32[8,8,256]{2,1,0:T(8,128)} %get-tuple-element.65), channel_id=1, source_target_pairs={{1,2},{3,4},{5,6},{7,0},{2,1},{4,3},{6,5},{0,7},{9,10},{11,12},{13... | collective-permute-start | bytes 196616 | tf_op jit(solution)/shard_map/ppermute | solution.py:645
  45.2 7.5 %collective-permute-start.4 = (f32[8,16,256]{2,1,0:T(8,128)S(1)}, f32[8,16,256]{2,1,0:T(8,128)S(1)}, u32[]{:S(2)}, u32[]{:S(2)}) collective-permute-start(f32[8,16,256]{2,1,0:T(8,128)S(1)} %get-tuple-element.81.x_pair_new), channel_id=1, source_target_pairs={{0,8},{16,24},{32,40},{48,56},{64,72},{80,88},{96,104},{112,120},{... | collective-permute-start | bytes 393224 | tf_op jit(solution)/shard_map/ppermute | solution.py:645
  45.3 8.4 %collective-permute-start.5 = (f32[8,16,256]{2,1,0:T(8,128)S(1)}, f32[8,16,256]{2,1,0:T(8,128)S(1)}, u32[]{:S(2)}, u32[]{:S(2)}) collective-permute-start(f32[8,16,256]{2,1,0:T(8,128)S(1)} %get-tuple-element.82.x_other_new), channel_id=1, source_target_pairs={{8,16},{24,32},{40,48},{56,64},{72,80},{88,96},{104,112},{120,0},{... | collective-permute-start | bytes 393224 | tf_op jit(solution)/shard_map/ppermute | solution.py:645
  47.6 1.4 %collective-permute-start.6 = (f32[8,8,256]{2,1,0:T(8,128)S(1)}, f32[8,8,256]{2,1,0:T(8,128)S(1)}, u32[]{:S(2)}, u32[]{:S(2)}) collective-permute-start(f32[8,8,256]{2,1,0:T(8,128)S(1)} %get-tuple-element.84), channel_id=1, source_target_pairs={{0,1},{2,3},{4,5},{6,7},{1,0},{3,2},{5,4},{7,6},{8,9},{10,11},{12,... | collective-permute-start | bytes 196616 | tf_op jit(solution)/shard_map/ppermute | solution.py:645
  47.7 5.0 %collective-permute-start.7 = (f32[8,8,256]{2,1,0:T(8,128)S(1)}, f32[8,8,256]{2,1,0:T(8,128)S(1)}, u32[]{:S(2)}, u32[]{:S(2)}) collective-permute-start(f32[8,8,256]{2,1,0:T(8,128)S(1)} %get-tuple-element.85), channel_id=1, source_target_pairs={{1,2},{3,4},{5,6},{7,0},{2,1},{4,3},{6,5},{0,7},{9,10},{11,12},{13... | collective-permute-start | bytes 196616 | tf_op jit(solution)/shard_map/ppermute | solution.py:645
  53.9 10.0 %collective-permute-start.10 = (f32[8,16,256]{2,1,0:T(8,128)S(1)}, f32[8,16,256]{2,1,0:T(8,128)S(1)}, u32[]{:S(2)}, u32[]{:S(2)}) collective-permute-start(f32[8,16,256]{2,1,0:T(8,128)S(1)} %get-tuple-element.86.x_pair_new), channel_id=1, source_target_pairs={{0,8},{16,24},{32,40},{48,56},{64,72},{80,88},{96,104},{112,120},{... | collective-permute-start | bytes 393224 | tf_op jit(solution)/shard_map/ppermute | solution.py:645
  54.4 9.6 %collective-permute-start.11 = (f32[8,16,256]{2,1,0:T(8,128)S(1)}, f32[8,16,256]{2,1,0:T(8,128)S(1)}, u32[]{:S(2)}, u32[]{:S(2)}) collective-permute-start(f32[8,16,256]{2,1,0:T(8,128)S(1)} %get-tuple-element.87.x_other_new), channel_id=1, source_target_pairs={{8,16},{24,32},{40,48},{56,64},{72,80},{88,96},{104,112},{120,0},{... | collective-permute-start | bytes 393224 | tf_op jit(solution)/shard_map/ppermute | solution.py:645
  58.7 3.7 %collective-permute-start.8 = (f32[8,8,256]{2,1,0:T(8,128)S(1)}, f32[8,8,256]{2,1,0:T(8,128)S(1)}, u32[]{:S(2)}, u32[]{:S(2)}) collective-permute-start(f32[8,8,256]{2,1,0:T(8,128)S(1)} %get-tuple-element.89), channel_id=1, source_target_pairs={{0,1},{2,3},{4,5},{6,7},{1,0},{3,2},{5,4},{7,6},{8,9},{10,11},{12,... | collective-permute-start | bytes 196616 | tf_op jit(solution)/shard_map/ppermute | solution.py:645
  58.8 5.2 %collective-permute-start.9 = (f32[8,8,256]{2,1,0:T(8,128)S(1)}, f32[8,8,256]{2,1,0:T(8,128)S(1)}, u32[]{:S(2)}, u32[]{:S(2)}) collective-permute-start(f32[8,8,256]{2,1,0:T(8,128)S(1)} %get-tuple-element.90), channel_id=1, source_target_pairs={{1,2},{3,4},{5,6},{7,0},{2,1},{4,3},{6,5},{0,7},{9,10},{11,12},{13... | collective-permute-start | bytes 196616 | tf_op jit(solution)/shard_map/ppermute | solution.py:645
  64.2 8.3 %collective-permute-start.12 = (f32[8,16,256]{2,1,0:T(8,128)S(1)}, f32[8,16,256]{2,1,0:T(8,128)S(1)}, u32[]{:S(2)}, u32[]{:S(2)}) collective-permute-start(f32[8,16,256]{2,1,0:T(8,128)S(1)} %get-tuple-element.94.x_pair_new), channel_id=1, source_target_pairs={{0,8},{16,24},{32,40},{48,56},{64,72},{80,88},{96,104},{112,120},{... | collective-permute-start | bytes 393224 | tf_op jit(solution)/shard_map/ppermute | solution.py:645
  64.3 8.4 %collective-permute-start.13 = (f32[8,16,256]{2,1,0:T(8,128)S(1)}, f32[8,16,256]{2,1,0:T(8,128)S(1)}, u32[]{:S(2)}, u32[]{:S(2)}) collective-permute-start(f32[8,16,256]{2,1,0:T(8,128)S(1)} %get-tuple-element.95.x_other_new), channel_id=1, source_target_pairs={{8,16},{24,32},{40,48},{56,64},{72,80},{88,96},{104,112},{120,0},{... | collective-permute-start | bytes 393224 | tf_op jit(solution)/shard_map/ppermute | solution.py:645
  67.4 1.3 %collective-permute-start.14 = (f32[8,8,256]{2,1,0:T(8,128)S(1)}, f32[8,8,256]{2,1,0:T(8,128)S(1)}, u32[]{:S(2)}, u32[]{:S(2)}) collective-permute-start(f32[8,8,256]{2,1,0:T(8,128)S(1)} %get-tuple-element.97), channel_id=1, source_target_pairs={{0,1},{2,3},{4,5},{6,7},{1,0},{3,2},{5,4},{7,6},{8,9},{10,11},{12,... | collective-permute-start | bytes 196616 | tf_op jit(solution)/shard_map/ppermute | solution.py:645
  67.5 5.0 %collective-permute-start.15 = (f32[8,8,256]{2,1,0:T(8,128)S(1)}, f32[8,8,256]{2,1,0:T(8,128)S(1)}, u32[]{:S(2)}, u32[]{:S(2)}) collective-permute-start(f32[8,8,256]{2,1,0:T(8,128)S(1)} %get-tuple-element.98), channel_id=1, source_target_pairs={{1,2},{3,4},{5,6},{7,0},{2,1},{4,3},{6,5},{0,7},{9,10},{11,12},{13... | collective-permute-start | bytes 196616 | tf_op jit(solution)/shard_map/ppermute | solution.py:645
  73.0 9.0 %collective-permute-start.16 = (f32[8,16,256]{2,1,0:T(8,128)S(1)}, f32[8,16,256]{2,1,0:T(8,128)S(1)}, u32[]{:S(2)}, u32[]{:S(2)}) collective-permute-start(f32[8,16,256]{2,1,0:T(8,128)S(1)} %get-tuple-element.99.x_pair_new), channel_id=1, source_target_pairs={{0,8},{16,24},{32,40},{48,56},{64,72},{80,88},{96,104},{112,120},{... | collective-permute-start | bytes 393224 | tf_op jit(solution)/shard_map/ppermute | solution.py:645
  73.1 8.9 %collective-permute-start.17 = (f32[8,16,256]{2,1,0:T(8,128)S(1)}, f32[8,16,256]{2,1,0:T(8,128)S(1)}, u32[]{:S(2)}, u32[]{:S(2)}) collective-permute-start(f32[8,16,256]{2,1,0:T(8,128)S(1)} %get-tuple-element.100.x_other_new), channel_id=1, source_target_pairs={{8,16},{24,32},{40,48},{56,64},{72,80},{88,96},{104,112},{120,0},{... | collective-permute-start | bytes 393224 | tf_op jit(solution)/shard_map/ppermute | solution.py:645
  76.9 4.3 %collective-permute-start.18 = (f32[8,8,256]{2,1,0:T(8,128)S(1)}, f32[8,8,256]{2,1,0:T(8,128)S(1)}, u32[]{:S(2)}, u32[]{:S(2)}) collective-permute-start(f32[8,8,256]{2,1,0:T(8,128)S(1)} %get-tuple-element.102), channel_id=1, source_target_pairs={{0,1},{2,3},{4,5},{6,7},{1,0},{3,2},{5,4},{7,6},{8,9},{10,11},{12,... | collective-permute-start | bytes 196616 | tf_op jit(solution)/shard_map/ppermute | solution.py:645
  77.0 5.0 %collective-permute-start.19 = (f32[8,8,256]{2,1,0:T(8,128)S(1)}, f32[8,8,256]{2,1,0:T(8,128)S(1)}, u32[]{:S(2)}, u32[]{:S(2)}) collective-permute-start(f32[8,8,256]{2,1,0:T(8,128)S(1)} %get-tuple-element.103), channel_id=1, source_target_pairs={{1,2},{3,4},{5,6},{7,0},{2,1},{4,3},{6,5},{0,7},{9,10},{11,12},{13... | collective-permute-start | bytes 196616 | tf_op jit(solution)/shard_map/ppermute | solution.py:645
  83.6 26.6 %all-to-all-start.1 = ((f32[128,8,256]{2,1,0:T(8,128)}), f32[128,8,256]{2,1,0:T(8,128)S(1)}, u32[]{:S(2)}, u32[]{:S(2)}) async-start(f32[128,8,256]{2,1,0:T(8,128)} %bitcast.10), calls=%async_computation.1 | async-start | bytes 2097152 | tf_op jit(solution)/shard_map/all_to_all | solution.py:209
  89.1 15.6 %collective-permute-start.20 = (f32[8,16,256]{2,1,0:T(8,128)S(1)}, f32[8,16,256]{2,1,0:T(8,128)S(1)}, u32[]{:S(2)}, u32[]{:S(2)}) collective-permute-start(f32[8,16,256]{2,1,0:T(8,128)S(1)} %get-tuple-element.112.x_pair_new), channel_id=1, source_target_pairs={{0,8},{16,24},{32,40},{48,56},{64,72},{80,88},{96,104},{112,120},{... | collective-permute-start | bytes 393224 | tf_op jit(solution)/shard_map/ppermute | solution.py:645
  90.2 19.0 %collective-permute-start.21 = (f32[8,16,256]{2,1,0:T(8,128)S(1)}, f32[8,16,256]{2,1,0:T(8,128)S(1)}, u32[]{:S(2)}, u32[]{:S(2)}) collective-permute-start(f32[8,16,256]{2,1,0:T(8,128)S(1)} %get-tuple-element.113.x_other_new), channel_id=1, source_target_pairs={{8,16},{24,32},{40,48},{56,64},{72,80},{88,96},{104,112},{120,0},{... | collective-permute-start | bytes 393224 | tf_op jit(solution)/shard_map/ppermute | solution.py:645
  95.5 3.7 %collective-permute-start.22 = (f32[8,8,256]{2,1,0:T(8,128)S(1)}, f32[8,8,256]{2,1,0:T(8,128)S(1)}, u32[]{:S(2)}, u32[]{:S(2)}) collective-permute-start(f32[8,8,256]{2,1,0:T(8,128)S(1)} %get-tuple-element.115), channel_id=1, source_target_pairs={{0,1},{2,3},{4,5},{6,7},{1,0},{3,2},{5,4},{7,6},{8,9},{10,11},{12,... | collective-permute-start | bytes 196616 | tf_op jit(solution)/shard_map/ppermute | solution.py:645
  95.6 8.0 %collective-permute-start.23 = (f32[8,8,256]{2,1,0:T(8,128)S(1)}, f32[8,8,256]{2,1,0:T(8,128)S(1)}, u32[]{:S(2)}, u32[]{:S(2)}) collective-permute-start(f32[8,8,256]{2,1,0:T(8,128)S(1)} %get-tuple-element.116), channel_id=1, source_target_pairs={{1,2},{3,4},{5,6},{7,0},{2,1},{4,3},{6,5},{0,7},{9,10},{11,12},{13... | collective-permute-start | bytes 196616 | tf_op jit(solution)/shard_map/ppermute | solution.py:645
  (11 other events, 26.3 us)
